TPU v7x, 256 devices: a whole 4x4x8 slice. The times are simulated.
256 devices in a mesh: grp: 4 (over x_hi, core), gx: 16 (over x_lo, z), gy: 4 (over y).
Axes of the slice: x: 4 (x_hi: 2, x_lo: 2; x = x_hi * 2 + x_lo), y: 4, z: 8, core: 2. Of those that a mesh axis runs over, the one named last changes fastest.
Arguments:
- flow_fields: float32 [4, 32, 32, 512], P('grp', None, 'gx', 'gy'), may hold values from -4 to 4
- level_set: float32 [4, 64, 64, 1024], P('grp', None, 'gx', 'gy'), may hold values from -9 to 9
- band_tiles: int32 [8, 16, 64], P(None, 'gx', 'gy'), may hold values 0 or 1
- nozzle_phase: int32 [64, 1024], P('gx', 'gy'), may hold values from 0 to 2
Outputs:
- flow_next: float32 [4, 32, 32, 512], P('grp', None, 'gx', 'gy')
All inputs are finite; a program needn't handle non-finite values. No bound on the sum of `band_tiles` on one device may be relied on, other than what follows from the above.
Results may differ from a plain program's by a relative error of at most 0.0003.
Values sent between devices are 32-bit elements; how exact they have to be, the bound alone decides.
No kernel may reach another device: no remote copies, remote signals or barrier semaphores. Data moves between devices by JAX's collectives and lax.ppermute only.
A program may use at most 64 MiB of HBM per device.

v0:
```python
import jax
import jax.numpy as jnp
from jax import lax
from jax.experimental import pallas as pl
from jax.experimental.pallas import tpu as pltpu
from jax.sharding import PartitionSpec as P


LANES = 128
FINE = 64
FLOW = 32
SLOT = 40
SHRINK = 0.25
WENO_EPS = 1e-06 * SHRINK * SHRINK
STEP_FINE = 0.3
STEP_FLOW = 0.2
SURFACE = 6.0
SPREAD = 1.5
IMPLICIT = 0.5
F32 = jnp.float32


def lane_ids(rows):
    return lax.broadcasted_iota(jnp.int32, (rows, LANES), 1)


def roll_lanes(value, shift):
    return pltpu.roll(value, shift % LANES, 1)


def exact_dot(left, right):
    return jnp.dot(left, right, precision=lax.Precision.HIGHEST, preferred_element_type=F32)


def chunk(index):
    return pl.multiple_of(index * 8, 8)


def pack_kernel(group_ref, flow_ref, level_ref, band_ref, nozzle_ref, one_ref, two_ref, three_ref, keep_ref, ring):
    group = group_ref[0]
    slot = jnp.where(group == 3, 0, group * SLOT)
    for row in range(4):
        block = level_ref[:, row, :] * SHRINK
        ring[0, row * FINE : (row + 1) * FINE, :] = block[:, :LANES]
        ring[1, row * FINE : (row + 1) * FINE, :] = block[:, LANES:]
    spread_tiles = jnp.where(
        lax.broadcasted_iota(jnp.int32, (16, 256), 1) // 16 == lax.broadcasted_iota(jnp.int32, (16, 256), 0), 1.0, 0.0
    )
    flags = exact_dot(band_ref[...].astype(F32), spread_tiles)
    phases = nozzle_ref[...].astype(F32)

    def quarter(first, second, target):
        offset = jnp.where(target % 2 == 0, 96, 32)
        plain = jnp.logical_or(target == 1, target == 2)
        low = jnp.where(plain, first, second)
        high = jnp.where(plain, second, first)
        joined = jnp.where(lane_ids(first.shape[0]) >= offset, low, high)
        return pltpu.roll(joined, LANES - offset, 1)

    for step, out_ref in enumerate((keep_ref, one_ref, two_ref, three_ref)):
        target = (group + step) % 4
        turn = (slot + 4 - 32 * target + 2 * LANES) % LANES
        for row in range(2):
            out_ref[row * FLOW : (row + 1) * FLOW, :] = pltpu.roll(flow_ref[:, row, :], turn, 1)

        def copy(index, carry, out_ref=out_ref, target=target):
            at = pl.multiple_of(index * 32, 32)
            out_ref[pl.ds(64 + at, 32), :] = quarter(ring[0, pl.ds(at, 32), :], ring[1, pl.ds(at, 32), :], target)
            return carry

        lax.fori_loop(0, 8, copy, 0)
    keep_ref[320:328, :] = quarter(flags[:, :LANES], flags[:, LANES:], group)
    keep_ref[328:332, :] = quarter(phases[:, :LANES], phases[:, LANES:], group)
    keep_ref[332:336, :] = jnp.zeros((4, LANES), F32)


def assemble_kernel(group_ref, keep_ref, one_ref, two_ref, three_ref, tile_ref, edge_ref):
    group = group_ref[0]
    lanes = lane_ids(64)
    parts = (keep_ref, one_ref, two_ref, three_ref)
    owners = [(group - step + 4) % 4 for step in range(4)]
    moving = jnp.zeros((64, LANES), F32)
    for part, owner in zip(parts, owners):
        inside = jnp.logical_and(lanes >= owner * SLOT, lanes < owner * SLOT + SLOT)
        inside = jnp.logical_and(inside, owner < 3)
        moving = jnp.where(inside, part[0:64, :], moving)
    tile_ref[0:64, :] = moving
    tile_ref[384:400, :] = keep_ref[320:336, :]
    for part, owner in zip(parts, owners):

        @pl.when(owner == 3)
        def _(part=part):
            tile_ref[64:128, :] = part[0:64, :]
            tile_ref[128:384, :] = part[64:320, :]

    pressure = tile_ref[64:128, :]
    pushed = jnp.where(lanes >= 124, roll_lanes(pressure, 88), roll_lanes(pressure, 120))
    edge_ref[0:64, :] = jnp.where(lanes >= 120, pushed, moving)
    start = jnp.where(group == 0, 0, 96)
    packed = jnp.zeros((FINE, LANES), F32)
    for row in range(4):
        turned = pltpu.roll(tile_ref[128 + row * FINE : 128 + (row + 1) * FINE, :], (32 * row - start + LANES) % LANES, 1)
        packed = jnp.where(lanes // 32 == row, turned, packed)
    edge_ref[64:128, :] = packed
    edge_ref[128:144, :] = keep_ref[320:336, :]


def edge_kernel(group_ref, tile_ref, edge_ref, fixed_ref, up_ref, down_ref):
    group = group_ref[0]
    lanes = lane_ids(64)
    first, last = group == 0, group == 3
    within = lanes % SLOT
    slots = lanes < 3 * SLOT
    low_edge = jnp.logical_and(jnp.logical_and(within < 4, slots), first)
    high_edge = jnp.logical_and(jnp.logical_and(within >= 36, slots), last)
    received = edge_ref[0:64, :]
    moving = jnp.where(jnp.logical_or(low_edge, high_edge), received, tile_ref[0:64, :])
    pressure = tile_ref[64:128, :]
    pressure = jnp.where(jnp.logical_and(lanes < 4, first), roll_lanes(received, 8), pressure)
    high_pressure = jnp.logical_and(jnp.logical_and(lanes >= 36, lanes < 40), last)
    pressure = jnp.where(high_pressure, roll_lanes(received, 40), pressure)
    fine_edge = jnp.logical_or(jnp.logical_and(lanes < 32, first), jnp.logical_and(lanes >= 96, last))
    start = jnp.where(first, 0, 96)
    fixed_ref[0:64, :] = moving
    fixed_ref[64:128, :] = pressure
    for row in range(4):
        turned = pltpu.roll(edge_ref[64:128, :], (start - 32 * row + LANES) % LANES, 1)
        level = jnp.where(fine_edge, turned, tile_ref[128 + row * FINE : 128 + (row + 1) * FINE, :])
        fixed_ref[128 + row * FINE : 128 + (row + 1) * FINE, :] = level
        if row < 3:
            down_ref[row * FINE : (row + 1) * FINE, :] = level
        if row > 0:
            up_ref[(row - 1) * FINE : row * FINE, :] = level
    marks = jnp.where(fine_edge[0:16, :], edge_ref[128:144, :], tile_ref[384:400, :])
    fixed_ref[384:400, :] = marks
    for out_ref, row in ((up_ref, 1), (down_ref, 0)):
        out_ref[192:224, :] = moving[row * FLOW : (row + 1) * FLOW, :]
        out_ref[224:256, :] = pressure[row * FLOW : (row + 1) * FLOW, :]
        out_ref[256:272, :] = marks


def bent(below, here, above):
    return (above - here) - (here - below)


def upwind_part(far_low, low, mid, high, far_high, slope, speed):
    ahead = speed >= 0.0
    one = jnp.where(ahead, far_low, far_high)
    two = jnp.where(ahead, low, high)
    four = jnp.where(ahead, high, low)
    curve_one = two - one
    curve_two = mid - two
    curve_three = four - mid
    third = 4.0 / 3.0
    smooth_one = (two * two + WENO_EPS) + curve_one * (third * curve_one + two)
    smooth_two = (two * mid + WENO_EPS) + third * (curve_two * curve_two)
    smooth_three = (mid * mid + WENO_EPS) + curve_three * (third * curve_three - mid)
    both_three = smooth_one * smooth_two
    both_two = smooth_one * smooth_three
    both_one = smooth_two * smooth_three
    weight_one = both_one * both_one
    weight_two = 6.0 * (both_two * both_two)
    weight_three = 3.0 * (both_three * both_three)
    top = weight_one * (2.0 * curve_one - 3.0 * curve_two) - (weight_two * curve_two + weight_three * curve_three)
    bottom = weight_one + weight_two + weight_three
    return speed * slope + (jnp.abs(speed) * (1.0 / 6.0)) * (top / bottom)


def fill_wrapped(wrapped, index, source, at):
    wrapped[index, 8:72, :] = source[at : at + FINE, :]
    wrapped[index, 0:8, :] = source[at + 56 : at + 64, :]
    wrapped[index, 72:80, :] = source[at : at + 8, :]


def section(rows, first_row, current, initial, speeds, wrapped, keep, blend, store):
    for index in range(rows):
        fill_wrapped(wrapped, index, *current[index + 3])

    def body(step, carry):
        z = chunk(step)

        def load(place):
            ref, at = place
            return ref[pl.ds(at + z, 8), :]

        values = [load(place) for place in current]
        bends = [bent(values[k - 1], values[k], values[k + 1]) for k in range(1, rows + 5)]
        for index in range(rows):
            here = values[index + 3]
            speed_row = (first_row + index + 2) // 2
            speed_x = speeds[0, speed_row, pl.ds(z, 8), :]
            speed_y = speeds[1, speed_row, pl.ds(z, 8), :]
            speed_z = speeds[2, speed_row, pl.ds(z, 8), :]
            rate = upwind_part(*bends[index : index + 5], (values[index + 4] - values[index + 2]) * 0.5, speed_x)
            after = roll_lanes(here, -1)
            before = roll_lanes(here, 1)
            mid = bent(before, here, after)
            rate = rate + upwind_part(
                roll_lanes(mid, 2),
                roll_lanes(mid, 1),
                mid,
                roll_lanes(mid, -1),
                roll_lanes(mid, -2),
                (after - before) * 0.5,
                speed_y,
            )
            column = [wrapped[index, pl.ds(z + 8 + offset, 8), :] for offset in range(-3, 4)]
            column[3] = here
            column_bends = [bent(column[k - 1], column[k], column[k + 1]) for k in range(1, 6)]
            rate = rate + upwind_part(*column_bends, (column[4] - column[2]) * 0.5, speed_z)
            moved = blend * (here - STEP_FINE * rate)
            if keep:
                moved = moved + keep * load(initial[index])
            store(index, z, moved)
        return carry

    lax.fori_loop(0, 8, body, 0)


def centred(below, above):
    return (above - below) * 0.5


def planes(value):
    return pltpu.roll(value, FLOW - 1, 0), pltpu.roll(value, 1, 0)


def by_slot(lanes, first, second, third):
    return jnp.where(lanes < SLOT, first, jnp.where(lanes < 2 * SLOT, second, third))


def sweep(below, here, above, source):
    up, down = planes(here)
    beside = below + above + roll_lanes(here, 1) + roll_lanes(here, -1) + up + down
    return (source + IMPLICIT * beside) / (1.0 + 6.0 * IMPLICIT)


def first_kernel(fixed_ref, left_ref, right_ref, out_ref, speed_ref, wrapped):
    moving = [
        left_ref[192:224, :],
        fixed_ref[0:32, :],
        fixed_ref[32:64, :],
        right_ref[192:224, :],
    ]
    stacked = jnp.concatenate(moving, axis=0)
    source_lane = lax.broadcasted_iota(jnp.int32, (LANES, LANES), 0)
    fine_lane = lax.broadcasted_iota(jnp.int32, (LANES, LANES), 1)
    covered = jnp.logical_and(fine_lane >= 24, fine_lane < 104)
    for component in range(3):
        pick = jnp.logical_and(source_lane == SLOT * component + fine_lane // 2 - 12, covered)
        spread = exact_dot(stacked, jnp.where(pick, 1.0, 0.0))
        for row in range(4):
            part = spread[row * FLOW : (row + 1) * FLOW, :]
            speed_ref[component, row, pl.ds(0, FLOW, stride=2), :] = part
            speed_ref[component, row, pl.ds(1, FLOW, stride=2), :] = part

    lanes = lane_ids(FLOW)
    pressure = [
        left_ref[224:256, :],
        fixed_ref[64:96, :],
        fixed_ref[96:128, :],
        right_ref[224:256, :],
    ]
    pressure = [by_slot(lanes, p, roll_lanes(p, 40), roll_lanes(p, 80)) for p in pressure]
    for row in range(2):
        here, push = moving[row + 1], pressure[row + 1]
        back, further = roll_lanes(here, 88), roll_lanes(here, 40)
        along_x = by_slot(lanes, here, further, roll_lanes(here, 80))
        along_y = by_slot(lanes, back, here, further)
        along_z = by_slot(lanes, roll_lanes(here, 48), back, here)
        up, down = planes(here)
        push_up, push_down = planes(push)
        advect = -(
            along_x * centred(moving[row], moving[row + 2])
            + along_y * centred(roll_lanes(here, 1), roll_lanes(here, -1))
            + along_z * centred(down, up)
        )
        gradient = by_slot(
            lanes,
            centred(pressure[row], pressure[row + 2]),
            centred(roll_lanes(push, 1), roll_lanes(push, -1)),
            centred(push_down, push_up),
        )
        out_ref[256 + row * FLOW : 256 + (row + 1) * FLOW, :] = here + STEP_FLOW * (advect - gradient)

    places = (
        [(left_ref, FINE * row) for row in range(3)]
        + [(fixed_ref, 128 + FINE * row) for row in range(4)]
        + [(right_ref, FINE * row) for row in range(3)]
    )

    def store(index, z, value):
        out_ref[pl.ds(index * FINE + z, 8), :] = value

    section(4, 0, places, None, speed_ref, wrapped, 0.0, 1.0, store)


def second_kernel(own_ref, left_ref, right_ref, fixed_ref, old_left, old_right, speed_ref, out_ref, up_ref, down_ref, wrapped):
    source = [ref[256 + row * FLOW : 256 + (row + 1) * FLOW, :] for ref in (left_ref, own_ref, right_ref) for row in range(2)]
    for row in range(4):
        done = sweep(source[row], source[row + 1], source[row + 2], source[row + 1])
        out_ref[384 + row * FLOW : 384 + (row + 1) * FLOW, :] = done
        if row == 1:
            up_ref[256:288, :] = done
        if row == 2:
            down_ref[256:288, :] = done
    places = [(ref, FINE * row) for ref in (left_ref, own_ref, right_ref) for row in range(4)]
    initial = [(old_left, 128)] + [(fixed_ref, 128 + FINE * row) for row in range(4)] + [(old_right, 0)]

    def store(index, z, value):
        out_ref[pl.ds(index * FINE + z, 8), :] = value
        if index < 4:
            up_ref[pl.ds(index * FINE + z, 8), :] = value
        if index > 1:
            down_ref[pl.ds((index - 2) * FINE + z, 8), :] = value

    section(6, -1, places, initial, speed_ref, wrapped, 0.75, 0.25, store)


def third_kernel(
    own_ref, left_ref, right_ref, older, older_left, older_right, fixed_ref, old_left, old_right, speed_ref,
    out_ref, wrapped, shaped, normal_x, normal_z, summed,
):
    places = (
        [(left_ref, FINE * row) for row in range(4)]
        + [(own_ref, FINE * row) for row in range(6)]
        + [(right_ref, FINE * row) for row in range(4)]
    )
    initial = (
        [(old_left, 64), (old_left, 128)]
        + [(fixed_ref, 128 + FINE * row) for row in range(4)]
        + [(old_right, 0), (old_right, 64)]
    )
    marks = [(old_left, 256)] * 2 + [(fixed_ref, 384)] * 4 + [(old_right, 256)] * 2

    def store(index, z, value):
        ref, at = initial[index]
        mark_ref, mark_at = marks[index]
        flag = mark_ref[pl.ds(mark_at + z // 8, 1), :]
        value = jnp.where(flag > 0.5, value, ref[pl.ds(at + z, 8), :]) * (1.0 / SHRINK)
        phase = mark_ref[mark_at + 8 + (index + 2) % 4 : mark_at + 9 + (index + 2) % 4, :]
        bottom = jnp.logical_and(lax.broadcasted_iota(jnp.int32, (8, LANES), 0) == 0, z == 0)
        value = jnp.where(jnp.logical_and(bottom, phase == 2.0), SPREAD, value)
        value = jnp.where(jnp.logical_and(bottom, phase == 1.0), -SPREAD, value)
        shaped[index, pl.ds(8 + z, 8), :] = value

    section(8, -2, places, initial, speed_ref, wrapped, 1.0 / 3.0, 2.0 / 3.0, store)
    for index in range(8):
        shaped[index, 0:8, :] = shaped[index, 64:72, :]
        shaped[index, 72:80, :] = shaped[index, 8:16, :]

    def normals(step, carry):
        z = chunk(step)
        middle = [shaped[k, pl.ds(8 + z, 8), :] for k in range(8)]
        for row in range(6):
            here = middle[row + 1]
            slope_x = (middle[row + 2] - middle[row]) * 0.5
            slope_y = (roll_lanes(here, -1) - roll_lanes(here, 1)) * 0.5
            slope_z = (shaped[row + 1, pl.ds(9 + z, 8), :] - shaped[row + 1, pl.ds(7 + z, 8), :]) * 0.5
            inverse = lax.rsqrt(slope_x * slope_x + slope_y * slope_y + slope_z * slope_z + 1.0)
            normal_x[row, pl.ds(z, 8), :] = slope_x * inverse
            if 0 < row < 5:
                wrapped[row, pl.ds(z, 8), :] = slope_y * inverse
                normal_z[row - 1, pl.ds(8 + z, 8), :] = slope_z * inverse
        return carry

    lax.fori_loop(0, 8, normals, 0)
    for row in range(4):
        normal_z[row, 0:8, :] = normal_z[row, 64:72, :]
        normal_z[row, 72:80, :] = normal_z[row, 8:16, :]

    def forces(step, carry):
        z = chunk(step)
        for half in range(2):
            total = None
            for row in (2 * half, 2 * half + 1):
                level = shaped[row + 2, pl.ds(8 + z, 8), :]
                here_x = normal_x[row + 1, pl.ds(z, 8), :]
                here_y = wrapped[row + 1, pl.ds(z, 8), :]
                here_z = normal_z[row, pl.ds(8 + z, 8), :]
                curvature = (normal_x[row + 2, pl.ds(z, 8), :] - normal_x[row, pl.ds(z, 8), :]) * 0.5
                curvature = curvature + (roll_lanes(here_y, -1) - roll_lanes(here_y, 1)) * 0.5
                curvature = (
                    curvature + (normal_z[row, pl.ds(9 + z, 8), :] - normal_z[row, pl.ds(7 + z, 8), :]) * 0.5
                )
                delta = jnp.exp(level * level * (-1.0 / (2.0 * SPREAD * SPREAD))) * (1.0 / (SPREAD * 2.5066282746310002))
                strength = SURFACE * curvature * delta
                fraction = 0.5 + 0.5 * jnp.tanh(level * (1.0 / SPREAD))
                terms = (here_x * strength, here_y * strength, here_z * strength, fraction)
                total = terms if total is None else tuple(a + b for a, b in zip(total, terms))
            for component in range(4):
                summed[component, pl.ds(half * FINE + z, 8), :] = total[component]
        return carry

    lax.fori_loop(0, 8, forces, 0)

    source = [older_left[288:320, :], older[256:288, :], older[288:320, :], older_right[256:288, :]]
    once = [left_ref[256:288, :]] + [own_ref[384 + row * FLOW : 384 + (row + 1) * FLOW, :] for row in range(4)]
    once = once + [right_ref[256:288, :]]
    twice = [sweep(once[row], once[row + 1], once[row + 2], source[row]) for row in range(4)]
    thrice = [sweep(twice[row], twice[row + 1], twice[row + 2], source[row + 1]) for row in range(2)]

    source_lane = lax.broadcasted_iota(jnp.int32, (LANES, LANES), 0)
    out_lane = lax.broadcasted_iota(jnp.int32, (LANES, LANES), 1)
    part, column = out_lane // FLOW, out_lane % FLOW
    take = jnp.logical_and(source_lane == SLOT * part + 4 + column, part < 3)
    done = exact_dot(jnp.concatenate(thrice, axis=0), jnp.where(take, 1.0, 0.0))
    for component in range(4):
        take = jnp.logical_and((source_lane - 32) // 2 == column, part == component)
        take = jnp.logical_and(take, jnp.logical_and(source_lane >= 32, source_lane < 96))
        scale = 0.125 * STEP_FLOW if component < 3 else 0.125
        pairs = jnp.concatenate(
            [
                summed[component, pl.ds(half * FINE, FLOW, stride=2), :]
                + summed[component, pl.ds(half * FINE + 1, FLOW, stride=2), :]
                for half in range(2)
            ],
            axis=0,
        )
        done = done + exact_dot(pairs * scale, jnp.where(take, 1.0, 0.0))
    out_ref[...] = done


def merge_kernel(group_ref, own_ref, one_ref, two_ref, three_ref, out_ref):
    group = group_ref[0]
    lanes = lane_ids(64)
    merged = jnp.zeros((64, LANES), F32)
    for step, ref in enumerate((own_ref, one_ref, two_ref, three_ref)):
        owner = (group - step + 4) % 4
        turned = pltpu.roll(ref[...], (32 * owner - 32 * group + LANES) % LANES, 1)
        merged = jnp.where(lanes // 32 == owner, turned, merged)
    for row in range(2):
        out_ref[:, row, :] = merged[row * FLOW : (row + 1) * FLOW, :]


def call(kernel, outs, scratch, *args, scalars=0):
    vmem = pl.BlockSpec(memory_space=pltpu.VMEM)
    smem = pl.BlockSpec(memory_space=pltpu.SMEM)
    shapes = [jax.ShapeDtypeStruct(shape, F32) for shape in outs]
    return pl.pallas_call(
        kernel,
        out_shape=shapes if len(shapes) > 1 else shapes[0],
        in_specs=[smem] * scalars + [vmem] * (len(args) - scalars),
        out_specs=[vmem] * len(shapes) if len(shapes) > 1 else vmem,
        scratch_shapes=[pltpu.VMEM(shape, F32) for shape in scratch],
        name=kernel.__name__,
    )(*args)


def shifted(value, axis, shift):
    count = lax.axis_size(axis)
    return lax.ppermute(value, axis, [(i, (i + shift) % count) for i in range(count)])


def to_next_block(value):
    groups, blocks = lax.axis_size("grp"), lax.axis_size("gy")
    pairs = [(j, (j + 1) % blocks) for j in range(blocks)]
    base = (groups - 1) * blocks
    pairs += [(base + j, base + (j - 1) % blocks) for j in range(blocks)]
    return lax.ppermute(value, ("grp", "gy"), pairs)


def on_device(flow_fields, level_set, band_tiles, nozzle_phase):
    group = lax.axis_index("grp").astype(jnp.int32)[None]
    message = (320, LANES)
    to_one, to_two, to_three, keep = call(
        pack_kernel,
        [message, message, message, (336, LANES)],
        [(2, 4 * FINE, LANES)],
        group,
        flow_fields[0],
        level_set[0],
        band_tiles[:, 0, :],
        nozzle_phase,
        scalars=1,
    )
    got = [shifted(value, "grp", step + 1) for step, value in enumerate((to_one, to_two, to_three))]
    tile, edge = call(assemble_kernel, [(400, LANES), (144, LANES)], [], group, keep, *got, scalars=1)
    edge = to_next_block(edge)
    fixed, up, down = call(
        edge_kernel, [(400, LANES), (272, LANES), (272, LANES)], [], group, tile, edge, scalars=1
    )
    old_left, old_right = shifted(up, "gx", 1), shifted(down, "gx", -1)
    own, speeds = call(
        first_kernel, [(320, LANES), (3, 4, FINE, LANES)], [(4, 80, LANES)], fixed, old_left, old_right
    )
    left, right = shifted(own, "gx", 1), shifted(own, "gx", -1)
    newer, up, down = call(
        second_kernel,
        [(512, LANES), (288, LANES), (288, LANES)],
        [(6, 80, LANES)],
        own,
        left,
        right,
        fixed,
        old_left,
        old_right,
        speeds,
    )
    newer_left, newer_right = shifted(up, "gx", 1), shifted(down, "gx", -1)
    result = call(
        third_kernel,
        [(64, LANES)],
        [(8, 80, LANES), (8, 80, LANES), (6, FINE, LANES), (4, 80, LANES), (4, 2 * FINE, LANES)],
        newer,
        newer_left,
        newer_right,
        own,
        left,
        right,
        fixed,
        old_left,
        old_right,
        speeds,
    )
    got = [shifted(result, "grp", step + 1) for step in range(3)]
    return call(merge_kernel, [(FLOW, 2, LANES)], [], group, result, *got, scalars=1)[None]


def solution(mesh):
    placed = (
        P("grp", None, "gx", "gy"),
        P("grp", None, "gx", "gy"),
        P(None, "gx", "gy"),
        P("gx", "gy"),
    )
    return jax.shard_map(
        on_device, mesh=mesh, in_specs=placed, out_specs=P("grp", None, "gx", "gy"), check_vma=False
    )
```

profile of v0, /device:TPU:1, one launch (start us, length us, event | category | flops | bytes accessed | tf_op | source)
XLA Modules:
  0.0 81.7 jit_solution(6031043727097985740)
XLA Ops:
  0.0 4.8 %pack_kernel.1 = (f32[320,128]{1,0:T(8,128)}, f32[320,128]{1,0:T(8,128)}, f32[320,128]{1,0:T(8,128)}, f32[336,128]{1,0:T(8,128)}) custom-call(s32[1]{0:T(128)} %bitcast.group_ref, f32[32,2,128]{2,1,0:T(2,128)} %bitcast.6, f32[64,4,256]{2,1,0:T(4,128)} %bitcast.5, s32[8,16]{1,0:T(8,128)} %bitcast.7, s32[4,256]{1,0:T(4,128)} %nozzle_ref.1), custom_call_target="tpu_custom_call" | custom-call | tf_op jit(solution)/shard_map/pack_kernel/pallas_call | solution.py:440
  4.8 4.1 %collective-permute-start = (f32[320,128]{1,0:T(8,128)}, f32[320,128]{1,0:T(8,128)S(1)}, u32[]{:S(2)}, u32[]{:S(2)}) collective-permute-start(f32[320,128]{1,0:T(8,128)} %get-tuple-element.20), channel_id=1, source_target_pairs={{0,64},{64,128},{128,192},{192,0},{1,65},{65,129},{129,193},{193,1... | collective-permute-start | bytes 491528 | tf_op jit(solution)/shard_map/ppermute | solution.py:452
  9.0 1.9 %collective-permute-start.1 = (f32[320,128]{1,0:T(8,128)}, f32[320,128]{1,0:T(8,128)S(1)}, u32[]{:S(2)}, u32[]{:S(2)}) collective-permute-start(f32[320,128]{1,0:T(8,128)} %get-tuple-element.21), channel_id=1, source_target_pairs={{0,128},{64,192},{128,0},{192,64},{1,129},{65,193},{129,1},{193,65... | collective-permute-start | bytes 491528 | tf_op jit(solution)/shard_map/ppermute | solution.py:452
  10.9 1.8 %collective-permute-done.one_ref = f32[320,128]{1,0:T(8,128)S(1)} collective-permute-done((f32[320,128]{1,0:T(8,128)}, f32[320,128]{1,0:T(8,128)S(1)}, u32[]{:S(2)}, u32[]{:S(2)}) %collective-permute-start) | collective-permute-done | bytes 163872 | tf_op jit(solution)/shard_map/ppermute | solution.py:452
  12.7 5.8 %collective-permute-done.1.two_ref = f32[320,128]{1,0:T(8,128)S(1)} collective-permute-done((f32[320,128]{1,0:T(8,128)}, f32[320,128]{1,0:T(8,128)S(1)}, u32[]{:S(2)}, u32[]{:S(2)}) %collective-permute-start.1) | collective-permute-done | bytes 163872 | tf_op jit(solution)/shard_map/ppermute | solution.py:452
  18.5 0.6 collective-permute-done.2.three_ref
  19.1 0.1 copy-done.5
  19.1 0.6 copy-done.6
  19.7 1.9 %assemble_kernel.1 = (f32[400,128]{1,0:T(8,128)}, f32[144,128]{1,0:T(8,128)}) custom-call(s32[1]{0:T(128)} %bitcast.group_ref, f32[336,128]{1,0:T(8,128)} %get-tuple-element.19.keep_ref, f32[320,128]{1,0:T(8,128)} %copy-done.4, f32[320,128]{1,0:T(8,128)} %copy-done.5, f32[320,128]{1,0:T(8,128)} %copy-done.6), custom_call_target="tpu_custom_call" | custom-call | tf_op jit(solution)/shard_map/assemble_kernel/pallas_call | solution.py:440
  21.7 0.7 collective-permute-start.3
  22.4 0.6 copy-done.9
  23.0 1.9 %edge_kernel.1 = (f32[400,128]{1,0:T(8,128)}, f32[272,128]{1,0:T(8,128)}, f32[272,128]{1,0:T(8,128)}) custom-call(s32[1]{0:T(128)} %bitcast.group_ref, f32[400,128]{1,0:T(8,128)} %get-tuple-element.23.tile_ref, f32[144,128]{1,0:T(8,128)} %copy-done.9), custom_call_target="tpu_custom_call" | custom-call | tf_op jit(solution)/shard_map/edge_kernel/pallas_call | solution.py:440
  24.9 4.8 %collective-permute-start.5 = (f32[272,128]{1,0:T(8,128)}, f32[272,128]{1,0:T(8,128)S(1)}, u32[]{:S(2)}, u32[]{:S(2)}) collective-permute-start(f32[272,128]{1,0:T(8,128)} %get-tuple-element.27), channel_id=1, source_target_pairs={{0,60},{4,0},{8,4},{12,8},{16,12},{20,16},{24,20},{28,24},{32,28},... | collective-permute-start | bytes 417800 | tf_op jit(solution)/shard_map/ppermute | solution.py:452
  29.7 2.6 %collective-permute-done.4.left_ref.old_left = f32[272,128]{1,0:T(8,128)S(1)} collective-permute-done((f32[272,128]{1,0:T(8,128)}, f32[272,128]{1,0:T(8,128)S(1)}, u32[]{:S(2)}, u32[]{:S(2)}) %collective-permute-start.4) | collective-permute-done | bytes 139296 | tf_op jit(solution)/shard_map/ppermute | solution.py:452
  32.3 0.6 copy-done
  33.0 0.1 copy-done.1
  33.0 3.6 %first_kernel.1 = (f32[320,128]{1,0:T(8,128)}, f32[3,4,64,128]{3,2,1,0:T(8,128)}) custom-call(f32[400,128]{1,0:T(8,128)} %get-tuple-element.25.fixed_ref, f32[272,128]{1,0:T(8,128)} %copy-done, f32[272,128]{1,0:T(8,128)} %copy-done.1), custom_call_target="tpu_custom_call" | custom-call | tf_op jit(solution)/shard_map/first_kernel/pallas_call | solution.py:440
  36.6 3.5 %collective-permute-start.7 = (f32[320,128]{1,0:T(8,128)}, f32[320,128]{1,0:T(8,128)S(1)}, u32[]{:S(2)}, u32[]{:S(2)}) collective-permute-start(f32[320,128]{1,0:T(8,128)} %get-tuple-element.28.own_ref.older), channel_id=1, source_target_pairs={{0,60},{4,0},{8,4},{12,8},{16,12},{20,16},{24,20},{28,24},{32,28},... | collective-permute-start | bytes 491528 | tf_op jit(solution)/shard_map/ppermute | solution.py:452
  40.1 2.6 %collective-permute-done.7.right_ref.older_right = f32[320,128]{1,0:T(8,128)S(1)} collective-permute-done((f32[320,128]{1,0:T(8,128)}, f32[320,128]{1,0:T(8,128)S(1)}, u32[]{:S(2)}, u32[]{:S(2)}) %collective-permute-start.7) | collective-permute-done | bytes 163872 | tf_op jit(solution)/shard_map/ppermute | solution.py:452
  42.7 3.9 %collective-permute-done.6.left_ref.older_left = f32[320,128]{1,0:T(8,128)S(1)} collective-permute-done((f32[320,128]{1,0:T(8,128)}, f32[320,128]{1,0:T(8,128)S(1)}, u32[]{:S(2)}, u32[]{:S(2)}) %collective-permute-start.6) | collective-permute-done | bytes 163872 | tf_op jit(solution)/shard_map/ppermute | solution.py:452
  46.6 0.6 copy-done.3
  47.2 4.1 %second_kernel.1 = (f32[512,128]{1,0:T(8,128)}, f32[288,128]{1,0:T(8,128)}, f32[288,128]{1,0:T(8,128)}) custom-call(f32[320,128]{1,0:T(8,128)} %get-tuple-element.28.own_ref.older, f32[320,128]{1,0:T(8,128)} %copy-done.3, f32[320,128]{1,0:T(8,128)} %copy-done.2, f32[400,128]{1,0:T(8,128)} %get-tuple-element.25.fixed_ref, f32[272,128]{1,0:T(8,128)} %copy-done, ...), custom_call_target="tpu_custom_call" | custom-call | tf_op jit(solution)/shard_map/second_kernel/pallas_call | solution.py:440
  51.4 3.6 %collective-permute-start.9 = (f32[288,128]{1,0:T(8,128)}, f32[288,128]{1,0:T(8,128)S(1)}, u32[]{:S(2)}, u32[]{:S(2)}) collective-permute-start(f32[288,128]{1,0:T(8,128)} %get-tuple-element.32), channel_id=1, source_target_pairs={{0,60},{4,0},{8,4},{12,8},{16,12},{20,16},{24,20},{28,24},{32,28},... | collective-permute-start | bytes 442376 | tf_op jit(solution)/shard_map/ppermute | solution.py:452
  54.9 2.7 %collective-permute-done.8.left_ref = f32[288,128]{1,0:T(8,128)S(1)} collective-permute-done((f32[288,128]{1,0:T(8,128)}, f32[288,128]{1,0:T(8,128)S(1)}, u32[]{:S(2)}, u32[]{:S(2)}) %collective-permute-start.8) | collective-permute-done | bytes 147488 | tf_op jit(solution)/shard_map/ppermute | solution.py:452
  57.7 0.7 copy-done.7
  58.4 6.4 %third_kernel.1.own_ref = f32[64,128]{1,0:T(8,128)} custom-call(f32[512,128]{1,0:T(8,128)} %get-tuple-element.30.own_ref, f32[288,128]{1,0:T(8,128)} %copy-done.7, f32[288,128]{1,0:T(8,128)} %copy-done.8, f32[320,128]{1,0:T(8,128)} %get-tuple-element.28.own_ref.older, f32[320,128]{1,0:T(8,128)} %copy-done.3, f32[320,128]{1,0:T(8,128)} %copy-done.2, ...), custom_call_target="tpu_custom_call" | custom-call | tf_op jit(solution)/shard_map/third_kernel/pallas_call | solution.py:440
  64.8 9.6 %collective-permute-start.12 = (f32[64,128]{1,0:T(8,128)}, f32[64,128]{1,0:T(8,128)S(1)}, u32[]{:S(2)}, u32[]{:S(2)}) collective-permute-start(f32[64,128]{1,0:T(8,128)} %third_kernel.1.own_ref), channel_id=1, source_target_pairs={{0,192},{64,0},{128,64},{192,128},{1,193},{65,1},{129,65},{193,129... | collective-permute-start | bytes 98312 | tf_op jit(solution)/shard_map/ppermute | solution.py:452
  74.4 3.1 %collective-permute-start.10 = (f32[64,128]{1,0:T(8,128)}, f32[64,128]{1,0:T(8,128)S(1)}, u32[]{:S(2)}, u32[]{:S(2)}) collective-permute-start(f32[64,128]{1,0:T(8,128)} %third_kernel.1.own_ref), channel_id=1, source_target_pairs={{0,64},{64,128},{128,192},{192,0},{1,65},{65,129},{129,193},{193,1... | collective-permute-start | bytes 98312 | tf_op jit(solution)/shard_map/ppermute | solution.py:452
  77.6 1.3 %collective-permute-done.11.two_ref = f32[64,128]{1,0:T(8,128)S(1)} collective-permute-done((f32[64,128]{1,0:T(8,128)}, f32[64,128]{1,0:T(8,128)S(1)}, u32[]{:S(2)}, u32[]{:S(2)}) %collective-permute-start.11) | collective-permute-done | bytes 32800 | tf_op jit(solution)/shard_map/ppermute | solution.py:452
  78.9 0.6 copy-done.11
  79.5 0.6 copy-done.12
  80.1 1.5 %merge_kernel.1 = f32[32,2,128]{2,1,0:T(2,128)} custom-call(s32[1]{0:T(128)} %bitcast.group_ref, f32[64,128]{1,0:T(8,128)} %third_kernel.1.own_ref, f32[64,128]{1,0:T(8,128)} %copy-done.12, f32[64,128]{1,0:T(8,128)} %copy-done.11, f32[64,128]{1,0:T(8,128)} %copy-done.10), custom_call_target="tpu_custom_call" | custom-call | tf_op jit(solution)/shard_map/merge_kernel/pallas_call | solution.py:440
  (27 shorter events, 0.1 us)
Async XLA Ops:
  4.8 7.9 %collective-permute-start = (f32[320,128]{1,0:T(8,128)}, f32[320,128]{1,0:T(8,128)S(1)}, u32[]{:S(2)}, u32[]{:S(2)}) collective-permute-start(f32[320,128]{1,0:T(8,128)} %get-tuple-element.20), channel_id=1, source_target_pairs={{0,64},{64,128},{128,192},{192,0},{1,65},{65,129},{129,193},{193,1... | collective-permute-start | bytes 491528 | tf_op jit(solution)/shard_map/ppermute | solution.py:452
  9.0 9.5 %collective-permute-start.1 = (f32[320,128]{1,0:T(8,128)}, f32[320,128]{1,0:T(8,128)S(1)}, u32[]{:S(2)}, u32[]{:S(2)}) collective-permute-start(f32[320,128]{1,0:T(8,128)} %get-tuple-element.21), channel_id=1, source_target_pairs={{0,128},{64,192},{128,0},{192,64},{1,129},{65,193},{129,1},{193,65... | collective-permute-start | bytes 491528 | tf_op jit(solution)/shard_map/ppermute | solution.py:452
  10.9 8.2 %collective-permute-start.2 = (f32[320,128]{1,0:T(8,128)}, f32[320,128]{1,0:T(8,128)S(1)}, u32[]{:S(2)}, u32[]{:S(2)}) collective-permute-start(f32[320,128]{1,0:T(8,128)} %get-tuple-element.22), channel_id=1, source_target_pairs={{0,192},{64,0},{128,64},{192,128},{1,193},{65,1},{129,65},{193,129... | collective-permute-start | bytes 491528 | tf_op jit(solution)/shard_map/ppermute | solution.py:452
  12.7 6.4 %copy-start.4 = (f32[320,128]{1,0:T(8,128)}, f32[320,128]{1,0:T(8,128)S(1)}, u32[]{:S(2)}) copy-start(f32[320,128]{1,0:T(8,128)S(1)} %collective-permute-done.one_ref) | copy-start | bytes 491524
  18.5 0.7 copy-start.5
  19.1 0.7 copy-start.6
  21.7 0.7 collective-permute-start.3
  22.4 0.6 copy-start.9
  24.9 7.5 %collective-permute-start.4 = (f32[272,128]{1,0:T(8,128)}, f32[272,128]{1,0:T(8,128)S(1)}, u32[]{:S(2)}, u32[]{:S(2)}) collective-permute-start(f32[272,128]{1,0:T(8,128)} %get-tuple-element.26), channel_id=1, source_target_pairs={{0,4},{4,8},{8,12},{12,16},{16,20},{20,24},{24,28},{28,32},{32,36}... | collective-permute-start | bytes 417800 | tf_op jit(solution)/shard_map/ppermute | solution.py:452
  24.9 7.5 %collective-permute-start.5 = (f32[272,128]{1,0:T(8,128)}, f32[272,128]{1,0:T(8,128)S(1)}, u32[]{:S(2)}, u32[]{:S(2)}) collective-permute-start(f32[272,128]{1,0:T(8,128)} %get-tuple-element.27), channel_id=1, source_target_pairs={{0,60},{4,0},{8,4},{12,8},{16,12},{20,16},{24,20},{28,24},{32,28},... | collective-permute-start | bytes 417800 | tf_op jit(solution)/shard_map/ppermute | solution.py:452
  32.3 0.6 copy-start
  32.3 0.7 copy-start.1
  36.6 6.1 %collective-permute-start.7 = (f32[320,128]{1,0:T(8,128)}, f32[320,128]{1,0:T(8,128)S(1)}, u32[]{:S(2)}, u32[]{:S(2)}) collective-permute-start(f32[320,128]{1,0:T(8,128)} %get-tuple-element.28.own_ref.older), channel_id=1, source_target_pairs={{0,60},{4,0},{8,4},{12,8},{16,12},{20,16},{24,20},{28,24},{32,28},... | collective-permute-start | bytes 491528 | tf_op jit(solution)/shard_map/ppermute | solution.py:452
  40.1 6.5 %collective-permute-start.6 = (f32[320,128]{1,0:T(8,128)}, f32[320,128]{1,0:T(8,128)S(1)}, u32[]{:S(2)}, u32[]{:S(2)}) collective-permute-start(f32[320,128]{1,0:T(8,128)} %get-tuple-element.28.own_ref.older), channel_id=1, source_target_pairs={{0,4},{4,8},{8,12},{12,16},{16,20},{20,24},{24,28},{28,32},{32,36}... | collective-permute-start | bytes 491528 | tf_op jit(solution)/shard_map/ppermute | solution.py:452
  42.7 3.9 %copy-start.2 = (f32[320,128]{1,0:T(8,128)}, f32[320,128]{1,0:T(8,128)S(1)}, u32[]{:S(2)}) copy-start(f32[320,128]{1,0:T(8,128)S(1)} %collective-permute-done.7.right_ref.older_right) | copy-start | bytes 491524
  46.6 0.7 copy-start.3
  51.4 6.3 %collective-permute-start.8 = (f32[288,128]{1,0:T(8,128)}, f32[288,128]{1,0:T(8,128)S(1)}, u32[]{:S(2)}, u32[]{:S(2)}) collective-permute-start(f32[288,128]{1,0:T(8,128)} %get-tuple-element.31), channel_id=1, source_target_pairs={{0,4},{4,8},{8,12},{12,16},{16,20},{20,24},{24,28},{28,32},{32,36}... | collective-permute-start | bytes 442376 | tf_op jit(solution)/shard_map/ppermute | solution.py:452
  51.4 6.3 %collective-permute-start.9 = (f32[288,128]{1,0:T(8,128)}, f32[288,128]{1,0:T(8,128)S(1)}, u32[]{:S(2)}, u32[]{:S(2)}) collective-permute-start(f32[288,128]{1,0:T(8,128)} %get-tuple-element.32), channel_id=1, source_target_pairs={{0,60},{4,0},{8,4},{12,8},{16,12},{20,16},{24,20},{28,24},{32,28},... | collective-permute-start | bytes 442376 | tf_op jit(solution)/shard_map/ppermute | solution.py:452
  57.7 0.7 copy-start.7
  57.7 0.7 copy-start.8
  64.8 12.8 %collective-permute-start.12 = (f32[64,128]{1,0:T(8,128)}, f32[64,128]{1,0:T(8,128)S(1)}, u32[]{:S(2)}, u32[]{:S(2)}) collective-permute-start(f32[64,128]{1,0:T(8,128)} %third_kernel.1.own_ref), channel_id=1, source_target_pairs={{0,192},{64,0},{128,64},{192,128},{1,193},{65,1},{129,65},{193,129... | collective-permute-start | bytes 98312 | tf_op jit(solution)/shard_map/ppermute | solution.py:452
  74.4 4.5 %collective-permute-start.11 = (f32[64,128]{1,0:T(8,128)}, f32[64,128]{1,0:T(8,128)S(1)}, u32[]{:S(2)}, u32[]{:S(2)}) collective-permute-start(f32[64,128]{1,0:T(8,128)} %third_kernel.1.own_ref), channel_id=1, source_target_pairs={{0,128},{64,192},{128,0},{192,64},{1,129},{65,193},{129,1},{193,65... | collective-permute-start | bytes 98312 | tf_op jit(solution)/shard_map/ppermute | solution.py:452
  74.4 4.5 %collective-permute-start.10 = (f32[64,128]{1,0:T(8,128)}, f32[64,128]{1,0:T(8,128)S(1)}, u32[]{:S(2)}, u32[]{:S(2)}) collective-permute-start(f32[64,128]{1,0:T(8,128)} %third_kernel.1.own_ref), channel_id=1, source_target_pairs={{0,64},{64,128},{128,192},{192,0},{1,65},{65,129},{129,193},{193,1... | collective-permute-start | bytes 98312 | tf_op jit(solution)/shard_map/ppermute | solution.py:452
  77.6 1.3 %copy-start.10 = (f32[64,128]{1,0:T(8,128)}, f32[64,128]{1,0:T(8,128)S(1)}, u32[]{:S(2)}) copy-start(f32[64,128]{1,0:T(8,128)S(1)} %collective-permute-done.12.three_ref) | copy-start | bytes 98308
  78.9 0.6 copy-start.11
  79.5 0.6 copy-start.12
where the time goes:
time: 82 us; the launch traced here: 81.7 us
  starting transfers between devices  31.4 us (38%)
  Pallas kernels  24.3 us (30%)
  waiting for transfers between devices  21.4 us (26%)
  local copies, waits for them, and re-layouts  4.56 us (6%)
    ppermute x12, starting transfers between devices, shifted(): lax.ppermute(value, axis, [(i, (i + shift) % count) for i in range(count)])  30.7 us
    pallas_call x7, Pallas kernels, call(): pl.pallas_call(kernel, out_shape=shapes if len(shapes) > 1 else shapes[0]...  24.3 us
    ppermute x12, waiting for transfers between devices, shifted(): lax.ppermute(value, axis, [(i, (i + shift) % count) for i in range(count)])  21.4 us
    unnamed x26, local copies, waits for them, and re-layouts  4.56 us
  transfers between devices with their start and end apart: 13, of which 8 were waited for; matrix products, arithmetic and copies ran while one was open for 0% of the time, Pallas kernels for 0%

commit v1 on v0

--- a/solution.py
+++ b/solution.py
@@ -63,12 +63,9 @@
         for row in range(2):
             out_ref[row * FLOW : (row + 1) * FLOW, :] = pltpu.roll(flow_ref[:, row, :], turn, 1)
 
-        def copy(index, carry, out_ref=out_ref, target=target):
-            at = pl.multiple_of(index * 32, 32)
-            out_ref[pl.ds(64 + at, 32), :] = quarter(ring[0, pl.ds(at, 32), :], ring[1, pl.ds(at, 32), :], target)
-            return carry
-
-        lax.fori_loop(0, 8, copy, 0)
+        for row in range(4):
+            at = row * FINE
+            out_ref[64 + at : 128 + at, :] = quarter(ring[0, at : at + FINE, :], ring[1, at : at + FINE, :], target)
     keep_ref[320:328, :] = quarter(flags[:, :LANES], flags[:, LANES:], group)
     keep_ref[328:332, :] = quarter(phases[:, :LANES], phases[:, LANES:], group)
     keep_ref[332:336, :] = jnp.zeros((4, LANES), F32)
@@ -433,18 +430,21 @@
         out_ref[:, row, :] = merged[row * FLOW : (row + 1) * FLOW, :]
 
 
-def call(kernel, outs, scratch, *args, scalars=0):
+def call(kernel, outs, scratch, *args, scalars=0, outer=False, last=False):
     vmem = pl.BlockSpec(memory_space=pltpu.VMEM)
     smem = pl.BlockSpec(memory_space=pltpu.SMEM)
-    shapes = [jax.ShapeDtypeStruct(shape, F32) for shape in outs]
+    shapes = [jax.ShapeDtypeStruct(shape, F32) if last else pltpu.VMEM(shape, F32) for shape in outs]
+    held = list(args[scalars:])
+    if not outer:
+        held = [pltpu.with_memory_space_constraint(value, pltpu.VMEM) for value in held]
     return pl.pallas_call(
         kernel,
         out_shape=shapes if len(shapes) > 1 else shapes[0],
-        in_specs=[smem] * scalars + [vmem] * (len(args) - scalars),
+        in_specs=[smem] * scalars + [vmem] * len(held),
         out_specs=[vmem] * len(shapes) if len(shapes) > 1 else vmem,
         scratch_shapes=[pltpu.VMEM(shape, F32) for shape in scratch],
         name=kernel.__name__,
-    )(*args)
+    )(*args[:scalars], *held)
 
 
 def shifted(value, axis, shift):
@@ -473,6 +473,7 @@
         band_tiles[:, 0, :],
         nozzle_phase,
         scalars=1,
+        outer=True,
     )
     got = [shifted(value, "grp", step + 1) for step, value in enumerate((to_one, to_two, to_three))]
     tile, edge = call(assemble_kernel, [(400, LANES), (144, LANES)], [], group, keep, *got, scalars=1)
@@ -514,7 +515,7 @@
         speeds,
     )
     got = [shifted(result, "grp", step + 1) for step in range(3)]
-    return call(merge_kernel, [(FLOW, 2, LANES)], [], group, result, *got, scalars=1)[None]
+    return call(merge_kernel, [(FLOW, 2, LANES)], [], group, result, *got, scalars=1, last=True)[None]
 
 
 def solution(mesh):

time: 82 us -> 64.5 us (0.79); the launches traced: 81.7 us -> 63.3 us
  Pallas kernels: 24.3 us -> 10.3 us
  local copies, waits for them, and re-layouts: 4.56 us -> 0 us
    pallas_call x7, Pallas kernels: 24.3 us -> 10.3 us  [call(): pl.pallas_call(kernel, out_shape=shapes if len(shapes) > 1 else shapes[0]...]
    unnamed x26 -> x0, local copies, waits for them, and re-layouts: 4.56 us -> none
where the time goes in v1:
time: 64.5 us; the launch traced here: 63.3 us
  starting transfers between devices  31.8 us (49%)
  waiting for transfers between devices  21.1 us (33%)
  Pallas kernels  10.3 us (16%)
    ppermute x12, starting transfers between devices, shifted(): lax.ppermute(value, axis, [(i, (i + shift) % count) for i in range(count)])  31.1 us
    ppermute x12, waiting for transfers between devices, shifted(): lax.ppermute(value, axis, [(i, (i + shift) % count) for i in range(count)])  21.1 us
    pallas_call x7, Pallas kernels, call(): pl.pallas_call(kernel, out_shape=shapes if len(shapes) > 1 else shapes[0]...  10.3 us
  transfers between devices with their start and end apart: 13, of which 8 were waited for; matrix products, arithmetic and copies ran while one was open for 0% of the time, Pallas kernels for 0%

profile of v1, /device:TPU:1, one launch (start us, length us, event | category | flops | bytes accessed | tf_op | source)
XLA Modules:
  0.0 63.3 jit_solution(15227173463652721458)
XLA Ops:
  0.0 1.4 %pack_kernel.1 = (f32[320,128]{1,0:T(8,128)S(1)}, f32[320,128]{1,0:T(8,128)S(1)}, f32[320,128]{1,0:T(8,128)S(1)}, f32[336,128]{1,0:T(8,128)S(1)}) custom-call(s32[1]{0:T(128)} %bitcast.group_ref, f32[32,2,128]{2,1,0:T(2,128)} %bitcast.6, f32[64,4,256]{2,1,0:T(4,128)} %bitcast.5, s32[8,16]{1,0:T(8,128)} %bitcast.7, s32[4,256]{1,0:T(4,128)} %nozzle_ref.1), custom_call_target="tpu_custom_call" | custom-call | tf_op jit(solution)/shard_map/pack_kernel/pallas_call | solution.py:440
  1.4 4.2 %collective-permute-start = (f32[320,128]{1,0:T(8,128)S(1)}, f32[320,128]{1,0:T(8,128)S(1)}, u32[]{:S(2)}, u32[]{:S(2)}) collective-permute-start(f32[320,128]{1,0:T(8,128)S(1)} %get-tuple-element.20), channel_id=1, source_target_pairs={{0,64},{64,128},{128,192},{192,0},{1,65},{65,129},{129,193},{193,1... | collective-permute-start | bytes 491528 | tf_op jit(solution)/shard_map/ppermute | solution.py:452
  5.6 1.9 %collective-permute-start.1 = (f32[320,128]{1,0:T(8,128)S(1)}, f32[320,128]{1,0:T(8,128)S(1)}, u32[]{:S(2)}, u32[]{:S(2)}) collective-permute-start(f32[320,128]{1,0:T(8,128)S(1)} %get-tuple-element.21), channel_id=1, source_target_pairs={{0,128},{64,192},{128,0},{192,64},{1,129},{65,193},{129,1},{193,65... | collective-permute-start | bytes 491528 | tf_op jit(solution)/shard_map/ppermute | solution.py:452
  7.5 0.0 collective-permute-start.2
  7.5 1.4 %collective-permute-done.one_ref = f32[320,128]{1,0:T(8,128)S(1)} collective-permute-done((f32[320,128]{1,0:T(8,128)S(1)}, f32[320,128]{1,0:T(8,128)S(1)}, u32[]{:S(2)}, u32[]{:S(2)}) %collective-permute-start) | collective-permute-done | bytes 163872 | tf_op jit(solution)/shard_map/ppermute | solution.py:452
  8.9 5.9 %collective-permute-done.1.two_ref = f32[320,128]{1,0:T(8,128)S(1)} collective-permute-done((f32[320,128]{1,0:T(8,128)S(1)}, f32[320,128]{1,0:T(8,128)S(1)}, u32[]{:S(2)}, u32[]{:S(2)}) %collective-permute-start.1) | collective-permute-done | bytes 163872 | tf_op jit(solution)/shard_map/ppermute | solution.py:452
  14.8 0.7 %collective-permute-done.2.three_ref = f32[320,128]{1,0:T(8,128)S(1)} collective-permute-done((f32[320,128]{1,0:T(8,128)S(1)}, f32[320,128]{1,0:T(8,128)S(1)}, u32[]{:S(2)}, u32[]{:S(2)}) %collective-permute-start.2) | collective-permute-done | bytes 163872 | tf_op jit(solution)/shard_map/ppermute | solution.py:452
  15.5 0.2 assemble_kernel.1
  15.6 0.7 %collective-permute-start.3 = (f32[144,128]{1,0:T(8,128)S(1)}, f32[144,128]{1,0:T(8,128)S(1)}, u32[]{:S(2)}, u32[]{:S(2)}) collective-permute-start(f32[144,128]{1,0:T(8,128)S(1)} %get-tuple-element.24), channel_id=1, source_target_pairs={{0,1},{1,2},{2,3},{3,0},{192,195},{193,192},{194,193},{195,194},{4... | collective-permute-start | bytes 221192 | tf_op jit(solution)/shard_map/ppermute | solution.py:460
  16.3 0.0 collective-permute-done.3.edge_ref
  16.3 0.1 edge_kernel.1
  16.4 0.1 collective-permute-start.4
  16.5 4.9 %collective-permute-start.5 = (f32[272,128]{1,0:T(8,128)S(1)}, f32[272,128]{1,0:T(8,128)S(1)}, u32[]{:S(2)}, u32[]{:S(2)}) collective-permute-start(f32[272,128]{1,0:T(8,128)S(1)} %get-tuple-element.27), channel_id=1, source_target_pairs={{0,60},{4,0},{8,4},{12,8},{16,12},{20,16},{24,20},{28,24},{32,28},... | collective-permute-start | bytes 417800 | tf_op jit(solution)/shard_map/ppermute | solution.py:452
  21.4 2.4 %collective-permute-done.4.left_ref.old_left = f32[272,128]{1,0:T(8,128)S(1)} collective-permute-done((f32[272,128]{1,0:T(8,128)S(1)}, f32[272,128]{1,0:T(8,128)S(1)}, u32[]{:S(2)}, u32[]{:S(2)}) %collective-permute-start.4) | collective-permute-done | bytes 139296 | tf_op jit(solution)/shard_map/ppermute | solution.py:452
  23.8 0.0 collective-permute-done.5.right_ref.old_right
  23.8 1.8 %first_kernel.1 = (f32[320,128]{1,0:T(8,128)S(1)}, f32[3,4,64,128]{3,2,1,0:T(8,128)S(1)}) custom-call(f32[400,128]{1,0:T(8,128)S(1)} %get-tuple-element.25.fixed_ref, f32[272,128]{1,0:T(8,128)S(1)} %collective-permute-done.4.left_ref.old_left, f32[272,128]{1,0:T(8,128)S(1)} %collective-permute-done.5.right_ref.old_right), custom_call_target="tpu_custom_call" | custom-call | tf_op jit(solution)/shard_map/first_kernel/pallas_call | solution.py:440
  25.6 3.7 %collective-permute-start.7 = (f32[320,128]{1,0:T(8,128)S(1)}, f32[320,128]{1,0:T(8,128)S(1)}, u32[]{:S(2)}, u32[]{:S(2)}) collective-permute-start(f32[320,128]{1,0:T(8,128)S(1)} %get-tuple-element.28.own_ref.older), channel_id=1, source_target_pairs={{0,60},{4,0},{8,4},{12,8},{16,12},{20,16},{24,20},{28,24},{32,28},... | collective-permute-start | bytes 491528 | tf_op jit(solution)/shard_map/ppermute | solution.py:452
  29.3 2.3 %collective-permute-done.7.right_ref.older_right = f32[320,128]{1,0:T(8,128)S(1)} collective-permute-done((f32[320,128]{1,0:T(8,128)S(1)}, f32[320,128]{1,0:T(8,128)S(1)}, u32[]{:S(2)}, u32[]{:S(2)}) %collective-permute-start.7) | collective-permute-done | bytes 163872 | tf_op jit(solution)/shard_map/ppermute | solution.py:452
  31.6 4.0 %collective-permute-done.6.left_ref.older_left = f32[320,128]{1,0:T(8,128)S(1)} collective-permute-done((f32[320,128]{1,0:T(8,128)S(1)}, f32[320,128]{1,0:T(8,128)S(1)}, u32[]{:S(2)}, u32[]{:S(2)}) %collective-permute-start.6) | collective-permute-done | bytes 163872 | tf_op jit(solution)/shard_map/ppermute | solution.py:452
  35.6 1.9 %second_kernel.1 = (f32[512,128]{1,0:T(8,128)S(1)}, f32[288,128]{1,0:T(8,128)S(1)}, f32[288,128]{1,0:T(8,128)S(1)}) custom-call(f32[320,128]{1,0:T(8,128)S(1)} %get-tuple-element.28.own_ref.older, f32[320,128]{1,0:T(8,128)S(1)} %collective-permute-done.6.left_ref.older_left, f32[320,128]{1,0:T(8,128)S(1)} %collective-permute-done.7.right_ref.older_right, ...), custom_call_target="tpu_custom_call" | custom-call | tf_op jit(solution)/shard_map/second_kernel/pallas_call | solution.py:440
  37.5 0.1 collective-permute-start.8
  37.6 3.6 %collective-permute-start.9 = (f32[288,128]{1,0:T(8,128)S(1)}, f32[288,128]{1,0:T(8,128)S(1)}, u32[]{:S(2)}, u32[]{:S(2)}) collective-permute-start(f32[288,128]{1,0:T(8,128)S(1)} %get-tuple-element.32), channel_id=1, source_target_pairs={{0,60},{4,0},{8,4},{12,8},{16,12},{20,16},{24,20},{28,24},{32,28},... | collective-permute-start | bytes 442376 | tf_op jit(solution)/shard_map/ppermute | solution.py:452
  41.2 3.5 %collective-permute-done.8.left_ref = f32[288,128]{1,0:T(8,128)S(1)} collective-permute-done((f32[288,128]{1,0:T(8,128)S(1)}, f32[288,128]{1,0:T(8,128)S(1)}, u32[]{:S(2)}, u32[]{:S(2)}) %collective-permute-start.8) | collective-permute-done | bytes 147488 | tf_op jit(solution)/shard_map/ppermute | solution.py:452
  44.7 0.0 collective-permute-done.9.right_ref
  44.7 4.1 %third_kernel.1.own_ref = f32[64,128]{1,0:T(8,128)S(1)} custom-call(f32[512,128]{1,0:T(8,128)S(1)} %get-tuple-element.30.own_ref, f32[288,128]{1,0:T(8,128)S(1)} %collective-permute-done.8.left_ref, f32[288,128]{1,0:T(8,128)S(1)} %collective-permute-done.9.right_ref, f32[320,128]{1,0:T(8,128)S(1)} %get-tuple-element.28.own_ref.older, ...), custom_call_target="tpu_custom_call" | custom-call | tf_op jit(solution)/shard_map/third_kernel/pallas_call | solution.py:440
  48.8 9.4 %collective-permute-start.12 = (f32[64,128]{1,0:T(8,128)S(1)}, f32[64,128]{1,0:T(8,128)S(1)}, u32[]{:S(2)}, u32[]{:S(2)}) collective-permute-start(f32[64,128]{1,0:T(8,128)S(1)} %third_kernel.1.own_ref), channel_id=1, source_target_pairs={{0,192},{64,0},{128,64},{192,128},{1,193},{65,1},{129,65},{193,129... | collective-permute-start | bytes 98312 | tf_op jit(solution)/shard_map/ppermute | solution.py:452
  58.3 0.0 collective-permute-start.11
  58.3 3.2 %collective-permute-start.10 = (f32[64,128]{1,0:T(8,128)S(1)}, f32[64,128]{1,0:T(8,128)S(1)}, u32[]{:S(2)}, u32[]{:S(2)}) collective-permute-start(f32[64,128]{1,0:T(8,128)S(1)} %third_kernel.1.own_ref), channel_id=1, source_target_pairs={{0,64},{64,128},{128,192},{192,0},{1,65},{65,129},{129,193},{193,1... | collective-permute-start | bytes 98312 | tf_op jit(solution)/shard_map/ppermute | solution.py:452
  61.5 0.0 collective-permute-done.12.three_ref
  61.5 1.0 %collective-permute-done.11.two_ref = f32[64,128]{1,0:T(8,128)S(1)} collective-permute-done((f32[64,128]{1,0:T(8,128)S(1)}, f32[64,128]{1,0:T(8,128)S(1)}, u32[]{:S(2)}, u32[]{:S(2)}) %collective-permute-start.11) | collective-permute-done | bytes 32800 | tf_op jit(solution)/shard_map/ppermute | solution.py:452
  62.5 0.0 collective-permute-done.10.one_ref
  62.5 0.7 %merge_kernel.1 = f32[32,2,128]{2,1,0:T(2,128)} custom-call(s32[1]{0:T(128)} %bitcast.group_ref, f32[64,128]{1,0:T(8,128)S(1)} %third_kernel.1.own_ref, f32[64,128]{1,0:T(8,128)S(1)} %collective-permute-done.10.one_ref, f32[64,128]{1,0:T(8,128)S(1)} %collective-permute-done.11.two_ref, f32[64,128]{1,0:T(8,128)S(1)} %collective-permute-done.12.three_ref), custom_call_target="tpu_custom_call" | custom-call | tf_op jit(solution)/shard_map/merge_kernel/pallas_call | solution.py:440
  (1 shorter events, 0.0 us)
Async XLA Ops:
  1.4 7.5 %collective-permute-start = (f32[320,128]{1,0:T(8,128)S(1)}, f32[320,128]{1,0:T(8,128)S(1)}, u32[]{:S(2)}, u32[]{:S(2)}) collective-permute-start(f32[320,128]{1,0:T(8,128)S(1)} %get-tuple-element.20), channel_id=1, source_target_pairs={{0,64},{64,128},{128,192},{192,0},{1,65},{65,129},{129,193},{193,1... | collective-permute-start | bytes 491528 | tf_op jit(solution)/shard_map/ppermute | solution.py:452
  5.6 9.2 %collective-permute-start.1 = (f32[320,128]{1,0:T(8,128)S(1)}, f32[320,128]{1,0:T(8,128)S(1)}, u32[]{:S(2)}, u32[]{:S(2)}) collective-permute-start(f32[320,128]{1,0:T(8,128)S(1)} %get-tuple-element.21), channel_id=1, source_target_pairs={{0,128},{64,192},{128,0},{192,64},{1,129},{65,193},{129,1},{193,65... | collective-permute-start | bytes 491528 | tf_op jit(solution)/shard_map/ppermute | solution.py:452
  7.5 8.0 %collective-permute-start.2 = (f32[320,128]{1,0:T(8,128)S(1)}, f32[320,128]{1,0:T(8,128)S(1)}, u32[]{:S(2)}, u32[]{:S(2)}) collective-permute-start(f32[320,128]{1,0:T(8,128)S(1)} %get-tuple-element.22), channel_id=1, source_target_pairs={{0,192},{64,0},{128,64},{192,128},{1,193},{65,1},{129,65},{193,129... | collective-permute-start | bytes 491528 | tf_op jit(solution)/shard_map/ppermute | solution.py:452
  15.6 0.7 %collective-permute-start.3 = (f32[144,128]{1,0:T(8,128)S(1)}, f32[144,128]{1,0:T(8,128)S(1)}, u32[]{:S(2)}, u32[]{:S(2)}) collective-permute-start(f32[144,128]{1,0:T(8,128)S(1)} %get-tuple-element.24), channel_id=1, source_target_pairs={{0,1},{1,2},{2,3},{3,0},{192,195},{193,192},{194,193},{195,194},{4... | collective-permute-start | bytes 221192 | tf_op jit(solution)/shard_map/ppermute | solution.py:460
  16.4 7.3 %collective-permute-start.4 = (f32[272,128]{1,0:T(8,128)S(1)}, f32[272,128]{1,0:T(8,128)S(1)}, u32[]{:S(2)}, u32[]{:S(2)}) collective-permute-start(f32[272,128]{1,0:T(8,128)S(1)} %get-tuple-element.26), channel_id=1, source_target_pairs={{0,4},{4,8},{8,12},{12,16},{16,20},{20,24},{24,28},{28,32},{32,36}... | collective-permute-start | bytes 417800 | tf_op jit(solution)/shard_map/ppermute | solution.py:452
  16.5 7.2 %collective-permute-start.5 = (f32[272,128]{1,0:T(8,128)S(1)}, f32[272,128]{1,0:T(8,128)S(1)}, u32[]{:S(2)}, u32[]{:S(2)}) collective-permute-start(f32[272,128]{1,0:T(8,128)S(1)} %get-tuple-element.27), channel_id=1, source_target_pairs={{0,60},{4,0},{8,4},{12,8},{16,12},{20,16},{24,20},{28,24},{32,28},... | collective-permute-start | bytes 417800 | tf_op jit(solution)/shard_map/ppermute | solution.py:452
  25.6 6.0 %collective-permute-start.7 = (f32[320,128]{1,0:T(8,128)S(1)}, f32[320,128]{1,0:T(8,128)S(1)}, u32[]{:S(2)}, u32[]{:S(2)}) collective-permute-start(f32[320,128]{1,0:T(8,128)S(1)} %get-tuple-element.28.own_ref.older), channel_id=1, source_target_pairs={{0,60},{4,0},{8,4},{12,8},{16,12},{20,16},{24,20},{28,24},{32,28},... | collective-permute-start | bytes 491528 | tf_op jit(solution)/shard_map/ppermute | solution.py:452
  29.3 6.3 %collective-permute-start.6 = (f32[320,128]{1,0:T(8,128)S(1)}, f32[320,128]{1,0:T(8,128)S(1)}, u32[]{:S(2)}, u32[]{:S(2)}) collective-permute-start(f32[320,128]{1,0:T(8,128)S(1)} %get-tuple-element.28.own_ref.older), channel_id=1, source_target_pairs={{0,4},{4,8},{8,12},{12,16},{16,20},{20,24},{24,28},{28,32},{32,36}... | collective-permute-start | bytes 491528 | tf_op jit(solution)/shard_map/ppermute | solution.py:452
  37.5 7.1 %collective-permute-start.8 = (f32[288,128]{1,0:T(8,128)S(1)}, f32[288,128]{1,0:T(8,128)S(1)}, u32[]{:S(2)}, u32[]{:S(2)}) collective-permute-start(f32[288,128]{1,0:T(8,128)S(1)} %get-tuple-element.31), channel_id=1, source_target_pairs={{0,4},{4,8},{8,12},{12,16},{16,20},{20,24},{24,28},{28,32},{32,36}... | collective-permute-start | bytes 442376 | tf_op jit(solution)/shard_map/ppermute | solution.py:452
  37.6 7.0 %collective-permute-start.9 = (f32[288,128]{1,0:T(8,128)S(1)}, f32[288,128]{1,0:T(8,128)S(1)}, u32[]{:S(2)}, u32[]{:S(2)}) collective-permute-start(f32[288,128]{1,0:T(8,128)S(1)} %get-tuple-element.32), channel_id=1, source_target_pairs={{0,60},{4,0},{8,4},{12,8},{16,12},{20,16},{24,20},{28,24},{32,28},... | collective-permute-start | bytes 442376 | tf_op jit(solution)/shard_map/ppermute | solution.py:452
  48.8 12.7 %collective-permute-start.12 = (f32[64,128]{1,0:T(8,128)S(1)}, f32[64,128]{1,0:T(8,128)S(1)}, u32[]{:S(2)}, u32[]{:S(2)}) collective-permute-start(f32[64,128]{1,0:T(8,128)S(1)} %third_kernel.1.own_ref), channel_id=1, source_target_pairs={{0,192},{64,0},{128,64},{192,128},{1,193},{65,1},{129,65},{193,129... | collective-permute-start | bytes 98312 | tf_op jit(solution)/shard_map/ppermute | solution.py:452
  58.3 4.3 %collective-permute-start.11 = (f32[64,128]{1,0:T(8,128)S(1)}, f32[64,128]{1,0:T(8,128)S(1)}, u32[]{:S(2)}, u32[]{:S(2)}) collective-permute-start(f32[64,128]{1,0:T(8,128)S(1)} %third_kernel.1.own_ref), channel_id=1, source_target_pairs={{0,128},{64,192},{128,0},{192,64},{1,129},{65,193},{129,1},{193,65... | collective-permute-start | bytes 98312 | tf_op jit(solution)/shard_map/ppermute | solution.py:452
  58.3 4.3 %collective-permute-start.10 = (f32[64,128]{1,0:T(8,128)S(1)}, f32[64,128]{1,0:T(8,128)S(1)}, u32[]{:S(2)}, u32[]{:S(2)}) collective-permute-start(f32[64,128]{1,0:T(8,128)S(1)} %third_kernel.1.own_ref), channel_id=1, source_target_pairs={{0,64},{64,128},{128,192},{192,0},{1,65},{65,129},{129,193},{193,1... | collective-permute-start | bytes 98312 | tf_op jit(solution)/shard_map/ppermute | solution.py:452

commit v2 on v1

--- a/solution.py
+++ b/solution.py
@@ -10,6 +10,7 @@
 FINE = 64
 FLOW = 32
 SLOT = 40
+LEVEL = 64
 SHRINK = 0.25
 WENO_EPS = 1e-06 * SHRINK * SHRINK
 STEP_FINE = 0.3
@@ -36,104 +37,139 @@
     return pl.multiple_of(index * 8, 8)
 
 
-def pack_kernel(group_ref, flow_ref, level_ref, band_ref, nozzle_ref, one_ref, two_ref, three_ref, keep_ref, ring):
-    group = group_ref[0]
-    slot = jnp.where(group == 3, 0, group * SLOT)
+def pack_kernel(flow_ref, level_ref, band_ref, nozzle_ref, raw_ref, mark_ref):
+    for row in range(2):
+        raw_ref[row * FLOW : (row + 1) * FLOW, :] = flow_ref[:, row, :]
     for row in range(4):
         block = level_ref[:, row, :] * SHRINK
-        ring[0, row * FINE : (row + 1) * FINE, :] = block[:, :LANES]
-        ring[1, row * FINE : (row + 1) * FINE, :] = block[:, LANES:]
+        raw_ref[LEVEL + row * FINE : LEVEL + (row + 1) * FINE, :] = block[:, :LANES]
+        raw_ref[LEVEL + (row + 4) * FINE : LEVEL + (row + 5) * FINE, :] = block[:, LANES:]
     spread_tiles = jnp.where(
         lax.broadcasted_iota(jnp.int32, (16, 256), 1) // 16 == lax.broadcasted_iota(jnp.int32, (16, 256), 0), 1.0, 0.0
     )
     flags = exact_dot(band_ref[...].astype(F32), spread_tiles)
     phases = nozzle_ref[...].astype(F32)
-
-    def quarter(first, second, target):
-        offset = jnp.where(target % 2 == 0, 96, 32)
-        plain = jnp.logical_or(target == 1, target == 2)
-        low = jnp.where(plain, first, second)
-        high = jnp.where(plain, second, first)
-        joined = jnp.where(lane_ids(first.shape[0]) >= offset, low, high)
-        return pltpu.roll(joined, LANES - offset, 1)
-
-    for step, out_ref in enumerate((keep_ref, one_ref, two_ref, three_ref)):
-        target = (group + step) % 4
-        turn = (slot + 4 - 32 * target + 2 * LANES) % LANES
-        for row in range(2):
-            out_ref[row * FLOW : (row + 1) * FLOW, :] = pltpu.roll(flow_ref[:, row, :], turn, 1)
-
-        for row in range(4):
-            at = row * FINE
-            out_ref[64 + at : 128 + at, :] = quarter(ring[0, at : at + FINE, :], ring[1, at : at + FINE, :], target)
-    keep_ref[320:328, :] = quarter(flags[:, :LANES], flags[:, LANES:], group)
-    keep_ref[328:332, :] = quarter(phases[:, :LANES], phases[:, LANES:], group)
-    keep_ref[332:336, :] = jnp.zeros((4, LANES), F32)
-
-
-def assemble_kernel(group_ref, keep_ref, one_ref, two_ref, three_ref, tile_ref, edge_ref):
+    for half in range(2):
+        part = slice(half * LANES, (half + 1) * LANES)
+        mark_ref[half, 0:8, :] = flags[:, part]
+        mark_ref[half, 8:12, :] = phases[:, part]
+        mark_ref[half, 12:16, :] = jnp.zeros((4, LANES), F32)
+
+
+def level_rows(ref, tile, row):
+    at = LEVEL + (4 * tile + row) * FINE
+    return ref[at : at + FINE, :]
+
+
+def split_kernel(group_ref, raw_ref, other_ref, mark_ref, half_ref, edge_ref):
+    group = group_ref[0]
+    lanes = lane_ids(FINE)
+    half_ref[0:64, :] = raw_ref[0:64, :]
+
+    for core in range(2):
+        level, (lower, upper) = (
+            (raw_ref, (other_ref, raw_ref)) if core else (other_ref, (raw_ref, other_ref))
+        )
+
+        @pl.when(group % 2 == core)
+        def _(core=core, level=level, lower=lower, upper=upper):
+            for row in range(2):
+                half_ref[64 + row * FINE : 64 + (row + 1) * FINE, :] = level_rows(level, 0, 2 * core + row)
+            beyond = level_rows(level, 1, 0)
+            for row in range(1, 4):
+                beyond = jnp.where(lanes < 16 * row, beyond, roll_lanes(level_rows(level, 1, row), 16 * row))
+            half_ref[192:256, :] = beyond
+
+            def edges(tile, level_start, field_start):
+                packed = roll_lanes(level_rows(level, tile, 0), -level_start)
+                for row in range(1, 4):
+                    turned = roll_lanes(level_rows(level, tile, row), 16 * row - level_start)
+                    packed = jnp.where(lanes < 16 * row, packed, turned)
+                packed = jnp.where(lanes < 64, packed, roll_lanes(lower[0:64, :], 64 - field_start))
+                packed = jnp.where(lanes < 72, packed, roll_lanes(upper[0:64, :], 72 - field_start))
+                edge_ref[0:64, :] = packed
+                edge_ref[64:80, :] = mark_ref[tile]
+
+            ahead = jnp.logical_or(group == 0, group == 3)
+
+            @pl.when(ahead)
+            def _():
+                edges(1, 112, 120)
+
+            @pl.when(jnp.logical_not(ahead))
+            def _():
+                edges(0, 0, 0)
+
+
+def join_kernel(half_ref, edge_ref, out_ref):
+    out_ref[0:256, :] = half_ref[...]
+    out_ref[256:336, :] = edge_ref[...]
+
+
+def assemble_kernel(
+    group_ref, raw_ref, other_ref, mark_ref, half_ref, far_half_ref, fixed_ref, up_ref, down_ref
+):
     group = group_ref[0]
     lanes = lane_ids(64)
-    parts = (keep_ref, one_ref, two_ref, three_ref)
-    owners = [(group - step + 4) % 4 for step in range(4)]
-    moving = jnp.zeros((64, LANES), F32)
-    for part, owner in zip(parts, owners):
-        inside = jnp.logical_and(lanes >= owner * SLOT, lanes < owner * SLOT + SLOT)
-        inside = jnp.logical_and(inside, owner < 3)
-        moving = jnp.where(inside, part[0:64, :], moving)
-    tile_ref[0:64, :] = moving
-    tile_ref[384:400, :] = keep_ref[320:336, :]
-    for part, owner in zip(parts, owners):
-
-        @pl.when(owner == 3)
-        def _(part=part):
-            tile_ref[64:128, :] = part[0:64, :]
-            tile_ref[128:384, :] = part[64:320, :]
-
-    pressure = tile_ref[64:128, :]
-    pushed = jnp.where(lanes >= 124, roll_lanes(pressure, 88), roll_lanes(pressure, 120))
-    edge_ref[0:64, :] = jnp.where(lanes >= 120, pushed, moving)
-    start = jnp.where(group == 0, 0, 96)
-    packed = jnp.zeros((FINE, LANES), F32)
-    for row in range(4):
-        turned = pltpu.roll(tile_ref[128 + row * FINE : 128 + (row + 1) * FINE, :], (32 * row - start + LANES) % LANES, 1)
-        packed = jnp.where(lanes // 32 == row, turned, packed)
-    edge_ref[64:128, :] = packed
-    edge_ref[128:144, :] = keep_ref[320:336, :]
-
-
-def edge_kernel(group_ref, tile_ref, edge_ref, fixed_ref, up_ref, down_ref):
-    group = group_ref[0]
-    lanes = lane_ids(64)
-    first, last = group == 0, group == 3
-    within = lanes % SLOT
-    slots = lanes < 3 * SLOT
-    low_edge = jnp.logical_and(jnp.logical_and(within < 4, slots), first)
-    high_edge = jnp.logical_and(jnp.logical_and(within >= 36, slots), last)
-    received = edge_ref[0:64, :]
-    moving = jnp.where(jnp.logical_or(low_edge, high_edge), received, tile_ref[0:64, :])
-    pressure = tile_ref[64:128, :]
-    pressure = jnp.where(jnp.logical_and(lanes < 4, first), roll_lanes(received, 8), pressure)
-    high_pressure = jnp.logical_and(jnp.logical_and(lanes >= 36, lanes < 40), last)
-    pressure = jnp.where(high_pressure, roll_lanes(received, 40), pressure)
-    fine_edge = jnp.logical_or(jnp.logical_and(lanes < 32, first), jnp.logical_and(lanes >= 96, last))
-    start = jnp.where(first, 0, 96)
-    fixed_ref[0:64, :] = moving
-    fixed_ref[64:128, :] = pressure
-    for row in range(4):
-        turned = pltpu.roll(edge_ref[64:128, :], (start - 32 * row + LANES) % LANES, 1)
-        level = jnp.where(fine_edge, turned, tile_ref[128 + row * FINE : 128 + (row + 1) * FINE, :])
-        fixed_ref[128 + row * FINE : 128 + (row + 1) * FINE, :] = level
-        if row < 3:
-            down_ref[row * FINE : (row + 1) * FINE, :] = level
-        if row > 0:
-            up_ref[(row - 1) * FINE : row * FINE, :] = level
-    marks = jnp.where(fine_edge[0:16, :], edge_ref[128:144, :], tile_ref[384:400, :])
-    fixed_ref[384:400, :] = marks
-    for out_ref, row in ((up_ref, 1), (down_ref, 0)):
-        out_ref[192:224, :] = moving[row * FLOW : (row + 1) * FLOW, :]
-        out_ref[224:256, :] = pressure[row * FLOW : (row + 1) * FLOW, :]
-        out_ref[256:272, :] = marks
+
+    def assemble(own):
+        core, first, last = own % 2, own == 0, own == 3
+        local = (raw_ref, other_ref) if core == 0 else (other_ref, raw_ref)
+        remote = (half_ref, far_half_ref) if core == 0 else (far_half_ref, half_ref)
+        fields = [ref[0:64, :] for ref in ((*local, *remote) if own < 2 else (*remote, *local))]
+        near, far = half_ref[256:320, :], far_half_ref[256:320, :]
+
+        def placed(index, lane):
+            value = roll_lanes(fields[index], lane + 4 - 32 * own)
+            edge = (near, near, far, far)[index]
+            source = 64 + 8 * (index % 2)
+            if first:
+                value = jnp.where(lanes < lane + 4, roll_lanes(edge, lane - source - 4), value)
+            if last:
+                value = jnp.where(lanes >= lane + 36, roll_lanes(edge, lane + 36 - source), value)
+            return value
+
+        parts = [placed(index, SLOT * index) for index in range(3)]
+        moving = by_slot(lanes, *parts)
+        pressure = placed(3, 0)
+        fixed_ref[0:64, :] = moving
+        fixed_ref[64:128, :] = pressure
+        for row in range(4):
+            if own < 2:
+                low = remote[row // 2][64 + (row % 2) * FINE : 64 + (row % 2 + 1) * FINE, :]
+                high = roll_lanes(far_half_ref[192:256, :] if core == 0 else half_ref[192:256, :], -16 * row)
+            else:
+                level = raw_ref if core else other_ref
+                low, high = level_rows(level, 0, row), level_rows(level, 1, row)
+            value = {
+                0: lambda: jnp.where(lanes < 32, roll_lanes(far, 16 - 16 * row), roll_lanes(low, 32)),
+                1: lambda: roll_lanes(jnp.where(lanes < 32, high, low), 96),
+                2: lambda: roll_lanes(jnp.where(lanes < 96, high, low), 32),
+                3: lambda: jnp.where(lanes < 96, roll_lanes(high, 96), roll_lanes(far, 96 - 16 * row)),
+            }[own]()
+            fixed_ref[128 + row * FINE : 128 + (row + 1) * FINE, :] = value
+            if row < 3:
+                down_ref[row * FINE : (row + 1) * FINE, :] = value
+            if row > 0:
+                up_ref[(row - 1) * FINE : row * FINE, :] = value
+        low, high, beside, few = mark_ref[0], mark_ref[1], half_ref[320:336, :], lane_ids(16)
+        marks = {
+            0: lambda: roll_lanes(jnp.where(few < 96, low, beside), 32),
+            1: lambda: roll_lanes(jnp.where(few < 32, high, low), 96),
+            2: lambda: roll_lanes(jnp.where(few < 96, high, low), 32),
+            3: lambda: roll_lanes(jnp.where(few < 32, beside, high), 96),
+        }[own]()
+        fixed_ref[384:400, :] = marks
+        for out_ref, row in ((up_ref, 1), (down_ref, 0)):
+            out_ref[192:224, :] = moving[row * FLOW : (row + 1) * FLOW, :]
+            out_ref[224:256, :] = pressure[row * FLOW : (row + 1) * FLOW, :]
+            out_ref[256:272, :] = marks
+
+    for own in range(4):
+
+        @pl.when(group == own)
+        def _(own=own):
+            assemble(own)
 
 
 def bent(below, here, above):
@@ -418,14 +454,18 @@
     out_ref[...] = done
 
 
-def merge_kernel(group_ref, own_ref, one_ref, two_ref, three_ref, out_ref):
+def sort_kernel(group_ref, own_ref, other_ref, keep_ref, send_ref):
     group = group_ref[0]
     lanes = lane_ids(64)
-    merged = jnp.zeros((64, LANES), F32)
-    for step, ref in enumerate((own_ref, one_ref, two_ref, three_ref)):
-        owner = (group - step + 4) % 4
-        turned = pltpu.roll(ref[...], (32 * owner - 32 * group + LANES) % LANES, 1)
-        merged = jnp.where(lanes // 32 == owner, turned, merged)
+    beside = group + 1 - 2 * (group % 2)
+    for target, out_ref in ((group, keep_ref), ((group + 2) % 4, send_ref)):
+        own = pltpu.roll(own_ref[...], (32 * group - 32 * target + LANES) % LANES, 1)
+        other = pltpu.roll(other_ref[...], (32 * beside - 32 * target + LANES) % LANES, 1)
+        out_ref[...] = jnp.where(lanes // 32 == group, own, other)
+
+
+def merge_kernel(group_ref, keep_ref, far_ref, out_ref):
+    merged = jnp.where(lane_ids(64) // 64 == group_ref[0] // 2, keep_ref[...], far_ref[...])
     for row in range(2):
         out_ref[:, row, :] = merged[row * FLOW : (row + 1) * FLOW, :]
 
@@ -452,34 +492,45 @@
     return lax.ppermute(value, axis, [(i, (i + shift) % count) for i in range(count)])
 
 
-def to_next_block(value):
-    groups, blocks = lax.axis_size("grp"), lax.axis_size("gy")
-    pairs = [(j, (j + 1) % blocks) for j in range(blocks)]
-    base = (groups - 1) * blocks
-    pairs += [(base + j, base + (j - 1) % blocks) for j in range(blocks)]
+def crossed(value, bit):
+    return lax.ppermute(value, "grp", [(i, i ^ bit) for i in range(lax.axis_size("grp"))])
+
+
+def to_next_blocks(value):
+    blocks = lax.axis_size("gy")
+    pairs = []
+    for source, target, step in ((0, 0, 1), (1, 3, -1), (2, 2, -1), (3, 1, 1)):
+        pairs += [(source * blocks + j, target * blocks + (j + step) % blocks) for j in range(blocks)]
     return lax.ppermute(value, ("grp", "gy"), pairs)
 
 
 def on_device(flow_fields, level_set, band_tiles, nozzle_phase):
     group = lax.axis_index("grp").astype(jnp.int32)[None]
-    message = (320, LANES)
-    to_one, to_two, to_three, keep = call(
+    raw, marks = call(
         pack_kernel,
-        [message, message, message, (336, LANES)],
-        [(2, 4 * FINE, LANES)],
-        group,
+        [(LEVEL + 8 * FINE, LANES), (2, 16, LANES)],
+        [],
         flow_fields[0],
         level_set[0],
         band_tiles[:, 0, :],
         nozzle_phase,
+        outer=True,
+    )
+    other = crossed(raw, 1)
+    half, edge = call(split_kernel, [(256, LANES), (80, LANES)], [], group, raw, other, marks, scalars=1)
+    half = call(join_kernel, [(336, LANES)], [], crossed(half, 2), to_next_blocks(edge))
+    far_half = crossed(half, 1)
+    fixed, up, down = call(
+        assemble_kernel,
+        [(400, LANES), (272, LANES), (272, LANES)],
+        [],
+        group,
+        raw,
+        other,
+        marks,
+        half,
+        far_half,
         scalars=1,
-        outer=True,
-    )
-    got = [shifted(value, "grp", step + 1) for step, value in enumerate((to_one, to_two, to_three))]
-    tile, edge = call(assemble_kernel, [(400, LANES), (144, LANES)], [], group, keep, *got, scalars=1)
-    edge = to_next_block(edge)
-    fixed, up, down = call(
-        edge_kernel, [(400, LANES), (272, LANES), (272, LANES)], [], group, tile, edge, scalars=1
     )
     old_left, old_right = shifted(up, "gx", 1), shifted(down, "gx", -1)
     own, speeds = call(
@@ -514,8 +565,10 @@
         old_right,
         speeds,
     )
-    got = [shifted(result, "grp", step + 1) for step in range(3)]
-    return call(merge_kernel, [(FLOW, 2, LANES)], [], group, result, *got, scalars=1, last=True)[None]
+    keep, send = call(
+        sort_kernel, [(64, LANES), (64, LANES)], [], group, result, crossed(result, 1), scalars=1
+    )
+    return call(merge_kernel, [(FLOW, 2, LANES)], [], group, keep, crossed(send, 2), scalars=1, last=True)[None]
 
 
 def solution(mesh):

time: 64.5 us -> 59.3 us (0.919); the launches traced: 63.3 us -> 59.2 us
  starting transfers between devices: 31.8 us -> 25 us
  waiting for transfers between devices: 21.1 us -> 23.8 us
    ppermute x12 -> x6, starting transfers between devices: 31.1 us -> 13.4 us  [shifted(): lax.ppermute(value, axis, [(i, (i + shift) % count) for i in range(count)])]
    ppermute x1 -> x6, starting transfers between devices: 0.67 us -> 11.6 us  [the longest x5 8.94 us: crossed(): lax.ppermute(value, 'grp', [(i, i ^ bit) for i in range(lax.axis_size('gr...]
    ppermute x1 -> x6, waiting for transfers between devices: 0.01 us -> 10.9 us  [the longest x5 6.69 us: crossed(): lax.ppermute(value, 'grp', [(i, i ^ bit) for i in range(lax.axis_size('gr...]
    ppermute x12 -> x6, waiting for transfers between devices: 21.1 us -> 12.9 us  [shifted(): lax.ppermute(value, axis, [(i, (i + shift) % count) for i in range(count)])]
    pallas_call x7 -> x9, Pallas kernels: 10.3 us -> 10.3 us  [call(): pl.pallas_call(kernel, out_shape=shapes if len(shapes) > 1 else shapes[0]...]
  transfers between devices with their start and end apart: 13 -> 12, of which waited for: 8 -> 9; matrix products, arithmetic and copies ran while one was open for 0% -> 0% of each run, Pallas kernels for 0% -> 0%
where the time goes in v2:
time: 59.3 us; the launch traced here: 59.2 us
  starting transfers between devices  25 us (42%)
  waiting for transfers between devices  23.8 us (40%)
  Pallas kernels  10.3 us (17%)
    ppermute x6, starting transfers between devices, shifted(): lax.ppermute(value, axis, [(i, (i + shift) % count) for i in range(count)])  13.4 us
    ppermute x6, waiting for transfers between devices, shifted(): lax.ppermute(value, axis, [(i, (i + shift) % count) for i in range(count)])  12.9 us
    pallas_call x9, Pallas kernels, call(): pl.pallas_call(kernel, out_shape=shapes if len(shapes) > 1 else shapes[0]...  10.3 us
    ppermute x5, starting transfers between devices, crossed(): lax.ppermute(value, 'grp', [(i, i ^ bit) for i in range(lax.axis_size('gr...  8.94 us
    ppermute x5, waiting for transfers between devices, crossed(): lax.ppermute(value, 'grp', [(i, i ^ bit) for i in range(lax.axis_size('gr...  6.69 us
    ppermute x1, waiting for transfers between devices, to_next_blocks(): return lax.ppermute(value, ('grp', 'gy'), pairs)  4.19 us
    ppermute x1, starting transfers between devices, to_next_blocks(): return lax.ppermute(value, ('grp', 'gy'), pairs)  2.69 us
  transfers between devices with their start and end apart: 12, of which 9 were waited for; matrix products, arithmetic and copies ran while one was open for 0% of the time, Pallas kernels for 0%

profile of v2, /device:TPU:1, one launch (start us, length us, event | category | flops | bytes accessed | tf_op | source)
XLA Modules:
  0.0 59.2 jit_solution(20288277334490832)
XLA Ops:
  0.0 1.3 %pack_kernel.1 = (f32[576,128]{1,0:T(8,128)S(1)}, f32[2,16,128]{2,1,0:T(8,128)S(1)}) custom-call(f32[32,2,128]{2,1,0:T(2,128)} %bitcast.6, f32[64,4,256]{2,1,0:T(4,128)} %bitcast.5, s32[8,16]{1,0:T(8,128)} %bitcast.7, s32[4,256]{1,0:T(4,128)} %nozzle_ref.1), custom_call_target="tpu_custom_call" | custom-call | tf_op jit(solution)/shard_map/pack_kernel/pallas_call | solution.py:480
  1.3 3.2 %collective-permute-start = (f32[576,128]{1,0:T(8,128)S(1)}, f32[576,128]{1,0:T(8,128)S(1)}, u32[]{:S(2)}, u32[]{:S(2)}) collective-permute-start(f32[576,128]{1,0:T(8,128)S(1)} %get-tuple-element.19.raw_ref), channel_id=1, source_target_pairs={{0,64},{64,0},{128,192},{192,128},{1,65},{65,1},{129,193},{193,129... | collective-permute-start | bytes 884744 | tf_op jit(solution)/shard_map/ppermute | solution.py:496
  4.5 1.2 %collective-permute-done.other_ref = f32[576,128]{1,0:T(8,128)S(1)} collective-permute-done((f32[576,128]{1,0:T(8,128)S(1)}, f32[576,128]{1,0:T(8,128)S(1)}, u32[]{:S(2)}, u32[]{:S(2)}) %collective-permute-start) | collective-permute-done | bytes 294944 | tf_op jit(solution)/shard_map/ppermute | solution.py:496
  5.7 0.2 split_kernel.1
  5.9 1.1 %collective-permute-start.1 = (f32[256,128]{1,0:T(8,128)S(1)}, f32[256,128]{1,0:T(8,128)S(1)}, u32[]{:S(2)}, u32[]{:S(2)}) collective-permute-start(f32[256,128]{1,0:T(8,128)S(1)} %get-tuple-element.21), channel_id=1, source_target_pairs={{0,128},{64,192},{128,0},{192,64},{1,129},{65,193},{129,1},{193,65... | collective-permute-start | bytes 393224 | tf_op jit(solution)/shard_map/ppermute | solution.py:496
  7.0 2.7 %collective-permute-start.2 = (f32[80,128]{1,0:T(8,128)S(1)}, f32[80,128]{1,0:T(8,128)S(1)}, u32[]{:S(2)}, u32[]{:S(2)}) collective-permute-start(f32[80,128]{1,0:T(8,128)S(1)} %get-tuple-element.22), channel_id=1, source_target_pairs={{0,1},{1,2},{2,3},{3,0},{64,195},{65,192},{66,193},{67,194},{128,1... | collective-permute-start | bytes 122888 | tf_op jit(solution)/shard_map/ppermute | solution.py:504
  9.7 4.2 %collective-permute-done.2.edge_ref = f32[80,128]{1,0:T(8,128)S(1)} collective-permute-done((f32[80,128]{1,0:T(8,128)S(1)}, f32[80,128]{1,0:T(8,128)S(1)}, u32[]{:S(2)}, u32[]{:S(2)}) %collective-permute-start.2) | collective-permute-done | bytes 40992 | tf_op jit(solution)/shard_map/ppermute | solution.py:504
  13.9 0.0 collective-permute-done.1.half_ref
  13.9 0.1 collective-permute-start.3
  14.0 1.4 %collective-permute-done.3.far_half_ref = f32[336,128]{1,0:T(8,128)S(1)} collective-permute-done((f32[336,128]{1,0:T(8,128)S(1)}, f32[336,128]{1,0:T(8,128)S(1)}, u32[]{:S(2)}, u32[]{:S(2)}) %collective-permute-start.3) | collective-permute-done | bytes 172064 | tf_op jit(solution)/shard_map/ppermute | solution.py:496
  15.4 0.2 assemble_kernel.1
  15.6 1.7 %collective-permute-start.4 = (f32[272,128]{1,0:T(8,128)S(1)}, f32[272,128]{1,0:T(8,128)S(1)}, u32[]{:S(2)}, u32[]{:S(2)}) collective-permute-start(f32[272,128]{1,0:T(8,128)S(1)} %get-tuple-element.24), channel_id=1, source_target_pairs={{0,4},{4,8},{8,12},{12,16},{16,20},{20,24},{24,28},{28,32},{32,36}... | collective-permute-start | bytes 417800 | tf_op jit(solution)/shard_map/ppermute | solution.py:492
  17.3 4.6 %collective-permute-start.5 = (f32[272,128]{1,0:T(8,128)S(1)}, f32[272,128]{1,0:T(8,128)S(1)}, u32[]{:S(2)}, u32[]{:S(2)}) collective-permute-start(f32[272,128]{1,0:T(8,128)S(1)} %get-tuple-element.25), channel_id=1, source_target_pairs={{0,60},{4,0},{8,4},{12,8},{16,12},{20,16},{24,20},{28,24},{32,28},... | collective-permute-start | bytes 417800 | tf_op jit(solution)/shard_map/ppermute | solution.py:492
  21.9 3.8 %collective-permute-done.4.left_ref.old_left = f32[272,128]{1,0:T(8,128)S(1)} collective-permute-done((f32[272,128]{1,0:T(8,128)S(1)}, f32[272,128]{1,0:T(8,128)S(1)}, u32[]{:S(2)}, u32[]{:S(2)}) %collective-permute-start.4) | collective-permute-done | bytes 139296 | tf_op jit(solution)/shard_map/ppermute | solution.py:492
  25.7 0.0 collective-permute-done.5.right_ref.old_right
  25.7 1.8 %first_kernel.1 = (f32[320,128]{1,0:T(8,128)S(1)}, f32[3,4,64,128]{3,2,1,0:T(8,128)S(1)}) custom-call(f32[400,128]{1,0:T(8,128)S(1)} %get-tuple-element.23.fixed_ref, f32[272,128]{1,0:T(8,128)S(1)} %collective-permute-done.4.left_ref.old_left, f32[272,128]{1,0:T(8,128)S(1)} %collective-permute-done.5.right_ref.old_right), custom_call_target="tpu_custom_call" | custom-call | tf_op jit(solution)/shard_map/first_kernel/pallas_call | solution.py:480
  27.5 3.5 %collective-permute-start.7 = (f32[320,128]{1,0:T(8,128)S(1)}, f32[320,128]{1,0:T(8,128)S(1)}, u32[]{:S(2)}, u32[]{:S(2)}) collective-permute-start(f32[320,128]{1,0:T(8,128)S(1)} %get-tuple-element.26.own_ref.older), channel_id=1, source_target_pairs={{0,60},{4,0},{8,4},{12,8},{16,12},{20,16},{24,20},{28,24},{32,28},... | collective-permute-start | bytes 491528 | tf_op jit(solution)/shard_map/ppermute | solution.py:492
  31.0 0.0 collective-permute-start.6
  31.0 2.5 %collective-permute-done.7.right_ref.older_right = f32[320,128]{1,0:T(8,128)S(1)} collective-permute-done((f32[320,128]{1,0:T(8,128)S(1)}, f32[320,128]{1,0:T(8,128)S(1)}, u32[]{:S(2)}, u32[]{:S(2)}) %collective-permute-start.7) | collective-permute-done | bytes 163872 | tf_op jit(solution)/shard_map/ppermute | solution.py:492
  33.5 4.0 %collective-permute-done.6.left_ref.older_left = f32[320,128]{1,0:T(8,128)S(1)} collective-permute-done((f32[320,128]{1,0:T(8,128)S(1)}, f32[320,128]{1,0:T(8,128)S(1)}, u32[]{:S(2)}, u32[]{:S(2)}) %collective-permute-start.6) | collective-permute-done | bytes 163872 | tf_op jit(solution)/shard_map/ppermute | solution.py:492
  37.5 1.9 %second_kernel.1 = (f32[512,128]{1,0:T(8,128)S(1)}, f32[288,128]{1,0:T(8,128)S(1)}, f32[288,128]{1,0:T(8,128)S(1)}) custom-call(f32[320,128]{1,0:T(8,128)S(1)} %get-tuple-element.26.own_ref.older, f32[320,128]{1,0:T(8,128)S(1)} %collective-permute-done.6.left_ref.older_left, f32[320,128]{1,0:T(8,128)S(1)} %collective-permute-done.7.right_ref.older_right, ...), custom_call_target="tpu_custom_call" | custom-call | tf_op jit(solution)/shard_map/second_kernel/pallas_call | solution.py:480
  39.5 0.1 collective-permute-start.8
  39.6 3.6 %collective-permute-start.9 = (f32[288,128]{1,0:T(8,128)S(1)}, f32[288,128]{1,0:T(8,128)S(1)}, u32[]{:S(2)}, u32[]{:S(2)}) collective-permute-start(f32[288,128]{1,0:T(8,128)S(1)} %get-tuple-element.30), channel_id=1, source_target_pairs={{0,60},{4,0},{8,4},{12,8},{16,12},{20,16},{24,20},{28,24},{32,28},... | collective-permute-start | bytes 442376 | tf_op jit(solution)/shard_map/ppermute | solution.py:492
  43.1 2.5 %collective-permute-done.8.left_ref = f32[288,128]{1,0:T(8,128)S(1)} collective-permute-done((f32[288,128]{1,0:T(8,128)S(1)}, f32[288,128]{1,0:T(8,128)S(1)}, u32[]{:S(2)}, u32[]{:S(2)}) %collective-permute-start.8) | collective-permute-done | bytes 147488 | tf_op jit(solution)/shard_map/ppermute | solution.py:492
  45.7 0.0 collective-permute-done.9.right_ref
  45.7 4.1 %third_kernel.1.own_ref = f32[64,128]{1,0:T(8,128)S(1)} custom-call(f32[512,128]{1,0:T(8,128)S(1)} %get-tuple-element.28.own_ref, f32[288,128]{1,0:T(8,128)S(1)} %collective-permute-done.8.left_ref, f32[288,128]{1,0:T(8,128)S(1)} %collective-permute-done.9.right_ref, f32[320,128]{1,0:T(8,128)S(1)} %get-tuple-element.26.own_ref.older, ...), custom_call_target="tpu_custom_call" | custom-call | tf_op jit(solution)/shard_map/third_kernel/pallas_call | solution.py:480
  49.8 3.4 %collective-permute-start.10 = (f32[64,128]{1,0:T(8,128)S(1)}, f32[64,128]{1,0:T(8,128)S(1)}, u32[]{:S(2)}, u32[]{:S(2)}) collective-permute-start(f32[64,128]{1,0:T(8,128)S(1)} %third_kernel.1.own_ref), channel_id=1, source_target_pairs={{0,64},{64,0},{128,192},{192,128},{1,65},{65,1},{129,193},{193,129... | collective-permute-start | bytes 98312 | tf_op jit(solution)/shard_map/ppermute | solution.py:496
  53.2 0.9 %collective-permute-done.10.other_ref = f32[64,128]{1,0:T(8,128)S(1)} collective-permute-done((f32[64,128]{1,0:T(8,128)S(1)}, f32[64,128]{1,0:T(8,128)S(1)}, u32[]{:S(2)}, u32[]{:S(2)}) %collective-permute-start.10) | collective-permute-done | bytes 32800 | tf_op jit(solution)/shard_map/ppermute | solution.py:496
  54.1 0.1 sort_kernel.1
  54.2 1.1 %collective-permute-start.11 = (f32[64,128]{1,0:T(8,128)S(1)}, f32[64,128]{1,0:T(8,128)S(1)}, u32[]{:S(2)}, u32[]{:S(2)}) collective-permute-start(f32[64,128]{1,0:T(8,128)S(1)} %get-tuple-element.32), channel_id=1, source_target_pairs={{0,128},{64,192},{128,0},{192,64},{1,129},{65,193},{129,1},{193,65... | collective-permute-start | bytes 98312 | tf_op jit(solution)/shard_map/ppermute | solution.py:496
  55.3 3.2 %collective-permute-done.11.far_ref = f32[64,128]{1,0:T(8,128)S(1)} collective-permute-done((f32[64,128]{1,0:T(8,128)S(1)}, f32[64,128]{1,0:T(8,128)S(1)}, u32[]{:S(2)}, u32[]{:S(2)}) %collective-permute-start.11) | collective-permute-done | bytes 32800 | tf_op jit(solution)/shard_map/ppermute | solution.py:496
  58.5 0.6 %merge_kernel.1 = f32[32,2,128]{2,1,0:T(2,128)} custom-call(s32[1]{0:T(128)} %bitcast.group_ref, f32[64,128]{1,0:T(8,128)S(1)} %get-tuple-element.31.keep_ref, f32[64,128]{1,0:T(8,128)S(1)} %collective-permute-done.11.far_ref), custom_call_target="tpu_custom_call" | custom-call | tf_op jit(solution)/shard_map/merge_kernel/pallas_call | solution.py:480
  (1 shorter events, 0.0 us)
Async XLA Ops:
  1.3 4.4 %collective-permute-start = (f32[576,128]{1,0:T(8,128)S(1)}, f32[576,128]{1,0:T(8,128)S(1)}, u32[]{:S(2)}, u32[]{:S(2)}) collective-permute-start(f32[576,128]{1,0:T(8,128)S(1)} %get-tuple-element.19.raw_ref), channel_id=1, source_target_pairs={{0,64},{64,0},{128,192},{192,128},{1,65},{65,1},{129,193},{193,129... | collective-permute-start | bytes 884744 | tf_op jit(solution)/shard_map/ppermute | solution.py:496
  5.9 8.0 %collective-permute-start.1 = (f32[256,128]{1,0:T(8,128)S(1)}, f32[256,128]{1,0:T(8,128)S(1)}, u32[]{:S(2)}, u32[]{:S(2)}) collective-permute-start(f32[256,128]{1,0:T(8,128)S(1)} %get-tuple-element.21), channel_id=1, source_target_pairs={{0,128},{64,192},{128,0},{192,64},{1,129},{65,193},{129,1},{193,65... | collective-permute-start | bytes 393224 | tf_op jit(solution)/shard_map/ppermute | solution.py:496
  7.0 6.9 %collective-permute-start.2 = (f32[80,128]{1,0:T(8,128)S(1)}, f32[80,128]{1,0:T(8,128)S(1)}, u32[]{:S(2)}, u32[]{:S(2)}) collective-permute-start(f32[80,128]{1,0:T(8,128)S(1)} %get-tuple-element.22), channel_id=1, source_target_pairs={{0,1},{1,2},{2,3},{3,0},{64,195},{65,192},{66,193},{67,194},{128,1... | collective-permute-start | bytes 122888 | tf_op jit(solution)/shard_map/ppermute | solution.py:504
  13.9 1.5 %collective-permute-start.3 = (f32[336,128]{1,0:T(8,128)S(1)}, f32[336,128]{1,0:T(8,128)S(1)}, u32[]{:S(2)}, u32[]{:S(2)}) collective-permute-start(f32[336,128]{1,0:T(8,128)S(1)} %join_kernel.1.half_ref), channel_id=1, source_target_pairs={{0,64},{64,0},{128,192},{192,128},{1,65},{65,1},{129,193},{193,129... | collective-permute-start | bytes 516104 | tf_op jit(solution)/shard_map/ppermute | solution.py:496
  15.6 10.1 %collective-permute-start.4 = (f32[272,128]{1,0:T(8,128)S(1)}, f32[272,128]{1,0:T(8,128)S(1)}, u32[]{:S(2)}, u32[]{:S(2)}) collective-permute-start(f32[272,128]{1,0:T(8,128)S(1)} %get-tuple-element.24), channel_id=1, source_target_pairs={{0,4},{4,8},{8,12},{12,16},{16,20},{20,24},{24,28},{28,32},{32,36}... | collective-permute-start | bytes 417800 | tf_op jit(solution)/shard_map/ppermute | solution.py:492
  17.3 8.4 %collective-permute-start.5 = (f32[272,128]{1,0:T(8,128)S(1)}, f32[272,128]{1,0:T(8,128)S(1)}, u32[]{:S(2)}, u32[]{:S(2)}) collective-permute-start(f32[272,128]{1,0:T(8,128)S(1)} %get-tuple-element.25), channel_id=1, source_target_pairs={{0,60},{4,0},{8,4},{12,8},{16,12},{20,16},{24,20},{28,24},{32,28},... | collective-permute-start | bytes 417800 | tf_op jit(solution)/shard_map/ppermute | solution.py:492
  27.5 6.0 %collective-permute-start.7 = (f32[320,128]{1,0:T(8,128)S(1)}, f32[320,128]{1,0:T(8,128)S(1)}, u32[]{:S(2)}, u32[]{:S(2)}) collective-permute-start(f32[320,128]{1,0:T(8,128)S(1)} %get-tuple-element.26.own_ref.older), channel_id=1, source_target_pairs={{0,60},{4,0},{8,4},{12,8},{16,12},{20,16},{24,20},{28,24},{32,28},... | collective-permute-start | bytes 491528 | tf_op jit(solution)/shard_map/ppermute | solution.py:492
  31.0 6.6 %collective-permute-start.6 = (f32[320,128]{1,0:T(8,128)S(1)}, f32[320,128]{1,0:T(8,128)S(1)}, u32[]{:S(2)}, u32[]{:S(2)}) collective-permute-start(f32[320,128]{1,0:T(8,128)S(1)} %get-tuple-element.26.own_ref.older), channel_id=1, source_target_pairs={{0,4},{4,8},{8,12},{12,16},{16,20},{20,24},{24,28},{28,32},{32,36}... | collective-permute-start | bytes 491528 | tf_op jit(solution)/shard_map/ppermute | solution.py:492
  39.5 6.2 %collective-permute-start.8 = (f32[288,128]{1,0:T(8,128)S(1)}, f32[288,128]{1,0:T(8,128)S(1)}, u32[]{:S(2)}, u32[]{:S(2)}) collective-permute-start(f32[288,128]{1,0:T(8,128)S(1)} %get-tuple-element.29), channel_id=1, source_target_pairs={{0,4},{4,8},{8,12},{12,16},{16,20},{20,24},{24,28},{28,32},{32,36}... | collective-permute-start | bytes 442376 | tf_op jit(solution)/shard_map/ppermute | solution.py:492
  39.6 6.1 %collective-permute-start.9 = (f32[288,128]{1,0:T(8,128)S(1)}, f32[288,128]{1,0:T(8,128)S(1)}, u32[]{:S(2)}, u32[]{:S(2)}) collective-permute-start(f32[288,128]{1,0:T(8,128)S(1)} %get-tuple-element.30), channel_id=1, source_target_pairs={{0,60},{4,0},{8,4},{12,8},{16,12},{20,16},{24,20},{28,24},{32,28},... | collective-permute-start | bytes 442376 | tf_op jit(solution)/shard_map/ppermute | solution.py:492
  49.8 4.3 %collective-permute-start.10 = (f32[64,128]{1,0:T(8,128)S(1)}, f32[64,128]{1,0:T(8,128)S(1)}, u32[]{:S(2)}, u32[]{:S(2)}) collective-permute-start(f32[64,128]{1,0:T(8,128)S(1)} %third_kernel.1.own_ref), channel_id=1, source_target_pairs={{0,64},{64,0},{128,192},{192,128},{1,65},{65,1},{129,193},{193,129... | collective-permute-start | bytes 98312 | tf_op jit(solution)/shard_map/ppermute | solution.py:496
  54.2 4.4 %collective-permute-start.11 = (f32[64,128]{1,0:T(8,128)S(1)}, f32[64,128]{1,0:T(8,128)S(1)}, u32[]{:S(2)}, u32[]{:S(2)}) collective-permute-start(f32[64,128]{1,0:T(8,128)S(1)} %get-tuple-element.32), channel_id=1, source_target_pairs={{0,128},{64,192},{128,0},{192,64},{1,129},{65,193},{129,1},{193,65... | collective-permute-start | bytes 98312 | tf_op jit(solution)/shard_map/ppermute | solution.py:496

commit v3 on v2

--- a/solution.py
+++ b/solution.py
@@ -176,6 +176,20 @@
     return (above - here) - (here - below)
 
 
+def mixed(smooth_one, smooth_two, smooth_three, curve_one, curve_two, curve_three):
+    both_three = smooth_one * smooth_two
+    both_two = smooth_one * smooth_three
+    both_one = smooth_two * smooth_three
+    one = both_one * both_one
+    three = both_three * both_three
+    bottom = (one + 6.0 * (both_two * both_two)) + 3.0 * three
+    top = one * ((curve_one - curve_two) * (1.0 / 3.0)) + three * ((curve_two - curve_three) * 0.5)
+    return top / bottom - curve_two * (1.0 / 6.0)
+
+
+THIRDS = 4.0 / 3.0
+
+
 def upwind_part(far_low, low, mid, high, far_high, slope, speed):
     ahead = speed >= 0.0
     one = jnp.where(ahead, far_low, far_high)
@@ -184,19 +198,33 @@
     curve_one = two - one
     curve_two = mid - two
     curve_three = four - mid
-    third = 4.0 / 3.0
-    smooth_one = (two * two + WENO_EPS) + curve_one * (third * curve_one + two)
-    smooth_two = (two * mid + WENO_EPS) + third * (curve_two * curve_two)
-    smooth_three = (mid * mid + WENO_EPS) + curve_three * (third * curve_three - mid)
-    both_three = smooth_one * smooth_two
-    both_two = smooth_one * smooth_three
-    both_one = smooth_two * smooth_three
-    weight_one = both_one * both_one
-    weight_two = 6.0 * (both_two * both_two)
-    weight_three = 3.0 * (both_three * both_three)
-    top = weight_one * (2.0 * curve_one - 3.0 * curve_two) - (weight_two * curve_two + weight_three * curve_three)
-    bottom = weight_one + weight_two + weight_three
-    return speed * slope + (jnp.abs(speed) * (1.0 / 6.0)) * (top / bottom)
+    smooth_one = (two * two + WENO_EPS) + curve_one * (THIRDS * curve_one + two)
+    smooth_two = (two * mid + WENO_EPS) + THIRDS * (curve_two * curve_two)
+    smooth_three = (mid * mid + WENO_EPS) + curve_three * (THIRDS * curve_three - mid)
+    rest = mixed(smooth_one, smooth_two, smooth_three, curve_one, curve_two, curve_three)
+    return speed * slope + jnp.abs(speed) * rest
+
+
+def pair_terms(low, high, low_square, high_square):
+    change = high - low
+    wide = THIRDS * change
+    rising = high_square + change * (wide + high)
+    falling = low_square + change * (wide - low)
+    level = (low * high + WENO_EPS) + change * wide
+    return change, rising, falling, level
+
+
+def upwind_pairs(one, two, three, four, slope, speed):
+    ahead = speed >= 0.0
+    rest = mixed(
+        jnp.where(ahead, one[1], four[2]),
+        jnp.where(ahead, two[3], three[3]),
+        jnp.where(ahead, three[2], two[1]),
+        jnp.where(ahead, one[0], four[0]),
+        jnp.where(ahead, two[0], three[0]),
+        jnp.where(ahead, three[0], two[0]),
+    )
+    return speed * (slope + rest)
 
 
 def fill_wrapped(wrapped, index, source, at):
@@ -205,49 +233,99 @@
     wrapped[index, 72:80, :] = source[at : at + 8, :]
 
 
-def section(rows, first_row, current, initial, speeds, wrapped, keep, blend, store):
-    for index in range(rows):
-        fill_wrapped(wrapped, index, *current[index + 3])
+def load(place, z):
+    ref, at = place
+    return ref[pl.ds(at + z, 8), :]
+
+
+def speed_loader(own_ref, rim_ref, first_row):
+    def speed(component, index, z):
+        row = (first_row + index) // 2
+        ref, at = (own_ref, row) if 0 <= row < 2 else (rim_ref, 0 if row < 0 else 1)
+        return ref[component, at, pl.ds(z, 8), :]
+
+    return speed
+
+
+def across(here, wrapped, index, z, speed_y, speed_z):
+    after = roll_lanes(here, -1)
+    before = roll_lanes(here, 1)
+    mid = bent(before, here, after)
+    shifts = [roll_lanes(mid, 2), roll_lanes(mid, 1), mid, roll_lanes(mid, -1), roll_lanes(mid, -2)]
+    rate = upwind_part(*shifts, (after - before) * 0.5, speed_y)
+    column = [wrapped[index, pl.ds(z + 8 + offset, 8), :] for offset in range(-3, 4)]
+    column[3] = here
+    column_bends = [bent(column[k - 1], column[k], column[k + 1]) for k in range(1, 6)]
+    return rate + upwind_part(*column_bends, (column[4] - column[2]) * 0.5, speed_z)
+
+
+def across_rows(places, speed, wrapped, rate_ref):
+    for index, place in enumerate(places):
+        fill_wrapped(wrapped, index, *place)
 
     def body(step, carry):
         z = chunk(step)
-
-        def load(place):
-            ref, at = place
-            return ref[pl.ds(at + z, 8), :]
-
-        values = [load(place) for place in current]
-        bends = [bent(values[k - 1], values[k], values[k + 1]) for k in range(1, rows + 5)]
+        for index, place in enumerate(places):
+            rate = across(load(place, z), wrapped, index, z, speed(1, index, z), speed(2, index, z))
+            rate_ref[pl.ds(index * FINE + z, 8), :] = rate
+        return carry
+
+    lax.fori_loop(0, 8, body, 0)
+
+
+def section(current, initial, speed, rates, wrapped, keep, blend, store):
+    rows = len(rates)
+    for index in range(rows):
+        if rates[index] is None:
+            fill_wrapped(wrapped, index, *current[index + 3])
+
+    def body(step, carry):
+        z = chunk(step)
+        values = [load(place, z) for place in current]
+        steps = [values[k + 1] - values[k] for k in range(rows + 5)]
+        bends = [steps[k + 1] - steps[k] for k in range(rows + 4)]
+        squares = [value * value + WENO_EPS for value in bends]
+        pairs = {}
         for index in range(rows):
+            for k in range(index, index + 4):
+                if k not in pairs:
+                    pairs[k] = pair_terms(bends[k], bends[k + 1], squares[k], squares[k + 1])
             here = values[index + 3]
-            speed_row = (first_row + index + 2) // 2
-            speed_x = speeds[0, speed_row, pl.ds(z, 8), :]
-            speed_y = speeds[1, speed_row, pl.ds(z, 8), :]
-            speed_z = speeds[2, speed_row, pl.ds(z, 8), :]
-            rate = upwind_part(*bends[index : index + 5], (values[index + 4] - values[index + 2]) * 0.5, speed_x)
-            after = roll_lanes(here, -1)
-            before = roll_lanes(here, 1)
-            mid = bent(before, here, after)
-            rate = rate + upwind_part(
-                roll_lanes(mid, 2),
-                roll_lanes(mid, 1),
-                mid,
-                roll_lanes(mid, -1),
-                roll_lanes(mid, -2),
-                (after - before) * 0.5,
-                speed_y,
-            )
-            column = [wrapped[index, pl.ds(z + 8 + offset, 8), :] for offset in range(-3, 4)]
-            column[3] = here
-            column_bends = [bent(column[k - 1], column[k], column[k + 1]) for k in range(1, 6)]
-            rate = rate + upwind_part(*column_bends, (column[4] - column[2]) * 0.5, speed_z)
+            slope = (steps[index + 3] + steps[index + 2]) * 0.5
+            rate = upwind_pairs(*(pairs[k] for k in range(index, index + 4)), slope, speed(0, index, z))
+            if rates[index] is None:
+                rate = rate + across(here, wrapped, index, z, speed(1, index, z), speed(2, index, z))
+            else:
+                rate = rate + load(rates[index], z)
             moved = blend * (here - STEP_FINE * rate)
             if keep:
-                moved = moved + keep * load(initial[index])
+                moved = moved + keep * load(initial[index], z)
             store(index, z, moved)
         return carry
 
     lax.fori_loop(0, 8, body, 0)
+
+
+def spread_speeds(stacked, speed_ref):
+    source_lane = lax.broadcasted_iota(jnp.int32, (LANES, LANES), 0)
+    fine_lane = lax.broadcasted_iota(jnp.int32, (LANES, LANES), 1)
+    covered = jnp.logical_and(fine_lane >= 24, fine_lane < 104)
+    for component in range(3):
+        pick = jnp.logical_and(source_lane == SLOT * component + fine_lane // 2 - 12, covered)
+        spread = exact_dot(stacked, jnp.where(pick, 1.0, 0.0))
+        for row in range(2):
+            part = spread[row * FLOW : (row + 1) * FLOW, :]
+            speed_ref[component, row, pl.ds(0, FLOW, stride=2), :] = part
+            speed_ref[component, row, pl.ds(1, FLOW, stride=2), :] = part
+
+
+def in_pairs(work):
+    def body(step, carry):
+        for part in range(2):
+            work(pl.multiple_of(step * 16 + part * 8, 8))
+        return carry
+
+    lax.fori_loop(0, 4, body, 0)
 
 
 def centred(below, above):
@@ -268,25 +346,19 @@
     return (source + IMPLICIT * beside) / (1.0 + 6.0 * IMPLICIT)
 
 
-def first_kernel(fixed_ref, left_ref, right_ref, out_ref, speed_ref, wrapped):
+def inner_kernel(fixed_ref, speed_ref, rate_ref, wrapped):
+    spread_speeds(fixed_ref[0:64, :], speed_ref)
+    places = [(fixed_ref, 128 + FINE * row) for row in range(4)]
+    across_rows(places, speed_loader(speed_ref, None, 0), wrapped, rate_ref)
+
+
+def first_kernel(fixed_ref, left_ref, right_ref, speed_ref, rate_ref, out_ref):
     moving = [
         left_ref[192:224, :],
         fixed_ref[0:32, :],
         fixed_ref[32:64, :],
         right_ref[192:224, :],
     ]
-    stacked = jnp.concatenate(moving, axis=0)
-    source_lane = lax.broadcasted_iota(jnp.int32, (LANES, LANES), 0)
-    fine_lane = lax.broadcasted_iota(jnp.int32, (LANES, LANES), 1)
-    covered = jnp.logical_and(fine_lane >= 24, fine_lane < 104)
-    for component in range(3):
-        pick = jnp.logical_and(source_lane == SLOT * component + fine_lane // 2 - 12, covered)
-        spread = exact_dot(stacked, jnp.where(pick, 1.0, 0.0))
-        for row in range(4):
-            part = spread[row * FLOW : (row + 1) * FLOW, :]
-            speed_ref[component, row, pl.ds(0, FLOW, stride=2), :] = part
-            speed_ref[component, row, pl.ds(1, FLOW, stride=2), :] = part
-
     lanes = lane_ids(FLOW)
     pressure = [
         left_ref[224:256, :],
@@ -325,10 +397,20 @@
     def store(index, z, value):
         out_ref[pl.ds(index * FINE + z, 8), :] = value
 
-    section(4, 0, places, None, speed_ref, wrapped, 0.0, 1.0, store)
-
-
-def second_kernel(own_ref, left_ref, right_ref, fixed_ref, old_left, old_right, speed_ref, out_ref, up_ref, down_ref, wrapped):
+    rates = [(rate_ref, FINE * row) for row in range(4)]
+    section(places, None, speed_loader(speed_ref, None, 0), rates, None, 0.0, 1.0, store)
+
+
+def middle_kernel(own_ref, old_left, old_right, speed_ref, rim_ref, rate_ref, wrapped):
+    spread_speeds(jnp.concatenate([old_left[192:224, :], old_right[192:224, :]], axis=0), rim_ref)
+    places = [(own_ref, FINE * row) for row in range(4)]
+    across_rows(places, speed_loader(speed_ref, None, 0), wrapped, rate_ref)
+
+
+def second_kernel(
+    own_ref, left_ref, right_ref, fixed_ref, old_left, old_right, speed_ref, rim_ref, rate_ref,
+    out_ref, up_ref, down_ref, wrapped,
+):
     source = [ref[256 + row * FLOW : 256 + (row + 1) * FLOW, :] for ref in (left_ref, own_ref, right_ref) for row in range(2)]
     for row in range(4):
         done = sweep(source[row], source[row + 1], source[row + 2], source[row + 1])
@@ -347,11 +429,18 @@
         if index > 1:
             down_ref[pl.ds((index - 2) * FINE + z, 8), :] = value
 
-    section(6, -1, places, initial, speed_ref, wrapped, 0.75, 0.25, store)
+    rates = [None] + [(rate_ref, FINE * row) for row in range(4)] + [None]
+    section(places, initial, speed_loader(speed_ref, rim_ref, -1), rates, wrapped, 0.75, 0.25, store)
+
+
+def late_kernel(own_ref, speed_ref, rim_ref, rate_ref, wrapped):
+    places = [(own_ref, FINE * row) for row in range(6)]
+    across_rows(places, speed_loader(speed_ref, rim_ref, -1), wrapped, rate_ref)
 
 
 def third_kernel(
-    own_ref, left_ref, right_ref, older, older_left, older_right, fixed_ref, old_left, old_right, speed_ref,
+    own_ref, left_ref, right_ref, older, older_left, older_right, fixed_ref, old_left, old_right,
+    speed_ref, rim_ref, rate_ref,
     out_ref, wrapped, shaped, normal_x, normal_z, summed,
 ):
     places = (
@@ -377,13 +466,13 @@
         value = jnp.where(jnp.logical_and(bottom, phase == 1.0), -SPREAD, value)
         shaped[index, pl.ds(8 + z, 8), :] = value
 
-    section(8, -2, places, initial, speed_ref, wrapped, 1.0 / 3.0, 2.0 / 3.0, store)
+    rates = [None] + [(rate_ref, FINE * row) for row in range(6)] + [None]
+    section(places, initial, speed_loader(speed_ref, rim_ref, -2), rates, wrapped, 1.0 / 3.0, 2.0 / 3.0, store)
     for index in range(8):
         shaped[index, 0:8, :] = shaped[index, 64:72, :]
         shaped[index, 72:80, :] = shaped[index, 8:16, :]
 
-    def normals(step, carry):
-        z = chunk(step)
+    def normals(z):
         middle = [shaped[k, pl.ds(8 + z, 8), :] for k in range(8)]
         for row in range(6):
             here = middle[row + 1]
@@ -395,15 +484,13 @@
             if 0 < row < 5:
                 wrapped[row, pl.ds(z, 8), :] = slope_y * inverse
                 normal_z[row - 1, pl.ds(8 + z, 8), :] = slope_z * inverse
-        return carry
-
-    lax.fori_loop(0, 8, normals, 0)
+
+    in_pairs(normals)
     for row in range(4):
         normal_z[row, 0:8, :] = normal_z[row, 64:72, :]
         normal_z[row, 72:80, :] = normal_z[row, 8:16, :]
 
-    def forces(step, carry):
-        z = chunk(step)
+    def forces(z):
         for half in range(2):
             total = None
             for row in (2 * half, 2 * half + 1):
@@ -423,9 +510,8 @@
                 total = terms if total is None else tuple(a + b for a, b in zip(total, terms))
             for component in range(4):
                 summed[component, pl.ds(half * FINE + z, 8), :] = total[component]
-        return carry
-
-    lax.fori_loop(0, 8, forces, 0)
+
+    in_pairs(forces)
 
     source = [older_left[288:320, :], older[256:288, :], older[288:320, :], older_right[256:288, :]]
     once = [left_ref[256:288, :]] + [own_ref[384 + row * FLOW : 384 + (row + 1) * FLOW, :] for row in range(4)]
@@ -532,11 +618,14 @@
         far_half,
         scalars=1,
     )
+    speed_shape = (3, 2, FINE, LANES)
     old_left, old_right = shifted(up, "gx", 1), shifted(down, "gx", -1)
-    own, speeds = call(
-        first_kernel, [(320, LANES), (3, 4, FINE, LANES)], [(4, 80, LANES)], fixed, old_left, old_right
-    )
+    speeds, rates = call(inner_kernel, [speed_shape, (256, LANES)], [(4, 80, LANES)], fixed)
+    own = call(first_kernel, [(320, LANES)], [], fixed, old_left, old_right, speeds, rates)
     left, right = shifted(own, "gx", 1), shifted(own, "gx", -1)
+    rim, rates = call(
+        middle_kernel, [speed_shape, (256, LANES)], [(4, 80, LANES)], own, old_left, old_right, speeds
+    )
     newer, up, down = call(
         second_kernel,
         [(512, LANES), (288, LANES), (288, LANES)],
@@ -548,8 +637,11 @@
         old_left,
         old_right,
         speeds,
+        rim,
+        rates,
     )
     newer_left, newer_right = shifted(up, "gx", 1), shifted(down, "gx", -1)
+    rates = call(late_kernel, [(384, LANES)], [(6, 80, LANES)], newer, speeds, rim)
     result = call(
         third_kernel,
         [(64, LANES)],
@@ -564,6 +656,8 @@
         old_left,
         old_right,
         speeds,
+        rim,
+        rates,
     )
     keep, send = call(
         sort_kernel, [(64, LANES), (64, LANES)], [], group, result, crossed(result, 1), scalars=1

time: 59.3 us -> 56 us (0.944)
  waiting for transfers between devices: 23.8 us -> 18.4 us
  Pallas kernels: 10.3 us -> 12.1 us
    ppermute x6, waiting for transfers between devices: 12.9 us -> 7.49 us  [shifted(): lax.ppermute(value, axis, [(i, (i + shift) % count) for i in range(count)])]
    pallas_call x9 -> x12, Pallas kernels: 10.3 us -> 12.1 us  [call(): pl.pallas_call(kernel, out_shape=shapes if len(shapes) > 1 else shapes[0]...]
  transfers between devices with their start and end apart: 12 -> 12, of which waited for: 9 -> 9; matrix products, arithmetic and copies ran while one was open for 0% -> 0% of each run, Pallas kernels for 0% -> 9%
where the time goes in v3:
time: 56 us; the launch traced here: 55.9 us
  starting transfers between devices  25.3 us (45%)
  waiting for transfers between devices  18.4 us (33%)
  Pallas kernels  12.1 us (22%)
    ppermute x6, starting transfers between devices, shifted(): lax.ppermute(value, axis, [(i, (i + shift) % count) for i in range(count)])  13.4 us
    pallas_call x12, Pallas kernels, call(): pl.pallas_call(kernel, out_shape=shapes if len(shapes) > 1 else shapes[0]...  12.1 us
    ppermute x5, starting transfers between devices, crossed(): lax.ppermute(value, 'grp', [(i, i ^ bit) for i in range(lax.axis_size('gr...  9.26 us
    ppermute x6, waiting for transfers between devices, shifted(): lax.ppermute(value, axis, [(i, (i + shift) % count) for i in range(count)])  7.49 us
    ppermute x5, waiting for transfers between devices, crossed(): lax.ppermute(value, 'grp', [(i, i ^ bit) for i in range(lax.axis_size('gr...  6.68 us
    ppermute x1, waiting for transfers between devices, to_next_blocks(): return lax.ppermute(value, ('grp', 'gy'), pairs)  4.19 us
    ppermute x1, starting transfers between devices, to_next_blocks(): return lax.ppermute(value, ('grp', 'gy'), pairs)  2.69 us
  transfers between devices with their start and end apart: 12, of which 9 were waited for; matrix products, arithmetic and copies ran while one was open for 0% of the time, Pallas kernels for 9%

profile of v3, /device:TPU:1, one launch (start us, length us, event | category | flops | bytes accessed | tf_op | source)
XLA Modules:
  0.0 55.9 jit_solution(3189679179471454095)
XLA Ops:
  0.0 1.3 %pack_kernel.1 = (f32[576,128]{1,0:T(8,128)S(1)}, f32[2,16,128]{2,1,0:T(8,128)S(1)}) custom-call(f32[32,2,128]{2,1,0:T(2,128)} %bitcast.6, f32[64,4,256]{2,1,0:T(4,128)} %bitcast.5, s32[8,16]{1,0:T(8,128)} %bitcast.7, s32[4,256]{1,0:T(4,128)} %nozzle_ref.1), custom_call_target="tpu_custom_call" | custom-call | tf_op jit(solution)/shard_map/pack_kernel/pallas_call | solution.py:566
  1.3 3.2 %collective-permute-start = (f32[576,128]{1,0:T(8,128)S(1)}, f32[576,128]{1,0:T(8,128)S(1)}, u32[]{:S(2)}, u32[]{:S(2)}) collective-permute-start(f32[576,128]{1,0:T(8,128)S(1)} %get-tuple-element.21.raw_ref), channel_id=1, source_target_pairs={{0,64},{64,0},{128,192},{192,128},{1,65},{65,1},{129,193},{193,129... | collective-permute-start | bytes 884744 | tf_op jit(solution)/shard_map/ppermute | solution.py:582
  4.5 1.2 %collective-permute-done.other_ref = f32[576,128]{1,0:T(8,128)S(1)} collective-permute-done((f32[576,128]{1,0:T(8,128)S(1)}, f32[576,128]{1,0:T(8,128)S(1)}, u32[]{:S(2)}, u32[]{:S(2)}) %collective-permute-start) | collective-permute-done | bytes 294944 | tf_op jit(solution)/shard_map/ppermute | solution.py:582
  5.7 0.2 split_kernel.1
  5.9 1.1 %collective-permute-start.1 = (f32[256,128]{1,0:T(8,128)S(1)}, f32[256,128]{1,0:T(8,128)S(1)}, u32[]{:S(2)}, u32[]{:S(2)}) collective-permute-start(f32[256,128]{1,0:T(8,128)S(1)} %get-tuple-element.23), channel_id=1, source_target_pairs={{0,128},{64,192},{128,0},{192,64},{1,129},{65,193},{129,1},{193,65... | collective-permute-start | bytes 393224 | tf_op jit(solution)/shard_map/ppermute | solution.py:582
  7.0 2.7 %collective-permute-start.2 = (f32[80,128]{1,0:T(8,128)S(1)}, f32[80,128]{1,0:T(8,128)S(1)}, u32[]{:S(2)}, u32[]{:S(2)}) collective-permute-start(f32[80,128]{1,0:T(8,128)S(1)} %get-tuple-element.24), channel_id=1, source_target_pairs={{0,1},{1,2},{2,3},{3,0},{64,195},{65,192},{66,193},{67,194},{128,1... | collective-permute-start | bytes 122888 | tf_op jit(solution)/shard_map/ppermute | solution.py:590
  9.7 4.2 %collective-permute-done.2.edge_ref = f32[80,128]{1,0:T(8,128)S(1)} collective-permute-done((f32[80,128]{1,0:T(8,128)S(1)}, f32[80,128]{1,0:T(8,128)S(1)}, u32[]{:S(2)}, u32[]{:S(2)}) %collective-permute-start.2) | collective-permute-done | bytes 40992 | tf_op jit(solution)/shard_map/ppermute | solution.py:590
  13.9 0.0 collective-permute-done.1.half_ref
  13.9 0.1 collective-permute-start.3
  14.0 1.4 %collective-permute-done.3.far_half_ref = f32[336,128]{1,0:T(8,128)S(1)} collective-permute-done((f32[336,128]{1,0:T(8,128)S(1)}, f32[336,128]{1,0:T(8,128)S(1)}, u32[]{:S(2)}, u32[]{:S(2)}) %collective-permute-start.3) | collective-permute-done | bytes 172064 | tf_op jit(solution)/shard_map/ppermute | solution.py:582
  15.4 0.2 assemble_kernel.1
  15.6 1.7 %collective-permute-start.4 = (f32[272,128]{1,0:T(8,128)S(1)}, f32[272,128]{1,0:T(8,128)S(1)}, u32[]{:S(2)}, u32[]{:S(2)}) collective-permute-start(f32[272,128]{1,0:T(8,128)S(1)} %get-tuple-element.26), channel_id=1, source_target_pairs={{0,4},{4,8},{8,12},{12,16},{16,20},{20,24},{24,28},{28,32},{32,36}... | collective-permute-start | bytes 417800 | tf_op jit(solution)/shard_map/ppermute | solution.py:578
  17.3 4.6 %collective-permute-start.5 = (f32[272,128]{1,0:T(8,128)S(1)}, f32[272,128]{1,0:T(8,128)S(1)}, u32[]{:S(2)}, u32[]{:S(2)}) collective-permute-start(f32[272,128]{1,0:T(8,128)S(1)} %get-tuple-element.27), channel_id=1, source_target_pairs={{0,60},{4,0},{8,4},{12,8},{16,12},{20,16},{24,20},{28,24},{32,28},... | collective-permute-start | bytes 417800 | tf_op jit(solution)/shard_map/ppermute | solution.py:578
  21.9 1.8 %inner_kernel.1 = (f32[3,2,64,128]{3,2,1,0:T(8,128)S(1)}, f32[256,128]{1,0:T(8,128)S(1)}) custom-call(f32[400,128]{1,0:T(8,128)S(1)} %get-tuple-element.25.fixed_ref), custom_call_target="tpu_custom_call" | custom-call | tf_op jit(solution)/shard_map/inner_kernel/pallas_call | solution.py:566
  23.7 2.0 %collective-permute-done.4.left_ref.old_left = f32[272,128]{1,0:T(8,128)S(1)} collective-permute-done((f32[272,128]{1,0:T(8,128)S(1)}, f32[272,128]{1,0:T(8,128)S(1)}, u32[]{:S(2)}, u32[]{:S(2)}) %collective-permute-start.4) | collective-permute-done | bytes 139296 | tf_op jit(solution)/shard_map/ppermute | solution.py:578
  25.7 0.5 first_kernel.1.own_ref.older
  26.2 3.5 %collective-permute-start.7 = (f32[320,128]{1,0:T(8,128)S(1)}, f32[320,128]{1,0:T(8,128)S(1)}, u32[]{:S(2)}, u32[]{:S(2)}) collective-permute-start(f32[320,128]{1,0:T(8,128)S(1)} %first_kernel.1.own_ref.older), channel_id=1, source_target_pairs={{0,60},{4,0},{8,4},{12,8},{16,12},{20,16},{24,20},{28,24},{32,28},... | collective-permute-start | bytes 491528 | tf_op jit(solution)/shard_map/ppermute | solution.py:578
  29.7 1.8 %middle_kernel.1 = (f32[3,2,64,128]{3,2,1,0:T(8,128)S(1)}, f32[256,128]{1,0:T(8,128)S(1)}) custom-call(f32[320,128]{1,0:T(8,128)S(1)} %first_kernel.1.own_ref.older, f32[272,128]{1,0:T(8,128)S(1)} %collective-permute-done.4.left_ref.old_left, f32[272,128]{1,0:T(8,128)S(1)} %collective-permute-done.5.right_ref.old_right, ...), custom_call_target="tpu_custom_call" | custom-call | tf_op jit(solution)/shard_map/middle_kernel/pallas_call | solution.py:566
  31.4 0.8 %collective-permute-done.7.right_ref.older_right = f32[320,128]{1,0:T(8,128)S(1)} collective-permute-done((f32[320,128]{1,0:T(8,128)S(1)}, f32[320,128]{1,0:T(8,128)S(1)}, u32[]{:S(2)}, u32[]{:S(2)}) %collective-permute-start.7) | collective-permute-done | bytes 163872 | tf_op jit(solution)/shard_map/ppermute | solution.py:578
  32.2 3.7 %collective-permute-done.6.left_ref.older_left = f32[320,128]{1,0:T(8,128)S(1)} collective-permute-done((f32[320,128]{1,0:T(8,128)S(1)}, f32[320,128]{1,0:T(8,128)S(1)}, u32[]{:S(2)}, u32[]{:S(2)}) %collective-permute-start.6) | collective-permute-done | bytes 163872 | tf_op jit(solution)/shard_map/ppermute | solution.py:578
  36.0 1.5 %second_kernel.1 = (f32[512,128]{1,0:T(8,128)S(1)}, f32[288,128]{1,0:T(8,128)S(1)}, f32[288,128]{1,0:T(8,128)S(1)}) custom-call(f32[320,128]{1,0:T(8,128)S(1)} %first_kernel.1.own_ref.older, f32[320,128]{1,0:T(8,128)S(1)} %collective-permute-done.6.left_ref.older_left, f32[320,128]{1,0:T(8,128)S(1)} %collective-permute-done.7.right_ref.older_right, ...), custom_call_target="tpu_custom_call" | custom-call | tf_op jit(solution)/shard_map/second_kernel/pallas_call | solution.py:566
  37.5 0.1 collective-permute-start.8
  37.6 3.6 %collective-permute-start.9 = (f32[288,128]{1,0:T(8,128)S(1)}, f32[288,128]{1,0:T(8,128)S(1)}, u32[]{:S(2)}, u32[]{:S(2)}) collective-permute-start(f32[288,128]{1,0:T(8,128)S(1)} %get-tuple-element.34), channel_id=1, source_target_pairs={{0,60},{4,0},{8,4},{12,8},{16,12},{20,16},{24,20},{28,24},{32,28},... | collective-permute-start | bytes 442376 | tf_op jit(solution)/shard_map/ppermute | solution.py:578
  41.1 1.6 %late_kernel.1.rate_ref = f32[384,128]{1,0:T(8,128)S(1)} custom-call(f32[512,128]{1,0:T(8,128)S(1)} %get-tuple-element.32.own_ref, f32[3,2,64,128]{3,2,1,0:T(8,128)S(1)} %get-tuple-element.28.speed_ref, f32[3,2,64,128]{3,2,1,0:T(8,128)S(1)} %get-tuple-element.30.rim_ref), custom_call_target="tpu_custom_call" | custom-call | tf_op jit(solution)/shard_map/late_kernel/pallas_call | solution.py:566
  42.7 0.9 %collective-permute-done.8.left_ref = f32[288,128]{1,0:T(8,128)S(1)} collective-permute-done((f32[288,128]{1,0:T(8,128)S(1)}, f32[288,128]{1,0:T(8,128)S(1)}, u32[]{:S(2)}, u32[]{:S(2)}) %collective-permute-start.8) | collective-permute-done | bytes 147488 | tf_op jit(solution)/shard_map/ppermute | solution.py:578
  43.6 2.6 %third_kernel.1.own_ref = f32[64,128]{1,0:T(8,128)S(1)} custom-call(f32[512,128]{1,0:T(8,128)S(1)} %get-tuple-element.32.own_ref, f32[288,128]{1,0:T(8,128)S(1)} %collective-permute-done.8.left_ref, f32[288,128]{1,0:T(8,128)S(1)} %collective-permute-done.9.right_ref, f32[320,128]{1,0:T(8,128)S(1)} %first_kernel.1.own_ref.older, ...), custom_call_target="tpu_custom_call" | custom-call | tf_op jit(solution)/shard_map/third_kernel/pallas_call | solution.py:566
  46.2 3.7 %collective-permute-start.10 = (f32[64,128]{1,0:T(8,128)S(1)}, f32[64,128]{1,0:T(8,128)S(1)}, u32[]{:S(2)}, u32[]{:S(2)}) collective-permute-start(f32[64,128]{1,0:T(8,128)S(1)} %third_kernel.1.own_ref), channel_id=1, source_target_pairs={{0,64},{64,0},{128,192},{192,128},{1,65},{65,1},{129,193},{193,129... | collective-permute-start | bytes 98312 | tf_op jit(solution)/shard_map/ppermute | solution.py:582
  49.9 0.9 %collective-permute-done.10.other_ref = f32[64,128]{1,0:T(8,128)S(1)} collective-permute-done((f32[64,128]{1,0:T(8,128)S(1)}, f32[64,128]{1,0:T(8,128)S(1)}, u32[]{:S(2)}, u32[]{:S(2)}) %collective-permute-start.10) | collective-permute-done | bytes 32800 | tf_op jit(solution)/shard_map/ppermute | solution.py:582
  50.8 0.1 sort_kernel.1
  50.9 1.1 %collective-permute-start.11 = (f32[64,128]{1,0:T(8,128)S(1)}, f32[64,128]{1,0:T(8,128)S(1)}, u32[]{:S(2)}, u32[]{:S(2)}) collective-permute-start(f32[64,128]{1,0:T(8,128)S(1)} %get-tuple-element.36), channel_id=1, source_target_pairs={{0,128},{64,192},{128,0},{192,64},{1,129},{65,193},{129,1},{193,65... | collective-permute-start | bytes 98312 | tf_op jit(solution)/shard_map/ppermute | solution.py:582
  52.0 3.2 %collective-permute-done.11.far_ref = f32[64,128]{1,0:T(8,128)S(1)} collective-permute-done((f32[64,128]{1,0:T(8,128)S(1)}, f32[64,128]{1,0:T(8,128)S(1)}, u32[]{:S(2)}, u32[]{:S(2)}) %collective-permute-start.11) | collective-permute-done | bytes 32800 | tf_op jit(solution)/shard_map/ppermute | solution.py:582
  55.3 0.6 %merge_kernel.1 = f32[32,2,128]{2,1,0:T(2,128)} custom-call(s32[1]{0:T(128)} %bitcast.group_ref, f32[64,128]{1,0:T(8,128)S(1)} %get-tuple-element.35.keep_ref, f32[64,128]{1,0:T(8,128)S(1)} %collective-permute-done.11.far_ref), custom_call_target="tpu_custom_call" | custom-call | tf_op jit(solution)/shard_map/merge_kernel/pallas_call | solution.py:566
  (4 shorter events, 0.0 us)
Async XLA Ops:
  1.3 4.4 %collective-permute-start = (f32[576,128]{1,0:T(8,128)S(1)}, f32[576,128]{1,0:T(8,128)S(1)}, u32[]{:S(2)}, u32[]{:S(2)}) collective-permute-start(f32[576,128]{1,0:T(8,128)S(1)} %get-tuple-element.21.raw_ref), channel_id=1, source_target_pairs={{0,64},{64,0},{128,192},{192,128},{1,65},{65,1},{129,193},{193,129... | collective-permute-start | bytes 884744 | tf_op jit(solution)/shard_map/ppermute | solution.py:582
  5.9 8.0 %collective-permute-start.1 = (f32[256,128]{1,0:T(8,128)S(1)}, f32[256,128]{1,0:T(8,128)S(1)}, u32[]{:S(2)}, u32[]{:S(2)}) collective-permute-start(f32[256,128]{1,0:T(8,128)S(1)} %get-tuple-element.23), channel_id=1, source_target_pairs={{0,128},{64,192},{128,0},{192,64},{1,129},{65,193},{129,1},{193,65... | collective-permute-start | bytes 393224 | tf_op jit(solution)/shard_map/ppermute | solution.py:582
  7.0 6.9 %collective-permute-start.2 = (f32[80,128]{1,0:T(8,128)S(1)}, f32[80,128]{1,0:T(8,128)S(1)}, u32[]{:S(2)}, u32[]{:S(2)}) collective-permute-start(f32[80,128]{1,0:T(8,128)S(1)} %get-tuple-element.24), channel_id=1, source_target_pairs={{0,1},{1,2},{2,3},{3,0},{64,195},{65,192},{66,193},{67,194},{128,1... | collective-permute-start | bytes 122888 | tf_op jit(solution)/shard_map/ppermute | solution.py:590
  13.9 1.5 %collective-permute-start.3 = (f32[336,128]{1,0:T(8,128)S(1)}, f32[336,128]{1,0:T(8,128)S(1)}, u32[]{:S(2)}, u32[]{:S(2)}) collective-permute-start(f32[336,128]{1,0:T(8,128)S(1)} %join_kernel.1.half_ref), channel_id=1, source_target_pairs={{0,64},{64,0},{128,192},{192,128},{1,65},{65,1},{129,193},{193,129... | collective-permute-start | bytes 516104 | tf_op jit(solution)/shard_map/ppermute | solution.py:582
  15.6 10.1 %collective-permute-start.4 = (f32[272,128]{1,0:T(8,128)S(1)}, f32[272,128]{1,0:T(8,128)S(1)}, u32[]{:S(2)}, u32[]{:S(2)}) collective-permute-start(f32[272,128]{1,0:T(8,128)S(1)} %get-tuple-element.26), channel_id=1, source_target_pairs={{0,4},{4,8},{8,12},{12,16},{16,20},{20,24},{24,28},{28,32},{32,36}... | collective-permute-start | bytes 417800 | tf_op jit(solution)/shard_map/ppermute | solution.py:578
  17.3 8.4 %collective-permute-start.5 = (f32[272,128]{1,0:T(8,128)S(1)}, f32[272,128]{1,0:T(8,128)S(1)}, u32[]{:S(2)}, u32[]{:S(2)}) collective-permute-start(f32[272,128]{1,0:T(8,128)S(1)} %get-tuple-element.27), channel_id=1, source_target_pairs={{0,60},{4,0},{8,4},{12,8},{16,12},{20,16},{24,20},{28,24},{32,28},... | collective-permute-start | bytes 417800 | tf_op jit(solution)/shard_map/ppermute | solution.py:578
  26.2 6.0 %collective-permute-start.7 = (f32[320,128]{1,0:T(8,128)S(1)}, f32[320,128]{1,0:T(8,128)S(1)}, u32[]{:S(2)}, u32[]{:S(2)}) collective-permute-start(f32[320,128]{1,0:T(8,128)S(1)} %first_kernel.1.own_ref.older), channel_id=1, source_target_pairs={{0,60},{4,0},{8,4},{12,8},{16,12},{20,16},{24,20},{28,24},{32,28},... | collective-permute-start | bytes 491528 | tf_op jit(solution)/shard_map/ppermute | solution.py:578
  29.7 6.3 %collective-permute-start.6 = (f32[320,128]{1,0:T(8,128)S(1)}, f32[320,128]{1,0:T(8,128)S(1)}, u32[]{:S(2)}, u32[]{:S(2)}) collective-permute-start(f32[320,128]{1,0:T(8,128)S(1)} %first_kernel.1.own_ref.older), channel_id=1, source_target_pairs={{0,4},{4,8},{8,12},{12,16},{16,20},{20,24},{24,28},{28,32},{32,36}... | collective-permute-start | bytes 491528 | tf_op jit(solution)/shard_map/ppermute | solution.py:578
  37.5 6.2 %collective-permute-start.8 = (f32[288,128]{1,0:T(8,128)S(1)}, f32[288,128]{1,0:T(8,128)S(1)}, u32[]{:S(2)}, u32[]{:S(2)}) collective-permute-start(f32[288,128]{1,0:T(8,128)S(1)} %get-tuple-element.33), channel_id=1, source_target_pairs={{0,4},{4,8},{8,12},{12,16},{16,20},{20,24},{24,28},{28,32},{32,36}... | collective-permute-start | bytes 442376 | tf_op jit(solution)/shard_map/ppermute | solution.py:578
  37.6 6.1 %collective-permute-start.9 = (f32[288,128]{1,0:T(8,128)S(1)}, f32[288,128]{1,0:T(8,128)S(1)}, u32[]{:S(2)}, u32[]{:S(2)}) collective-permute-start(f32[288,128]{1,0:T(8,128)S(1)} %get-tuple-element.34), channel_id=1, source_target_pairs={{0,60},{4,0},{8,4},{12,8},{16,12},{20,16},{24,20},{28,24},{32,28},... | collective-permute-start | bytes 442376 | tf_op jit(solution)/shard_map/ppermute | solution.py:578
  46.2 4.6 %collective-permute-start.10 = (f32[64,128]{1,0:T(8,128)S(1)}, f32[64,128]{1,0:T(8,128)S(1)}, u32[]{:S(2)}, u32[]{:S(2)}) collective-permute-start(f32[64,128]{1,0:T(8,128)S(1)} %third_kernel.1.own_ref), channel_id=1, source_target_pairs={{0,64},{64,0},{128,192},{192,128},{1,65},{65,1},{129,193},{193,129... | collective-permute-start | bytes 98312 | tf_op jit(solution)/shard_map/ppermute | solution.py:582
  50.9 4.4 %collective-permute-start.11 = (f32[64,128]{1,0:T(8,128)S(1)}, f32[64,128]{1,0:T(8,128)S(1)}, u32[]{:S(2)}, u32[]{:S(2)}) collective-permute-start(f32[64,128]{1,0:T(8,128)S(1)} %get-tuple-element.36), channel_id=1, source_target_pairs={{0,128},{64,192},{128,0},{192,64},{1,129},{65,193},{129,1},{193,65... | collective-permute-start | bytes 98312 | tf_op jit(solution)/shard_map/ppermute | solution.py:582

commit v4 on v3

--- a/solution.py
+++ b/solution.py
@@ -37,6 +37,16 @@
     return pl.multiple_of(index * 8, 8)
 
 
+def folded(first, second, last):
+    lanes = lane_ids(FINE)
+    inside = jnp.logical_and(lanes >= 24, lanes < 104)
+    return jnp.where(inside, first, roll_lanes(last, 80)), jnp.where(inside, second, roll_lanes(last, 32))
+
+
+def unfolded(first, second):
+    return jnp.where(lane_ids(FINE) < 72, roll_lanes(first, -80), roll_lanes(second, -32))
+
+
 def pack_kernel(flow_ref, level_ref, band_ref, nozzle_ref, raw_ref, mark_ref):
     for row in range(2):
         raw_ref[row * FLOW : (row + 1) * FLOW, :] = flow_ref[:, row, :]
@@ -134,6 +144,7 @@
         pressure = placed(3, 0)
         fixed_ref[0:64, :] = moving
         fixed_ref[64:128, :] = pressure
+        level_tiles = []
         for row in range(4):
             if own < 2:
                 low = remote[row // 2][64 + (row % 2) * FINE : 64 + (row % 2 + 1) * FINE, :]
@@ -148,10 +159,10 @@
                 3: lambda: jnp.where(lanes < 96, roll_lanes(high, 96), roll_lanes(far, 96 - 16 * row)),
             }[own]()
             fixed_ref[128 + row * FINE : 128 + (row + 1) * FINE, :] = value
-            if row < 3:
-                down_ref[row * FINE : (row + 1) * FINE, :] = value
-            if row > 0:
-                up_ref[(row - 1) * FINE : row * FINE, :] = value
+            level_tiles.append(value)
+        for out_ref, (near, next_row, far_row) in ((up_ref, (2, 3, 1)), (down_ref, (0, 1, 2))):
+            pair = folded(level_tiles[near], level_tiles[next_row], level_tiles[far_row])
+            out_ref[0:64, :], out_ref[64:128, :] = pair
         low, high, beside, few = mark_ref[0], mark_ref[1], half_ref[320:336, :], lane_ids(16)
         marks = {
             0: lambda: roll_lanes(jnp.where(few < 96, low, beside), 32),
@@ -161,9 +172,9 @@
         }[own]()
         fixed_ref[384:400, :] = marks
         for out_ref, row in ((up_ref, 1), (down_ref, 0)):
-            out_ref[192:224, :] = moving[row * FLOW : (row + 1) * FLOW, :]
-            out_ref[224:256, :] = pressure[row * FLOW : (row + 1) * FLOW, :]
-            out_ref[256:272, :] = marks
+            out_ref[128:160, :] = moving[row * FLOW : (row + 1) * FLOW, :]
+            out_ref[160:192, :] = pressure[row * FLOW : (row + 1) * FLOW, :]
+            out_ref[192:208, :] = marks
 
     for own in range(4):
 
@@ -352,19 +363,19 @@
     across_rows(places, speed_loader(speed_ref, None, 0), wrapped, rate_ref)
 
 
-def first_kernel(fixed_ref, left_ref, right_ref, speed_ref, rate_ref, out_ref):
+def first_kernel(fixed_ref, left_ref, right_ref, speed_ref, rate_ref, out_ref, send_ref, spare):
     moving = [
-        left_ref[192:224, :],
+        left_ref[128:160, :],
         fixed_ref[0:32, :],
         fixed_ref[32:64, :],
-        right_ref[192:224, :],
+        right_ref[128:160, :],
     ]
     lanes = lane_ids(FLOW)
     pressure = [
-        left_ref[224:256, :],
+        left_ref[160:192, :],
         fixed_ref[64:96, :],
         fixed_ref[96:128, :],
-        right_ref[224:256, :],
+        right_ref[160:192, :],
     ]
     pressure = [by_slot(lanes, p, roll_lanes(p, 40), roll_lanes(p, 80)) for p in pressure]
     for row in range(2):
@@ -386,12 +397,16 @@
             centred(roll_lanes(push, 1), roll_lanes(push, -1)),
             centred(push_down, push_up),
         )
-        out_ref[256 + row * FLOW : 256 + (row + 1) * FLOW, :] = here + STEP_FLOW * (advect - gradient)
-
+        pushed = here + STEP_FLOW * (advect - gradient)
+        out_ref[256 + row * FLOW : 256 + (row + 1) * FLOW, :] = pushed
+        send_ref[192 + row * FLOW : 192 + (row + 1) * FLOW, :] = pushed
+
+    spare[0:64, :] = unfolded(left_ref[0:64, :], left_ref[64:128, :])
+    spare[64:128, :] = unfolded(right_ref[0:64, :], right_ref[64:128, :])
     places = (
-        [(left_ref, FINE * row) for row in range(3)]
+        [(spare, 0), (left_ref, 0), (left_ref, 64)]
         + [(fixed_ref, 128 + FINE * row) for row in range(4)]
-        + [(right_ref, FINE * row) for row in range(3)]
+        + [(right_ref, 0), (right_ref, 64), (spare, 64)]
     )
 
     def store(index, z, value):
@@ -399,38 +414,49 @@
 
     rates = [(rate_ref, FINE * row) for row in range(4)]
     section(places, None, speed_loader(speed_ref, None, 0), rates, None, 0.0, 1.0, store)
+    send_ref[0:64, :], send_ref[64:128, :] = folded(out_ref[0:64, :], out_ref[64:128, :], out_ref[192:256, :])
+    send_ref[128:192, :] = out_ref[128:192, :]
 
 
 def middle_kernel(own_ref, old_left, old_right, speed_ref, rim_ref, rate_ref, wrapped):
-    spread_speeds(jnp.concatenate([old_left[192:224, :], old_right[192:224, :]], axis=0), rim_ref)
+    spread_speeds(jnp.concatenate([old_left[128:160, :], old_right[128:160, :]], axis=0), rim_ref)
     places = [(own_ref, FINE * row) for row in range(4)]
     across_rows(places, speed_loader(speed_ref, None, 0), wrapped, rate_ref)
 
 
 def second_kernel(
     own_ref, left_ref, right_ref, fixed_ref, old_left, old_right, speed_ref, rim_ref, rate_ref,
-    out_ref, up_ref, down_ref, wrapped,
+    out_ref, up_ref, down_ref, wrapped, spare,
 ):
-    source = [ref[256 + row * FLOW : 256 + (row + 1) * FLOW, :] for ref in (left_ref, own_ref, right_ref) for row in range(2)]
+    ends = ((left_ref, 192), (own_ref, 256), (right_ref, 192))
+    source = [ref[at + row * FLOW : at + (row + 1) * FLOW, :] for ref, at in ends for row in range(2)]
     for row in range(4):
         done = sweep(source[row], source[row + 1], source[row + 2], source[row + 1])
         out_ref[384 + row * FLOW : 384 + (row + 1) * FLOW, :] = done
         if row == 1:
-            up_ref[256:288, :] = done
+            up_ref[192:224, :] = done
         if row == 2:
-            down_ref[256:288, :] = done
-    places = [(ref, FINE * row) for ref in (left_ref, own_ref, right_ref) for row in range(4)]
-    initial = [(old_left, 128)] + [(fixed_ref, 128 + FINE * row) for row in range(4)] + [(old_right, 0)]
+            down_ref[192:224, :] = done
+    spare[0:64, :] = unfolded(left_ref[0:64, :], left_ref[64:128, :])
+    spare[64:128, :] = unfolded(right_ref[0:64, :], right_ref[64:128, :])
+    places = (
+        [(left_ref, FINE * row) for row in range(3)]
+        + [(spare, 0)]
+        + [(own_ref, FINE * row) for row in range(4)]
+        + [(right_ref, FINE * row) for row in range(3)]
+        + [(spare, 64)]
+    )
+    initial = [(old_left, 64)] + [(fixed_ref, 128 + FINE * row) for row in range(4)] + [(old_right, 0)]
 
     def store(index, z, value):
         out_ref[pl.ds(index * FINE + z, 8), :] = value
-        if index < 4:
-            up_ref[pl.ds(index * FINE + z, 8), :] = value
-        if index > 1:
-            down_ref[pl.ds((index - 2) * FINE + z, 8), :] = value
 
     rates = [None] + [(rate_ref, FINE * row) for row in range(4)] + [None]
     section(places, initial, speed_loader(speed_ref, rim_ref, -1), rates, wrapped, 0.75, 0.25, store)
+    for to_ref, at in ((up_ref, 0), (down_ref, 128)):
+        last = out_ref[at + 192 : at + 256, :]
+        to_ref[0:64, :], to_ref[64:128, :] = folded(out_ref[at : at + 64, :], out_ref[at + 64 : at + 128, :], last)
+        to_ref[128:192, :] = out_ref[at + 128 : at + 192, :]
 
 
 def late_kernel(own_ref, speed_ref, rim_ref, rate_ref, wrapped):
@@ -441,34 +467,38 @@
 def third_kernel(
     own_ref, left_ref, right_ref, older, older_left, older_right, fixed_ref, old_left, old_right,
     speed_ref, rim_ref, rate_ref,
-    out_ref, wrapped, shaped, normal_x, normal_z, summed,
+    out_ref, wrapped, shaped, normal_x, normal_z, summed, spare,
 ):
+    spare[0:64, :] = unfolded(left_ref[0:64, :], left_ref[64:128, :])
+    spare[64:128, :] = unfolded(right_ref[0:64, :], right_ref[64:128, :])
     places = (
-        [(left_ref, FINE * row) for row in range(4)]
+        [(left_ref, FINE * row) for row in range(3)]
+        + [(spare, 0)]
         + [(own_ref, FINE * row) for row in range(6)]
-        + [(right_ref, FINE * row) for row in range(4)]
+        + [(right_ref, FINE * row) for row in range(3)]
+        + [(spare, 64)]
     )
     initial = (
-        [(old_left, 64), (old_left, 128)]
+        [(old_left, 0), (old_left, 64)]
         + [(fixed_ref, 128 + FINE * row) for row in range(4)]
         + [(old_right, 0), (old_right, 64)]
     )
-    marks = [(old_left, 256)] * 2 + [(fixed_ref, 384)] * 4 + [(old_right, 256)] * 2
+    marks = [(old_left, 192)] * 2 + [(fixed_ref, 384)] * 4 + [(old_right, 192)] * 2
 
     def store(index, z, value):
         ref, at = initial[index]
         mark_ref, mark_at = marks[index]
         flag = mark_ref[pl.ds(mark_at + z // 8, 1), :]
         value = jnp.where(flag > 0.5, value, ref[pl.ds(at + z, 8), :]) * (1.0 / SHRINK)
-        phase = mark_ref[mark_at + 8 + (index + 2) % 4 : mark_at + 9 + (index + 2) % 4, :]
-        bottom = jnp.logical_and(lax.broadcasted_iota(jnp.int32, (8, LANES), 0) == 0, z == 0)
-        value = jnp.where(jnp.logical_and(bottom, phase == 2.0), SPREAD, value)
-        value = jnp.where(jnp.logical_and(bottom, phase == 1.0), -SPREAD, value)
         shaped[index, pl.ds(8 + z, 8), :] = value
 
     rates = [None] + [(rate_ref, FINE * row) for row in range(6)] + [None]
     section(places, initial, speed_loader(speed_ref, rim_ref, -2), rates, wrapped, 1.0 / 3.0, 2.0 / 3.0, store)
-    for index in range(8):
+    for index, (mark_ref, mark_at) in enumerate(marks):
+        at = mark_at + 8 + (index + 2) % 4
+        phase = mark_ref[at : at + 1, :]
+        inflow = jnp.where(phase == 2.0, SPREAD, jnp.where(phase == 1.0, -SPREAD, shaped[index, 8:9, :]))
+        shaped[index, 8:9, :] = inflow
         shaped[index, 0:8, :] = shaped[index, 64:72, :]
         shaped[index, 72:80, :] = shaped[index, 8:16, :]
 
@@ -513,9 +543,9 @@
 
     in_pairs(forces)
 
-    source = [older_left[288:320, :], older[256:288, :], older[288:320, :], older_right[256:288, :]]
-    once = [left_ref[256:288, :]] + [own_ref[384 + row * FLOW : 384 + (row + 1) * FLOW, :] for row in range(4)]
-    once = once + [right_ref[256:288, :]]
+    source = [older_left[224:256, :], older[256:288, :], older[288:320, :], older_right[192:224, :]]
+    once = [left_ref[192:224, :]] + [own_ref[384 + row * FLOW : 384 + (row + 1) * FLOW, :] for row in range(4)]
+    once = once + [right_ref[192:224, :]]
     twice = [sweep(once[row], once[row + 1], once[row + 2], source[row]) for row in range(4)]
     thrice = [sweep(twice[row], twice[row + 1], twice[row + 2], source[row + 1]) for row in range(2)]
 
@@ -608,7 +638,7 @@
     far_half = crossed(half, 1)
     fixed, up, down = call(
         assemble_kernel,
-        [(400, LANES), (272, LANES), (272, LANES)],
+        [(400, LANES), (208, LANES), (208, LANES)],
         [],
         group,
         raw,
@@ -621,15 +651,17 @@
     speed_shape = (3, 2, FINE, LANES)
     old_left, old_right = shifted(up, "gx", 1), shifted(down, "gx", -1)
     speeds, rates = call(inner_kernel, [speed_shape, (256, LANES)], [(4, 80, LANES)], fixed)
-    own = call(first_kernel, [(320, LANES)], [], fixed, old_left, old_right, speeds, rates)
-    left, right = shifted(own, "gx", 1), shifted(own, "gx", -1)
+    own, send = call(
+        first_kernel, [(320, LANES), (256, LANES)], [(128, LANES)], fixed, old_left, old_right, speeds, rates
+    )
+    left, right = shifted(send, "gx", 1), shifted(send, "gx", -1)
     rim, rates = call(
         middle_kernel, [speed_shape, (256, LANES)], [(4, 80, LANES)], own, old_left, old_right, speeds
     )
     newer, up, down = call(
         second_kernel,
-        [(512, LANES), (288, LANES), (288, LANES)],
-        [(6, 80, LANES)],
+        [(512, LANES), (224, LANES), (224, LANES)],
+        [(6, 80, LANES), (128, LANES)],
         own,
         left,
         right,
@@ -645,7 +677,7 @@
     result = call(
         third_kernel,
         [(64, LANES)],
-        [(8, 80, LANES), (8, 80, LANES), (6, FINE, LANES), (4, 80, LANES), (4, 2 * FINE, LANES)],
+        [(8, 80, LANES), (8, 80, LANES), (6, FINE, LANES), (4, 80, LANES), (4, 2 * FINE, LANES), (128, LANES)],
         newer,
         newer_left,
         newer_right,

time: 56 us -> 55 us (0.982)
  waiting for transfers between devices: 18.4 us -> 17.1 us
    ppermute x6, waiting for transfers between devices: 7.49 us -> 6.09 us  [shifted(): lax.ppermute(value, axis, [(i, (i + shift) % count) for i in range(count)])]
where the time goes in v4:
time: 55 us; the launch traced here: 54.9 us
  starting transfers between devices  25.2 us (46%)
  waiting for transfers between devices  17.1 us (31%)
  Pallas kernels  12.6 us (23%)
    ppermute x6, starting transfers between devices, shifted(): lax.ppermute(value, axis, [(i, (i + shift) % count) for i in range(count)])  13.4 us
    pallas_call x12, Pallas kernels, call(): pl.pallas_call(kernel, out_shape=shapes if len(shapes) > 1 else shapes[0]...  12.6 us
    ppermute x5, starting transfers between devices, crossed(): lax.ppermute(value, 'grp', [(i, i ^ bit) for i in range(lax.axis_size('gr...  9.13 us
    ppermute x5, waiting for transfers between devices, crossed(): lax.ppermute(value, 'grp', [(i, i ^ bit) for i in range(lax.axis_size('gr...  6.79 us
    ppermute x6, waiting for transfers between devices, shifted(): lax.ppermute(value, axis, [(i, (i + shift) % count) for i in range(count)])  6.09 us
    ppermute x1, waiting for transfers between devices, to_next_blocks(): return lax.ppermute(value, ('grp', 'gy'), pairs)  4.19 us
    ppermute x1, starting transfers between devices, to_next_blocks(): return lax.ppermute(value, ('grp', 'gy'), pairs)  2.69 us
  transfers between devices with their start and end apart: 12, of which 9 were waited for; matrix products, arithmetic and copies ran while one was open for 0% of the time, Pallas kernels for 9%

profile of v4, /device:TPU:1, one launch (start us, length us, event | category | flops | bytes accessed | tf_op | source)
XLA Modules:
  0.0 54.9 jit_solution(7679112710667135221)
XLA Ops:
  0.0 1.3 %pack_kernel.1 = (f32[576,128]{1,0:T(8,128)S(1)}, f32[2,16,128]{2,1,0:T(8,128)S(1)}) custom-call(f32[32,2,128]{2,1,0:T(2,128)} %bitcast.6, f32[64,4,256]{2,1,0:T(4,128)} %bitcast.5, s32[8,16]{1,0:T(8,128)} %bitcast.7, s32[4,256]{1,0:T(4,128)} %nozzle_ref.1), custom_call_target="tpu_custom_call" | custom-call | tf_op jit(solution)/shard_map/pack_kernel/pallas_call | solution.py:596
  1.3 3.2 %collective-permute-start = (f32[576,128]{1,0:T(8,128)S(1)}, f32[576,128]{1,0:T(8,128)S(1)}, u32[]{:S(2)}, u32[]{:S(2)}) collective-permute-start(f32[576,128]{1,0:T(8,128)S(1)} %get-tuple-element.23.raw_ref), channel_id=1, source_target_pairs={{0,64},{64,0},{128,192},{192,128},{1,65},{65,1},{129,193},{193,129... | collective-permute-start | bytes 884744 | tf_op jit(solution)/shard_map/ppermute | solution.py:612
  4.5 1.2 %collective-permute-done.other_ref = f32[576,128]{1,0:T(8,128)S(1)} collective-permute-done((f32[576,128]{1,0:T(8,128)S(1)}, f32[576,128]{1,0:T(8,128)S(1)}, u32[]{:S(2)}, u32[]{:S(2)}) %collective-permute-start) | collective-permute-done | bytes 294944 | tf_op jit(solution)/shard_map/ppermute | solution.py:612
  5.7 0.2 split_kernel.1
  5.9 1.1 %collective-permute-start.1 = (f32[256,128]{1,0:T(8,128)S(1)}, f32[256,128]{1,0:T(8,128)S(1)}, u32[]{:S(2)}, u32[]{:S(2)}) collective-permute-start(f32[256,128]{1,0:T(8,128)S(1)} %get-tuple-element.25), channel_id=1, source_target_pairs={{0,128},{64,192},{128,0},{192,64},{1,129},{65,193},{129,1},{193,65... | collective-permute-start | bytes 393224 | tf_op jit(solution)/shard_map/ppermute | solution.py:612
  7.0 2.7 %collective-permute-start.2 = (f32[80,128]{1,0:T(8,128)S(1)}, f32[80,128]{1,0:T(8,128)S(1)}, u32[]{:S(2)}, u32[]{:S(2)}) collective-permute-start(f32[80,128]{1,0:T(8,128)S(1)} %get-tuple-element.26), channel_id=1, source_target_pairs={{0,1},{1,2},{2,3},{3,0},{64,195},{65,192},{66,193},{67,194},{128,1... | collective-permute-start | bytes 122888 | tf_op jit(solution)/shard_map/ppermute | solution.py:620
  9.7 4.2 %collective-permute-done.2.edge_ref = f32[80,128]{1,0:T(8,128)S(1)} collective-permute-done((f32[80,128]{1,0:T(8,128)S(1)}, f32[80,128]{1,0:T(8,128)S(1)}, u32[]{:S(2)}, u32[]{:S(2)}) %collective-permute-start.2) | collective-permute-done | bytes 40992 | tf_op jit(solution)/shard_map/ppermute | solution.py:620
  13.9 0.1 collective-permute-start.3
  14.0 1.4 %collective-permute-done.3.far_half_ref = f32[336,128]{1,0:T(8,128)S(1)} collective-permute-done((f32[336,128]{1,0:T(8,128)S(1)}, f32[336,128]{1,0:T(8,128)S(1)}, u32[]{:S(2)}, u32[]{:S(2)}) %collective-permute-start.3) | collective-permute-done | bytes 172064 | tf_op jit(solution)/shard_map/ppermute | solution.py:612
  15.4 0.3 assemble_kernel.1
  15.7 1.7 %collective-permute-start.4 = (f32[208,128]{1,0:T(8,128)S(1)}, f32[208,128]{1,0:T(8,128)S(1)}, u32[]{:S(2)}, u32[]{:S(2)}) collective-permute-start(f32[208,128]{1,0:T(8,128)S(1)} %get-tuple-element.28), channel_id=1, source_target_pairs={{0,4},{4,8},{8,12},{12,16},{16,20},{20,24},{24,28},{28,32},{32,36}... | collective-permute-start | bytes 319496 | tf_op jit(solution)/shard_map/ppermute | solution.py:608
  17.4 4.6 %collective-permute-start.5 = (f32[208,128]{1,0:T(8,128)S(1)}, f32[208,128]{1,0:T(8,128)S(1)}, u32[]{:S(2)}, u32[]{:S(2)}) collective-permute-start(f32[208,128]{1,0:T(8,128)S(1)} %get-tuple-element.29), channel_id=1, source_target_pairs={{0,60},{4,0},{8,4},{12,8},{16,12},{20,16},{24,20},{28,24},{32,28},... | collective-permute-start | bytes 319496 | tf_op jit(solution)/shard_map/ppermute | solution.py:608
  22.0 1.8 %inner_kernel.1 = (f32[3,2,64,128]{3,2,1,0:T(8,128)S(1)}, f32[256,128]{1,0:T(8,128)S(1)}) custom-call(f32[400,128]{1,0:T(8,128)S(1)} %get-tuple-element.27.fixed_ref), custom_call_target="tpu_custom_call" | custom-call | tf_op jit(solution)/shard_map/inner_kernel/pallas_call | solution.py:596
  23.7 1.3 %collective-permute-done.4.left_ref.old_left = f32[208,128]{1,0:T(8,128)S(1)} collective-permute-done((f32[208,128]{1,0:T(8,128)S(1)}, f32[208,128]{1,0:T(8,128)S(1)}, u32[]{:S(2)}, u32[]{:S(2)}) %collective-permute-start.4) | collective-permute-done | bytes 106528 | tf_op jit(solution)/shard_map/ppermute | solution.py:608
  25.1 0.7 %first_kernel.1 = (f32[320,128]{1,0:T(8,128)S(1)}, f32[256,128]{1,0:T(8,128)S(1)}) custom-call(f32[400,128]{1,0:T(8,128)S(1)} %get-tuple-element.27.fixed_ref, f32[208,128]{1,0:T(8,128)S(1)} %collective-permute-done.4.left_ref.old_left, f32[208,128]{1,0:T(8,128)S(1)} %collective-permute-done.5.right_ref.old_right, ...), custom_call_target="tpu_custom_call" | custom-call | tf_op jit(solution)/shard_map/first_kernel/pallas_call | solution.py:596
  25.7 3.5 %collective-permute-start.7 = (f32[256,128]{1,0:T(8,128)S(1)}, f32[256,128]{1,0:T(8,128)S(1)}, u32[]{:S(2)}, u32[]{:S(2)}) collective-permute-start(f32[256,128]{1,0:T(8,128)S(1)} %get-tuple-element.33), channel_id=1, source_target_pairs={{0,60},{4,0},{8,4},{12,8},{16,12},{20,16},{24,20},{28,24},{32,28},... | collective-permute-start | bytes 393224 | tf_op jit(solution)/shard_map/ppermute | solution.py:608
  29.2 0.0 collective-permute-start.6
  29.2 1.8 %middle_kernel.1 = (f32[3,2,64,128]{3,2,1,0:T(8,128)S(1)}, f32[256,128]{1,0:T(8,128)S(1)}) custom-call(f32[320,128]{1,0:T(8,128)S(1)} %get-tuple-element.32.own_ref.older, f32[208,128]{1,0:T(8,128)S(1)} %collective-permute-done.4.left_ref.old_left, f32[208,128]{1,0:T(8,128)S(1)} %collective-permute-done.5.right_ref.old_right, ...), custom_call_target="tpu_custom_call" | custom-call | tf_op jit(solution)/shard_map/middle_kernel/pallas_call | solution.py:596
  31.0 0.2 collective-permute-done.7.right_ref.older_right
  31.1 4.0 %collective-permute-done.6.left_ref.older_left = f32[256,128]{1,0:T(8,128)S(1)} collective-permute-done((f32[256,128]{1,0:T(8,128)S(1)}, f32[256,128]{1,0:T(8,128)S(1)}, u32[]{:S(2)}, u32[]{:S(2)}) %collective-permute-start.6) | collective-permute-done | bytes 131104 | tf_op jit(solution)/shard_map/ppermute | solution.py:608
  35.1 1.6 %second_kernel.1 = (f32[512,128]{1,0:T(8,128)S(1)}, f32[224,128]{1,0:T(8,128)S(1)}, f32[224,128]{1,0:T(8,128)S(1)}) custom-call(f32[320,128]{1,0:T(8,128)S(1)} %get-tuple-element.32.own_ref.older, f32[256,128]{1,0:T(8,128)S(1)} %collective-permute-done.6.left_ref.older_left, f32[256,128]{1,0:T(8,128)S(1)} %collective-permute-done.7.right_ref.older_right, ...), custom_call_target="tpu_custom_call" | custom-call | tf_op jit(solution)/shard_map/second_kernel/pallas_call | solution.py:596
  36.8 0.1 collective-permute-start.8
  36.9 3.6 %collective-permute-start.9 = (f32[224,128]{1,0:T(8,128)S(1)}, f32[224,128]{1,0:T(8,128)S(1)}, u32[]{:S(2)}, u32[]{:S(2)}) collective-permute-start(f32[224,128]{1,0:T(8,128)S(1)} %get-tuple-element.38), channel_id=1, source_target_pairs={{0,60},{4,0},{8,4},{12,8},{16,12},{20,16},{24,20},{28,24},{32,28},... | collective-permute-start | bytes 344072 | tf_op jit(solution)/shard_map/ppermute | solution.py:608
  40.4 1.6 %late_kernel.1.rate_ref = f32[384,128]{1,0:T(8,128)S(1)} custom-call(f32[512,128]{1,0:T(8,128)S(1)} %get-tuple-element.36.own_ref, f32[3,2,64,128]{3,2,1,0:T(8,128)S(1)} %get-tuple-element.30.speed_ref, f32[3,2,64,128]{3,2,1,0:T(8,128)S(1)} %get-tuple-element.34.rim_ref), custom_call_target="tpu_custom_call" | custom-call | tf_op jit(solution)/shard_map/late_kernel/pallas_call | solution.py:596
  42.0 0.6 %collective-permute-done.8.left_ref = f32[224,128]{1,0:T(8,128)S(1)} collective-permute-done((f32[224,128]{1,0:T(8,128)S(1)}, f32[224,128]{1,0:T(8,128)S(1)}, u32[]{:S(2)}, u32[]{:S(2)}) %collective-permute-start.8) | collective-permute-done | bytes 114720 | tf_op jit(solution)/shard_map/ppermute | solution.py:608
  42.6 2.7 %third_kernel.1.own_ref = f32[64,128]{1,0:T(8,128)S(1)} custom-call(f32[512,128]{1,0:T(8,128)S(1)} %get-tuple-element.36.own_ref, f32[224,128]{1,0:T(8,128)S(1)} %collective-permute-done.8.left_ref, f32[224,128]{1,0:T(8,128)S(1)} %collective-permute-done.9.right_ref, f32[320,128]{1,0:T(8,128)S(1)} %get-tuple-element.32.own_ref.older, ...), custom_call_target="tpu_custom_call" | custom-call | tf_op jit(solution)/shard_map/third_kernel/pallas_call | solution.py:596
  45.3 3.7 %collective-permute-start.10 = (f32[64,128]{1,0:T(8,128)S(1)}, f32[64,128]{1,0:T(8,128)S(1)}, u32[]{:S(2)}, u32[]{:S(2)}) collective-permute-start(f32[64,128]{1,0:T(8,128)S(1)} %third_kernel.1.own_ref), channel_id=1, source_target_pairs={{0,64},{64,0},{128,192},{192,128},{1,65},{65,1},{129,193},{193,129... | collective-permute-start | bytes 98312 | tf_op jit(solution)/shard_map/ppermute | solution.py:612
  49.0 0.9 %collective-permute-done.10.other_ref = f32[64,128]{1,0:T(8,128)S(1)} collective-permute-done((f32[64,128]{1,0:T(8,128)S(1)}, f32[64,128]{1,0:T(8,128)S(1)}, u32[]{:S(2)}, u32[]{:S(2)}) %collective-permute-start.10) | collective-permute-done | bytes 32800 | tf_op jit(solution)/shard_map/ppermute | solution.py:612
  49.8 0.1 sort_kernel.1
  49.9 1.0 %collective-permute-start.11 = (f32[64,128]{1,0:T(8,128)S(1)}, f32[64,128]{1,0:T(8,128)S(1)}, u32[]{:S(2)}, u32[]{:S(2)}) collective-permute-start(f32[64,128]{1,0:T(8,128)S(1)} %get-tuple-element.40), channel_id=1, source_target_pairs={{0,128},{64,192},{128,0},{192,64},{1,129},{65,193},{129,1},{193,65... | collective-permute-start | bytes 98312 | tf_op jit(solution)/shard_map/ppermute | solution.py:612
  51.0 3.3 %collective-permute-done.11.far_ref = f32[64,128]{1,0:T(8,128)S(1)} collective-permute-done((f32[64,128]{1,0:T(8,128)S(1)}, f32[64,128]{1,0:T(8,128)S(1)}, u32[]{:S(2)}, u32[]{:S(2)}) %collective-permute-start.11) | collective-permute-done | bytes 32800 | tf_op jit(solution)/shard_map/ppermute | solution.py:612
  54.3 0.6 %merge_kernel.1 = f32[32,2,128]{2,1,0:T(2,128)} custom-call(s32[1]{0:T(128)} %bitcast.group_ref, f32[64,128]{1,0:T(8,128)S(1)} %get-tuple-element.39.keep_ref, f32[64,128]{1,0:T(8,128)S(1)} %collective-permute-done.11.far_ref), custom_call_target="tpu_custom_call" | custom-call | tf_op jit(solution)/shard_map/merge_kernel/pallas_call | solution.py:596
  (4 shorter events, 0.0 us)
Async XLA Ops:
  1.3 4.4 %collective-permute-start = (f32[576,128]{1,0:T(8,128)S(1)}, f32[576,128]{1,0:T(8,128)S(1)}, u32[]{:S(2)}, u32[]{:S(2)}) collective-permute-start(f32[576,128]{1,0:T(8,128)S(1)} %get-tuple-element.23.raw_ref), channel_id=1, source_target_pairs={{0,64},{64,0},{128,192},{192,128},{1,65},{65,1},{129,193},{193,129... | collective-permute-start | bytes 884744 | tf_op jit(solution)/shard_map/ppermute | solution.py:612
  5.9 8.0 %collective-permute-start.1 = (f32[256,128]{1,0:T(8,128)S(1)}, f32[256,128]{1,0:T(8,128)S(1)}, u32[]{:S(2)}, u32[]{:S(2)}) collective-permute-start(f32[256,128]{1,0:T(8,128)S(1)} %get-tuple-element.25), channel_id=1, source_target_pairs={{0,128},{64,192},{128,0},{192,64},{1,129},{65,193},{129,1},{193,65... | collective-permute-start | bytes 393224 | tf_op jit(solution)/shard_map/ppermute | solution.py:612
  7.0 6.9 %collective-permute-start.2 = (f32[80,128]{1,0:T(8,128)S(1)}, f32[80,128]{1,0:T(8,128)S(1)}, u32[]{:S(2)}, u32[]{:S(2)}) collective-permute-start(f32[80,128]{1,0:T(8,128)S(1)} %get-tuple-element.26), channel_id=1, source_target_pairs={{0,1},{1,2},{2,3},{3,0},{64,195},{65,192},{66,193},{67,194},{128,1... | collective-permute-start | bytes 122888 | tf_op jit(solution)/shard_map/ppermute | solution.py:620
  13.9 1.5 %collective-permute-start.3 = (f32[336,128]{1,0:T(8,128)S(1)}, f32[336,128]{1,0:T(8,128)S(1)}, u32[]{:S(2)}, u32[]{:S(2)}) collective-permute-start(f32[336,128]{1,0:T(8,128)S(1)} %join_kernel.1.half_ref), channel_id=1, source_target_pairs={{0,64},{64,0},{128,192},{192,128},{1,65},{65,1},{129,193},{193,129... | collective-permute-start | bytes 516104 | tf_op jit(solution)/shard_map/ppermute | solution.py:612
  15.7 9.4 %collective-permute-start.4 = (f32[208,128]{1,0:T(8,128)S(1)}, f32[208,128]{1,0:T(8,128)S(1)}, u32[]{:S(2)}, u32[]{:S(2)}) collective-permute-start(f32[208,128]{1,0:T(8,128)S(1)} %get-tuple-element.28), channel_id=1, source_target_pairs={{0,4},{4,8},{8,12},{12,16},{16,20},{20,24},{24,28},{28,32},{32,36}... | collective-permute-start | bytes 319496 | tf_op jit(solution)/shard_map/ppermute | solution.py:608
  17.4 7.7 %collective-permute-start.5 = (f32[208,128]{1,0:T(8,128)S(1)}, f32[208,128]{1,0:T(8,128)S(1)}, u32[]{:S(2)}, u32[]{:S(2)}) collective-permute-start(f32[208,128]{1,0:T(8,128)S(1)} %get-tuple-element.29), channel_id=1, source_target_pairs={{0,60},{4,0},{8,4},{12,8},{16,12},{20,16},{24,20},{28,24},{32,28},... | collective-permute-start | bytes 319496 | tf_op jit(solution)/shard_map/ppermute | solution.py:608
  25.7 5.4 %collective-permute-start.7 = (f32[256,128]{1,0:T(8,128)S(1)}, f32[256,128]{1,0:T(8,128)S(1)}, u32[]{:S(2)}, u32[]{:S(2)}) collective-permute-start(f32[256,128]{1,0:T(8,128)S(1)} %get-tuple-element.33), channel_id=1, source_target_pairs={{0,60},{4,0},{8,4},{12,8},{16,12},{20,16},{24,20},{28,24},{32,28},... | collective-permute-start | bytes 393224 | tf_op jit(solution)/shard_map/ppermute | solution.py:608
  29.2 5.9 %collective-permute-start.6 = (f32[256,128]{1,0:T(8,128)S(1)}, f32[256,128]{1,0:T(8,128)S(1)}, u32[]{:S(2)}, u32[]{:S(2)}) collective-permute-start(f32[256,128]{1,0:T(8,128)S(1)} %get-tuple-element.33), channel_id=1, source_target_pairs={{0,4},{4,8},{8,12},{12,16},{16,20},{20,24},{24,28},{28,32},{32,36}... | collective-permute-start | bytes 393224 | tf_op jit(solution)/shard_map/ppermute | solution.py:608
  36.8 5.8 %collective-permute-start.8 = (f32[224,128]{1,0:T(8,128)S(1)}, f32[224,128]{1,0:T(8,128)S(1)}, u32[]{:S(2)}, u32[]{:S(2)}) collective-permute-start(f32[224,128]{1,0:T(8,128)S(1)} %get-tuple-element.37), channel_id=1, source_target_pairs={{0,4},{4,8},{8,12},{12,16},{16,20},{20,24},{24,28},{28,32},{32,36}... | collective-permute-start | bytes 344072 | tf_op jit(solution)/shard_map/ppermute | solution.py:608
  36.9 5.7 %collective-permute-start.9 = (f32[224,128]{1,0:T(8,128)S(1)}, f32[224,128]{1,0:T(8,128)S(1)}, u32[]{:S(2)}, u32[]{:S(2)}) collective-permute-start(f32[224,128]{1,0:T(8,128)S(1)} %get-tuple-element.38), channel_id=1, source_target_pairs={{0,60},{4,0},{8,4},{12,8},{16,12},{20,16},{24,20},{28,24},{32,28},... | collective-permute-start | bytes 344072 | tf_op jit(solution)/shard_map/ppermute | solution.py:608
  45.3 4.5 %collective-permute-start.10 = (f32[64,128]{1,0:T(8,128)S(1)}, f32[64,128]{1,0:T(8,128)S(1)}, u32[]{:S(2)}, u32[]{:S(2)}) collective-permute-start(f32[64,128]{1,0:T(8,128)S(1)} %third_kernel.1.own_ref), channel_id=1, source_target_pairs={{0,64},{64,0},{128,192},{192,128},{1,65},{65,1},{129,193},{193,129... | collective-permute-start | bytes 98312 | tf_op jit(solution)/shard_map/ppermute | solution.py:612
  49.9 4.4 %collective-permute-start.11 = (f32[64,128]{1,0:T(8,128)S(1)}, f32[64,128]{1,0:T(8,128)S(1)}, u32[]{:S(2)}, u32[]{:S(2)}) collective-permute-start(f32[64,128]{1,0:T(8,128)S(1)} %get-tuple-element.40), channel_id=1, source_target_pairs={{0,128},{64,192},{128,0},{192,64},{1,129},{65,193},{129,1},{193,65... | collective-permute-start | bytes 98312 | tf_op jit(solution)/shard_map/ppermute | solution.py:612

commit v5 on v4

--- a/solution.py
+++ b/solution.py
@@ -45,6 +45,51 @@
 
 def unfolded(first, second):
     return jnp.where(lane_ids(FINE) < 72, roll_lanes(first, -80), roll_lanes(second, -32))
+
+
+def lay(value, base, first, last, shift):
+    lanes = lane_ids(value.shape[0])
+    inside = jnp.logical_and(lanes >= first, lanes < last)
+    if last > LANES:
+        inside = jnp.logical_or(lanes >= first, lanes < last - LANES)
+    return jnp.where(inside, roll_lanes(value, shift), base)
+
+
+def parted(limits, parts):
+    lanes = lane_ids(parts[0].shape[0])
+    value = parts[-1]
+    for limit, part in reversed(list(zip(limits, parts))):
+        value = jnp.where(lanes < limit, part, value)
+    return value
+
+
+def sent_pressure(ref):
+    return parted((16, 32), (roll_lanes(ref[64:96, :], -8), roll_lanes(ref[96:128, :], 8), roll_lanes(ref[128:160, :], -88)))
+
+
+def sent_source(ref, row):
+    at = row * FLOW
+    rest = ref[192:224, :]
+    return parted(
+        (48, 64),
+        (
+            roll_lanes(ref[128 + at : 160 + at, :], -104),
+            roll_lanes(ref[64 + at : 96 + at, :], 40),
+            rest if row else roll_lanes(rest, 64),
+        ),
+    )
+
+
+def sent_sweep(ref):
+    return parted(
+        (48, 96, 112),
+        (
+            roll_lanes(ref[128:160, :], -104),
+            roll_lanes(ref[160:192, :], -56),
+            roll_lanes(ref[64:96, :], -40),
+            roll_lanes(ref[96:128, :], -24),
+        ),
+    )
 
 
 def pack_kernel(flow_ref, level_ref, band_ref, nozzle_ref, raw_ref, mark_ref):
@@ -162,7 +207,12 @@
             level_tiles.append(value)
         for out_ref, (near, next_row, far_row) in ((up_ref, (2, 3, 1)), (down_ref, (0, 1, 2))):
             pair = folded(level_tiles[near], level_tiles[next_row], level_tiles[far_row])
-            out_ref[0:64, :], out_ref[64:128, :] = pair
+            out_ref[0:64, :] = pair[0]
+            row = 1 if near else 0
+            push = pressure[row * FLOW : (row + 1) * FLOW, :]
+            out_ref[64:96, :] = lay(push, pair[1][0:32, :], 8, 24, 8)
+            out_ref[96:128, :] = lay(push, pair[1][32:64, :], 8, 24, -8)
+            out_ref[128:160, :] = lay(push, moving[row * FLOW : (row + 1) * FLOW, :], 120, 128, 88)
         low, high, beside, few = mark_ref[0], mark_ref[1], half_ref[320:336, :], lane_ids(16)
         marks = {
             0: lambda: roll_lanes(jnp.where(few < 96, low, beside), 32),
@@ -171,10 +221,8 @@
             3: lambda: roll_lanes(jnp.where(few < 32, beside, high), 96),
         }[own]()
         fixed_ref[384:400, :] = marks
-        for out_ref, row in ((up_ref, 1), (down_ref, 0)):
-            out_ref[128:160, :] = moving[row * FLOW : (row + 1) * FLOW, :]
-            out_ref[160:192, :] = pressure[row * FLOW : (row + 1) * FLOW, :]
-            out_ref[192:208, :] = marks
+        for out_ref in (up_ref, down_ref):
+            out_ref[160:176, :] = marks
 
     for own in range(4):
 
@@ -372,10 +420,10 @@
     ]
     lanes = lane_ids(FLOW)
     pressure = [
-        left_ref[160:192, :],
+        sent_pressure(left_ref),
         fixed_ref[64:96, :],
         fixed_ref[96:128, :],
-        right_ref[160:192, :],
+        sent_pressure(right_ref),
     ]
     pressure = [by_slot(lanes, p, roll_lanes(p, 40), roll_lanes(p, 80)) for p in pressure]
     for row in range(2):
@@ -397,9 +445,7 @@
             centred(roll_lanes(push, 1), roll_lanes(push, -1)),
             centred(push_down, push_up),
         )
-        pushed = here + STEP_FLOW * (advect - gradient)
-        out_ref[256 + row * FLOW : 256 + (row + 1) * FLOW, :] = pushed
-        send_ref[192 + row * FLOW : 192 + (row + 1) * FLOW, :] = pushed
+        out_ref[256 + row * FLOW : 256 + (row + 1) * FLOW, :] = here + STEP_FLOW * (advect - gradient)
 
     spare[0:64, :] = unfolded(left_ref[0:64, :], left_ref[64:128, :])
     spare[64:128, :] = unfolded(right_ref[0:64, :], right_ref[64:128, :])
@@ -414,8 +460,11 @@
 
     rates = [(rate_ref, FINE * row) for row in range(4)]
     section(places, None, speed_loader(speed_ref, None, 0), rates, None, 0.0, 1.0, store)
-    send_ref[0:64, :], send_ref[64:128, :] = folded(out_ref[0:64, :], out_ref[64:128, :], out_ref[192:256, :])
-    send_ref[128:192, :] = out_ref[128:192, :]
+    source = out_ref[256:320, :]
+    send_ref[0:64, :], beside = folded(out_ref[0:64, :], out_ref[64:128, :], out_ref[192:256, :])
+    send_ref[64:128, :] = lay(source, beside, 8, 24, -40)
+    send_ref[128:192, :] = lay(source, out_ref[128:192, :], 104, 152, 104)
+    send_ref[192:224, :] = lay(source[0:32, :], source[32:64, :], 0, 64, 64)
 
 
 def middle_kernel(own_ref, old_left, old_right, speed_ref, rim_ref, rate_ref, wrapped):
@@ -428,15 +477,12 @@
     own_ref, left_ref, right_ref, fixed_ref, old_left, old_right, speed_ref, rim_ref, rate_ref,
     out_ref, up_ref, down_ref, wrapped, spare,
 ):
-    ends = ((left_ref, 192), (own_ref, 256), (right_ref, 192))
-    source = [ref[at + row * FLOW : at + (row + 1) * FLOW, :] for ref, at in ends for row in range(2)]
+    source = [sent_source(left_ref, row) for row in range(2)]
+    source += [own_ref[256 + row * FLOW : 256 + (row + 1) * FLOW, :] for row in range(2)]
+    source += [sent_source(right_ref, row) for row in range(2)]
     for row in range(4):
         done = sweep(source[row], source[row + 1], source[row + 2], source[row + 1])
         out_ref[384 + row * FLOW : 384 + (row + 1) * FLOW, :] = done
-        if row == 1:
-            up_ref[192:224, :] = done
-        if row == 2:
-            down_ref[192:224, :] = done
     spare[0:64, :] = unfolded(left_ref[0:64, :], left_ref[64:128, :])
     spare[64:128, :] = unfolded(right_ref[0:64, :], right_ref[64:128, :])
     places = (
@@ -455,8 +501,12 @@
     section(places, initial, speed_loader(speed_ref, rim_ref, -1), rates, wrapped, 0.75, 0.25, store)
     for to_ref, at in ((up_ref, 0), (down_ref, 128)):
         last = out_ref[at + 192 : at + 256, :]
-        to_ref[0:64, :], to_ref[64:128, :] = folded(out_ref[at : at + 64, :], out_ref[at + 64 : at + 128, :], last)
-        to_ref[128:192, :] = out_ref[at + 128 : at + 192, :]
+        to_ref[0:64, :], beside = folded(out_ref[at : at + 64, :], out_ref[at + 64 : at + 128, :], last)
+        done = out_ref[448:480, :] if at else out_ref[416:448, :]
+        to_ref[64:96, :] = lay(done, beside[0:32, :], 8, 24, 40)
+        to_ref[96:128, :] = lay(done, beside[32:64, :], 8, 16, 24)
+        to_ref[128:160, :] = lay(done, out_ref[at + 128 : at + 160, :], 104, 152, 104)
+        to_ref[160:192, :] = lay(done, out_ref[at + 160 : at + 192, :], 104, 152, 56)
 
 
 def late_kernel(own_ref, speed_ref, rim_ref, rate_ref, wrapped):
@@ -483,7 +533,7 @@
         + [(fixed_ref, 128 + FINE * row) for row in range(4)]
         + [(old_right, 0), (old_right, 64)]
     )
-    marks = [(old_left, 192)] * 2 + [(fixed_ref, 384)] * 4 + [(old_right, 192)] * 2
+    marks = [(old_left, 160)] * 2 + [(fixed_ref, 384)] * 4 + [(old_right, 160)] * 2
 
     def store(index, z, value):
         ref, at = initial[index]
@@ -543,9 +593,9 @@
 
     in_pairs(forces)
 
-    source = [older_left[224:256, :], older[256:288, :], older[288:320, :], older_right[192:224, :]]
-    once = [left_ref[192:224, :]] + [own_ref[384 + row * FLOW : 384 + (row + 1) * FLOW, :] for row in range(4)]
-    once = once + [right_ref[192:224, :]]
+    source = [sent_source(older_left, 1), older[256:288, :], older[288:320, :], sent_source(older_right, 0)]
+    once = [sent_sweep(left_ref)] + [own_ref[384 + row * FLOW : 384 + (row + 1) * FLOW, :] for row in range(4)]
+    once = once + [sent_sweep(right_ref)]
     twice = [sweep(once[row], once[row + 1], once[row + 2], source[row]) for row in range(4)]
     thrice = [sweep(twice[row], twice[row + 1], twice[row + 2], source[row + 1]) for row in range(2)]
 
@@ -638,7 +688,7 @@
     far_half = crossed(half, 1)
     fixed, up, down = call(
         assemble_kernel,
-        [(400, LANES), (208, LANES), (208, LANES)],
+        [(400, LANES), (176, LANES), (176, LANES)],
         [],
         group,
         raw,
@@ -652,7 +702,7 @@
     old_left, old_right = shifted(up, "gx", 1), shifted(down, "gx", -1)
     speeds, rates = call(inner_kernel, [speed_shape, (256, LANES)], [(4, 80, LANES)], fixed)
     own, send = call(
-        first_kernel, [(320, LANES), (256, LANES)], [(128, LANES)], fixed, old_left, old_right, speeds, rates
+        first_kernel, [(320, LANES), (224, LANES)], [(128, LANES)], fixed, old_left, old_right, speeds, rates
     )
     left, right = shifted(send, "gx", 1), shifted(send, "gx", -1)
     rim, rates = call(
@@ -660,7 +710,7 @@
     )
     newer, up, down = call(
         second_kernel,
-        [(512, LANES), (224, LANES), (224, LANES)],
+        [(512, LANES), (192, LANES), (192, LANES)],
         [(6, 80, LANES), (128, LANES)],
         own,
         left,

time: 55 us -> 54.6 us (level)
  waiting for transfers between devices: 17.1 us -> 16.5 us
    ppermute x6, waiting for transfers between devices: 6.09 us -> 5.43 us  [shifted(): lax.ppermute(value, axis, [(i, (i + shift) % count) for i in range(count)])]
  transfers between devices with their start and end apart: 12 -> 12, of which waited for: 9 -> 8; matrix products, arithmetic and copies ran while one was open for 0% -> 0% of each run, Pallas kernels for 9% -> 9%
where the time goes in v5:
time: 54.6 us; the launch traced here: 54.5 us
  starting transfers between devices  25.1 us (46%)
  waiting for transfers between devices  16.5 us (30%)
  Pallas kernels  12.8 us (23%)
    ppermute x6, starting transfers between devices, shifted(): lax.ppermute(value, axis, [(i, (i + shift) % count) for i in range(count)])  13.4 us
    pallas_call x12, Pallas kernels, call(): pl.pallas_call(kernel, out_shape=shapes if len(shapes) > 1 else shapes[0]...  12.8 us
    ppermute x5, starting transfers between devices, crossed(): lax.ppermute(value, 'grp', [(i, i ^ bit) for i in range(lax.axis_size('gr...  9.04 us
    ppermute x5, waiting for transfers between devices, crossed(): lax.ppermute(value, 'grp', [(i, i ^ bit) for i in range(lax.axis_size('gr...  6.82 us
    ppermute x6, waiting for transfers between devices, shifted(): lax.ppermute(value, axis, [(i, (i + shift) % count) for i in range(count)])  5.43 us
    ppermute x1, waiting for transfers between devices, to_next_blocks(): return lax.ppermute(value, ('grp', 'gy'), pairs)  4.19 us
    ppermute x1, starting transfers between devices, to_next_blocks(): return lax.ppermute(value, ('grp', 'gy'), pairs)  2.69 us
  transfers between devices with their start and end apart: 12, of which 8 were waited for; matrix products, arithmetic and copies ran while one was open for 0% of the time, Pallas kernels for 9%

profile of v5, /device:TPU:1, one launch (start us, length us, event | category | flops | bytes accessed | tf_op | source)
XLA Modules:
  0.0 54.5 jit_solution(6572696953666525340)
XLA Ops:
  0.0 1.3 %pack_kernel.1 = (f32[576,128]{1,0:T(8,128)S(1)}, f32[2,16,128]{2,1,0:T(8,128)S(1)}) custom-call(f32[32,2,128]{2,1,0:T(2,128)} %bitcast.6, f32[64,4,256]{2,1,0:T(4,128)} %bitcast.5, s32[8,16]{1,0:T(8,128)} %bitcast.7, s32[4,256]{1,0:T(4,128)} %nozzle_ref.1), custom_call_target="tpu_custom_call" | custom-call | tf_op jit(solution)/shard_map/pack_kernel/pallas_call | solution.py:646
  1.3 3.2 %collective-permute-start = (f32[576,128]{1,0:T(8,128)S(1)}, f32[576,128]{1,0:T(8,128)S(1)}, u32[]{:S(2)}, u32[]{:S(2)}) collective-permute-start(f32[576,128]{1,0:T(8,128)S(1)} %get-tuple-element.23.raw_ref), channel_id=1, source_target_pairs={{0,64},{64,0},{128,192},{192,128},{1,65},{65,1},{129,193},{193,129... | collective-permute-start | bytes 884744 | tf_op jit(solution)/shard_map/ppermute | solution.py:662
  4.5 1.2 %collective-permute-done.other_ref = f32[576,128]{1,0:T(8,128)S(1)} collective-permute-done((f32[576,128]{1,0:T(8,128)S(1)}, f32[576,128]{1,0:T(8,128)S(1)}, u32[]{:S(2)}, u32[]{:S(2)}) %collective-permute-start) | collective-permute-done | bytes 294944 | tf_op jit(solution)/shard_map/ppermute | solution.py:662
  5.7 0.2 split_kernel.1
  5.9 1.1 %collective-permute-start.1 = (f32[256,128]{1,0:T(8,128)S(1)}, f32[256,128]{1,0:T(8,128)S(1)}, u32[]{:S(2)}, u32[]{:S(2)}) collective-permute-start(f32[256,128]{1,0:T(8,128)S(1)} %get-tuple-element.25), channel_id=1, source_target_pairs={{0,128},{64,192},{128,0},{192,64},{1,129},{65,193},{129,1},{193,65... | collective-permute-start | bytes 393224 | tf_op jit(solution)/shard_map/ppermute | solution.py:662
  7.0 2.7 %collective-permute-start.2 = (f32[80,128]{1,0:T(8,128)S(1)}, f32[80,128]{1,0:T(8,128)S(1)}, u32[]{:S(2)}, u32[]{:S(2)}) collective-permute-start(f32[80,128]{1,0:T(8,128)S(1)} %get-tuple-element.26), channel_id=1, source_target_pairs={{0,1},{1,2},{2,3},{3,0},{64,195},{65,192},{66,193},{67,194},{128,1... | collective-permute-start | bytes 122888 | tf_op jit(solution)/shard_map/ppermute | solution.py:670
  9.7 4.2 %collective-permute-done.2.edge_ref = f32[80,128]{1,0:T(8,128)S(1)} collective-permute-done((f32[80,128]{1,0:T(8,128)S(1)}, f32[80,128]{1,0:T(8,128)S(1)}, u32[]{:S(2)}, u32[]{:S(2)}) %collective-permute-start.2) | collective-permute-done | bytes 40992 | tf_op jit(solution)/shard_map/ppermute | solution.py:670
  13.9 0.0 collective-permute-done.1.half_ref
  13.9 0.1 collective-permute-start.3
  14.0 1.4 %collective-permute-done.3.far_half_ref = f32[336,128]{1,0:T(8,128)S(1)} collective-permute-done((f32[336,128]{1,0:T(8,128)S(1)}, f32[336,128]{1,0:T(8,128)S(1)}, u32[]{:S(2)}, u32[]{:S(2)}) %collective-permute-start.3) | collective-permute-done | bytes 172064 | tf_op jit(solution)/shard_map/ppermute | solution.py:662
  15.4 0.3 assemble_kernel.1
  15.7 1.7 %collective-permute-start.4 = (f32[176,128]{1,0:T(8,128)S(1)}, f32[176,128]{1,0:T(8,128)S(1)}, u32[]{:S(2)}, u32[]{:S(2)}) collective-permute-start(f32[176,128]{1,0:T(8,128)S(1)} %get-tuple-element.28), channel_id=1, source_target_pairs={{0,4},{4,8},{8,12},{12,16},{16,20},{20,24},{24,28},{28,32},{32,36}... | collective-permute-start | bytes 270344 | tf_op jit(solution)/shard_map/ppermute | solution.py:658
  17.4 4.6 %collective-permute-start.5 = (f32[176,128]{1,0:T(8,128)S(1)}, f32[176,128]{1,0:T(8,128)S(1)}, u32[]{:S(2)}, u32[]{:S(2)}) collective-permute-start(f32[176,128]{1,0:T(8,128)S(1)} %get-tuple-element.29), channel_id=1, source_target_pairs={{0,60},{4,0},{8,4},{12,8},{16,12},{20,16},{24,20},{28,24},{32,28},... | collective-permute-start | bytes 270344 | tf_op jit(solution)/shard_map/ppermute | solution.py:658
  22.0 1.8 %inner_kernel.1 = (f32[3,2,64,128]{3,2,1,0:T(8,128)S(1)}, f32[256,128]{1,0:T(8,128)S(1)}) custom-call(f32[400,128]{1,0:T(8,128)S(1)} %get-tuple-element.27.fixed_ref), custom_call_target="tpu_custom_call" | custom-call | tf_op jit(solution)/shard_map/inner_kernel/pallas_call | solution.py:646
  23.8 1.0 %collective-permute-done.4.left_ref.old_left = f32[176,128]{1,0:T(8,128)S(1)} collective-permute-done((f32[176,128]{1,0:T(8,128)S(1)}, f32[176,128]{1,0:T(8,128)S(1)}, u32[]{:S(2)}, u32[]{:S(2)}) %collective-permute-start.4) | collective-permute-done | bytes 90144 | tf_op jit(solution)/shard_map/ppermute | solution.py:658
  24.8 0.7 %first_kernel.1 = (f32[320,128]{1,0:T(8,128)S(1)}, f32[224,128]{1,0:T(8,128)S(1)}) custom-call(f32[400,128]{1,0:T(8,128)S(1)} %get-tuple-element.27.fixed_ref, f32[176,128]{1,0:T(8,128)S(1)} %collective-permute-done.4.left_ref.old_left, f32[176,128]{1,0:T(8,128)S(1)} %collective-permute-done.5.right_ref.old_right, ...), custom_call_target="tpu_custom_call" | custom-call | tf_op jit(solution)/shard_map/first_kernel/pallas_call | solution.py:646
  25.6 3.5 %collective-permute-start.7 = (f32[224,128]{1,0:T(8,128)S(1)}, f32[224,128]{1,0:T(8,128)S(1)}, u32[]{:S(2)}, u32[]{:S(2)}) collective-permute-start(f32[224,128]{1,0:T(8,128)S(1)} %get-tuple-element.33), channel_id=1, source_target_pairs={{0,60},{4,0},{8,4},{12,8},{16,12},{20,16},{24,20},{28,24},{32,28},... | collective-permute-start | bytes 344072 | tf_op jit(solution)/shard_map/ppermute | solution.py:658
  29.0 1.8 %middle_kernel.1 = (f32[3,2,64,128]{3,2,1,0:T(8,128)S(1)}, f32[256,128]{1,0:T(8,128)S(1)}) custom-call(f32[320,128]{1,0:T(8,128)S(1)} %get-tuple-element.32.own_ref.older, f32[176,128]{1,0:T(8,128)S(1)} %collective-permute-done.4.left_ref.old_left, f32[176,128]{1,0:T(8,128)S(1)} %collective-permute-done.5.right_ref.old_right, ...), custom_call_target="tpu_custom_call" | custom-call | tf_op jit(solution)/shard_map/middle_kernel/pallas_call | solution.py:646
  30.8 0.0 collective-permute-done.7.right_ref.older_right
  30.8 4.0 %collective-permute-done.6.left_ref.older_left = f32[224,128]{1,0:T(8,128)S(1)} collective-permute-done((f32[224,128]{1,0:T(8,128)S(1)}, f32[224,128]{1,0:T(8,128)S(1)}, u32[]{:S(2)}, u32[]{:S(2)}) %collective-permute-start.6) | collective-permute-done | bytes 114720 | tf_op jit(solution)/shard_map/ppermute | solution.py:658
  34.8 1.7 %second_kernel.1 = (f32[512,128]{1,0:T(8,128)S(1)}, f32[192,128]{1,0:T(8,128)S(1)}, f32[192,128]{1,0:T(8,128)S(1)}) custom-call(f32[320,128]{1,0:T(8,128)S(1)} %get-tuple-element.32.own_ref.older, f32[224,128]{1,0:T(8,128)S(1)} %collective-permute-done.6.left_ref.older_left, f32[224,128]{1,0:T(8,128)S(1)} %collective-permute-done.7.right_ref.older_right, ...), custom_call_target="tpu_custom_call" | custom-call | tf_op jit(solution)/shard_map/second_kernel/pallas_call | solution.py:646
  36.5 0.1 collective-permute-start.8
  36.6 3.6 %collective-permute-start.9 = (f32[192,128]{1,0:T(8,128)S(1)}, f32[192,128]{1,0:T(8,128)S(1)}, u32[]{:S(2)}, u32[]{:S(2)}) collective-permute-start(f32[192,128]{1,0:T(8,128)S(1)} %get-tuple-element.38), channel_id=1, source_target_pairs={{0,60},{4,0},{8,4},{12,8},{16,12},{20,16},{24,20},{28,24},{32,28},... | collective-permute-start | bytes 294920 | tf_op jit(solution)/shard_map/ppermute | solution.py:658
  40.2 1.6 %late_kernel.1.rate_ref = f32[384,128]{1,0:T(8,128)S(1)} custom-call(f32[512,128]{1,0:T(8,128)S(1)} %get-tuple-element.36.own_ref, f32[3,2,64,128]{3,2,1,0:T(8,128)S(1)} %get-tuple-element.30.speed_ref, f32[3,2,64,128]{3,2,1,0:T(8,128)S(1)} %get-tuple-element.34.rim_ref), custom_call_target="tpu_custom_call" | custom-call | tf_op jit(solution)/shard_map/late_kernel/pallas_call | solution.py:646
  41.8 0.4 collective-permute-done.8.left_ref
  42.2 2.7 %third_kernel.1.own_ref = f32[64,128]{1,0:T(8,128)S(1)} custom-call(f32[512,128]{1,0:T(8,128)S(1)} %get-tuple-element.36.own_ref, f32[192,128]{1,0:T(8,128)S(1)} %collective-permute-done.8.left_ref, f32[192,128]{1,0:T(8,128)S(1)} %collective-permute-done.9.right_ref, f32[320,128]{1,0:T(8,128)S(1)} %get-tuple-element.32.own_ref.older, ...), custom_call_target="tpu_custom_call" | custom-call | tf_op jit(solution)/shard_map/third_kernel/pallas_call | solution.py:646
  44.9 3.6 %collective-permute-start.10 = (f32[64,128]{1,0:T(8,128)S(1)}, f32[64,128]{1,0:T(8,128)S(1)}, u32[]{:S(2)}, u32[]{:S(2)}) collective-permute-start(f32[64,128]{1,0:T(8,128)S(1)} %third_kernel.1.own_ref), channel_id=1, source_target_pairs={{0,64},{64,0},{128,192},{192,128},{1,65},{65,1},{129,193},{193,129... | collective-permute-start | bytes 98312 | tf_op jit(solution)/shard_map/ppermute | solution.py:662
  48.5 0.9 %collective-permute-done.10.other_ref = f32[64,128]{1,0:T(8,128)S(1)} collective-permute-done((f32[64,128]{1,0:T(8,128)S(1)}, f32[64,128]{1,0:T(8,128)S(1)}, u32[]{:S(2)}, u32[]{:S(2)}) %collective-permute-start.10) | collective-permute-done | bytes 32800 | tf_op jit(solution)/shard_map/ppermute | solution.py:662
  49.4 0.1 sort_kernel.1
  49.5 1.0 %collective-permute-start.11 = (f32[64,128]{1,0:T(8,128)S(1)}, f32[64,128]{1,0:T(8,128)S(1)}, u32[]{:S(2)}, u32[]{:S(2)}) collective-permute-start(f32[64,128]{1,0:T(8,128)S(1)} %get-tuple-element.40), channel_id=1, source_target_pairs={{0,128},{64,192},{128,0},{192,64},{1,129},{65,193},{129,1},{193,65... | collective-permute-start | bytes 98312 | tf_op jit(solution)/shard_map/ppermute | solution.py:662
  50.5 3.4 %collective-permute-done.11.far_ref = f32[64,128]{1,0:T(8,128)S(1)} collective-permute-done((f32[64,128]{1,0:T(8,128)S(1)}, f32[64,128]{1,0:T(8,128)S(1)}, u32[]{:S(2)}, u32[]{:S(2)}) %collective-permute-start.11) | collective-permute-done | bytes 32800 | tf_op jit(solution)/shard_map/ppermute | solution.py:662
  53.8 0.6 %merge_kernel.1 = f32[32,2,128]{2,1,0:T(2,128)} custom-call(s32[1]{0:T(128)} %bitcast.group_ref, f32[64,128]{1,0:T(8,128)S(1)} %get-tuple-element.39.keep_ref, f32[64,128]{1,0:T(8,128)S(1)} %collective-permute-done.11.far_ref), custom_call_target="tpu_custom_call" | custom-call | tf_op jit(solution)/shard_map/merge_kernel/pallas_call | solution.py:646
  (4 shorter events, 0.0 us)
Async XLA Ops:
  1.3 4.4 %collective-permute-start = (f32[576,128]{1,0:T(8,128)S(1)}, f32[576,128]{1,0:T(8,128)S(1)}, u32[]{:S(2)}, u32[]{:S(2)}) collective-permute-start(f32[576,128]{1,0:T(8,128)S(1)} %get-tuple-element.23.raw_ref), channel_id=1, source_target_pairs={{0,64},{64,0},{128,192},{192,128},{1,65},{65,1},{129,193},{193,129... | collective-permute-start | bytes 884744 | tf_op jit(solution)/shard_map/ppermute | solution.py:662
  5.9 8.0 %collective-permute-start.1 = (f32[256,128]{1,0:T(8,128)S(1)}, f32[256,128]{1,0:T(8,128)S(1)}, u32[]{:S(2)}, u32[]{:S(2)}) collective-permute-start(f32[256,128]{1,0:T(8,128)S(1)} %get-tuple-element.25), channel_id=1, source_target_pairs={{0,128},{64,192},{128,0},{192,64},{1,129},{65,193},{129,1},{193,65... | collective-permute-start | bytes 393224 | tf_op jit(solution)/shard_map/ppermute | solution.py:662
  7.0 6.9 %collective-permute-start.2 = (f32[80,128]{1,0:T(8,128)S(1)}, f32[80,128]{1,0:T(8,128)S(1)}, u32[]{:S(2)}, u32[]{:S(2)}) collective-permute-start(f32[80,128]{1,0:T(8,128)S(1)} %get-tuple-element.26), channel_id=1, source_target_pairs={{0,1},{1,2},{2,3},{3,0},{64,195},{65,192},{66,193},{67,194},{128,1... | collective-permute-start | bytes 122888 | tf_op jit(solution)/shard_map/ppermute | solution.py:670
  13.9 1.5 %collective-permute-start.3 = (f32[336,128]{1,0:T(8,128)S(1)}, f32[336,128]{1,0:T(8,128)S(1)}, u32[]{:S(2)}, u32[]{:S(2)}) collective-permute-start(f32[336,128]{1,0:T(8,128)S(1)} %join_kernel.1.half_ref), channel_id=1, source_target_pairs={{0,64},{64,0},{128,192},{192,128},{1,65},{65,1},{129,193},{193,129... | collective-permute-start | bytes 516104 | tf_op jit(solution)/shard_map/ppermute | solution.py:662
  15.7 9.1 %collective-permute-start.4 = (f32[176,128]{1,0:T(8,128)S(1)}, f32[176,128]{1,0:T(8,128)S(1)}, u32[]{:S(2)}, u32[]{:S(2)}) collective-permute-start(f32[176,128]{1,0:T(8,128)S(1)} %get-tuple-element.28), channel_id=1, source_target_pairs={{0,4},{4,8},{8,12},{12,16},{16,20},{20,24},{24,28},{28,32},{32,36}... | collective-permute-start | bytes 270344 | tf_op jit(solution)/shard_map/ppermute | solution.py:658
  17.4 7.4 %collective-permute-start.5 = (f32[176,128]{1,0:T(8,128)S(1)}, f32[176,128]{1,0:T(8,128)S(1)}, u32[]{:S(2)}, u32[]{:S(2)}) collective-permute-start(f32[176,128]{1,0:T(8,128)S(1)} %get-tuple-element.29), channel_id=1, source_target_pairs={{0,60},{4,0},{8,4},{12,8},{16,12},{20,16},{24,20},{28,24},{32,28},... | collective-permute-start | bytes 270344 | tf_op jit(solution)/shard_map/ppermute | solution.py:658
  25.6 5.2 %collective-permute-start.7 = (f32[224,128]{1,0:T(8,128)S(1)}, f32[224,128]{1,0:T(8,128)S(1)}, u32[]{:S(2)}, u32[]{:S(2)}) collective-permute-start(f32[224,128]{1,0:T(8,128)S(1)} %get-tuple-element.33), channel_id=1, source_target_pairs={{0,60},{4,0},{8,4},{12,8},{16,12},{20,16},{24,20},{28,24},{32,28},... | collective-permute-start | bytes 344072 | tf_op jit(solution)/shard_map/ppermute | solution.py:658
  29.0 5.8 %collective-permute-start.6 = (f32[224,128]{1,0:T(8,128)S(1)}, f32[224,128]{1,0:T(8,128)S(1)}, u32[]{:S(2)}, u32[]{:S(2)}) collective-permute-start(f32[224,128]{1,0:T(8,128)S(1)} %get-tuple-element.33), channel_id=1, source_target_pairs={{0,4},{4,8},{8,12},{12,16},{16,20},{20,24},{24,28},{28,32},{32,36}... | collective-permute-start | bytes 344072 | tf_op jit(solution)/shard_map/ppermute | solution.py:658
  36.5 5.7 %collective-permute-start.8 = (f32[192,128]{1,0:T(8,128)S(1)}, f32[192,128]{1,0:T(8,128)S(1)}, u32[]{:S(2)}, u32[]{:S(2)}) collective-permute-start(f32[192,128]{1,0:T(8,128)S(1)} %get-tuple-element.37), channel_id=1, source_target_pairs={{0,4},{4,8},{8,12},{12,16},{16,20},{20,24},{24,28},{28,32},{32,36}... | collective-permute-start | bytes 294920 | tf_op jit(solution)/shard_map/ppermute | solution.py:658
  36.6 5.6 %collective-permute-start.9 = (f32[192,128]{1,0:T(8,128)S(1)}, f32[192,128]{1,0:T(8,128)S(1)}, u32[]{:S(2)}, u32[]{:S(2)}) collective-permute-start(f32[192,128]{1,0:T(8,128)S(1)} %get-tuple-element.38), channel_id=1, source_target_pairs={{0,60},{4,0},{8,4},{12,8},{16,12},{20,16},{24,20},{28,24},{32,28},... | collective-permute-start | bytes 294920 | tf_op jit(solution)/shard_map/ppermute | solution.py:658
  44.9 4.5 %collective-permute-start.10 = (f32[64,128]{1,0:T(8,128)S(1)}, f32[64,128]{1,0:T(8,128)S(1)}, u32[]{:S(2)}, u32[]{:S(2)}) collective-permute-start(f32[64,128]{1,0:T(8,128)S(1)} %third_kernel.1.own_ref), channel_id=1, source_target_pairs={{0,64},{64,0},{128,192},{192,128},{1,65},{65,1},{129,193},{193,129... | collective-permute-start | bytes 98312 | tf_op jit(solution)/shard_map/ppermute | solution.py:662
  49.5 4.4 %collective-permute-start.11 = (f32[64,128]{1,0:T(8,128)S(1)}, f32[64,128]{1,0:T(8,128)S(1)}, u32[]{:S(2)}, u32[]{:S(2)}) collective-permute-start(f32[64,128]{1,0:T(8,128)S(1)} %get-tuple-element.40), channel_id=1, source_target_pairs={{0,128},{64,192},{128,0},{192,64},{1,129},{65,193},{129,1},{193,65... | collective-permute-start | bytes 98312 | tf_op jit(solution)/shard_map/ppermute | solution.py:662

commit v6 on v5

--- a/solution.py
+++ b/solution.py
@@ -92,6 +92,20 @@
     )
 
 
+def by_side(place_ref, first_ref, second_ref, left_ref, right_ref):
+    odd = place_ref[0] % 2 == 1
+
+    @pl.when(odd)
+    def _():
+        left_ref[...] = first_ref[...]
+        right_ref[...] = second_ref[...]
+
+    @pl.when(jnp.logical_not(odd))
+    def _():
+        left_ref[...] = second_ref[...]
+        right_ref[...] = first_ref[...]
+
+
 def pack_kernel(flow_ref, level_ref, band_ref, nozzle_ref, raw_ref, mark_ref):
     for row in range(2):
         raw_ref[row * FLOW : (row + 1) * FLOW, :] = flow_ref[:, row, :]
@@ -162,7 +176,8 @@
 
 
 def assemble_kernel(
-    group_ref, raw_ref, other_ref, mark_ref, half_ref, far_half_ref, fixed_ref, up_ref, down_ref
+    group_ref, place_ref, raw_ref, other_ref, mark_ref, half_ref, far_half_ref,
+    fixed_ref, first_ref, second_ref, up_ref, down_ref,
 ):
     group = group_ref[0]
     lanes = lane_ids(64)
@@ -230,6 +245,8 @@
         def _(own=own):
             assemble(own)
 
+    by_side(place_ref, down_ref, up_ref, first_ref, second_ref)
+
 
 def bent(below, here, above):
     return (above - here) - (here - below)
@@ -411,7 +428,10 @@
     across_rows(places, speed_loader(speed_ref, None, 0), wrapped, rate_ref)
 
 
-def first_kernel(fixed_ref, left_ref, right_ref, speed_ref, rate_ref, out_ref, send_ref, spare):
+def first_kernel(
+    place_ref, fixed_ref, one_ref, two_ref, speed_ref, rate_ref, out_ref, send_ref, left_ref, right_ref, spare
+):
+    by_side(place_ref, one_ref, two_ref, left_ref, right_ref)
     moving = [
         left_ref[128:160, :],
         fixed_ref[0:32, :],
@@ -474,12 +494,14 @@
 
 
 def second_kernel(
-    own_ref, left_ref, right_ref, fixed_ref, old_left, old_right, speed_ref, rim_ref, rate_ref,
-    out_ref, up_ref, down_ref, wrapped, spare,
+    place_ref, own_ref, one_ref, two_ref, fixed_ref, old_left, old_right, speed_ref, rim_ref, rate_ref,
+    out_ref, first_ref, second_ref, wrapped, spare, left_ref, right_ref, up_ref, down_ref,
 ):
+    by_side(place_ref, one_ref, two_ref, left_ref, right_ref)
     source = [sent_source(left_ref, row) for row in range(2)]
     source += [own_ref[256 + row * FLOW : 256 + (row + 1) * FLOW, :] for row in range(2)]
     source += [sent_source(right_ref, row) for row in range(2)]
+    out_ref[512:544, :], out_ref[544:576, :] = source[1], source[4]
     for row in range(4):
         done = sweep(source[row], source[row + 1], source[row + 2], source[row + 1])
         out_ref[384 + row * FLOW : 384 + (row + 1) * FLOW, :] = done
@@ -507,6 +529,7 @@
         to_ref[96:128, :] = lay(done, beside[32:64, :], 8, 16, 24)
         to_ref[128:160, :] = lay(done, out_ref[at + 128 : at + 160, :], 104, 152, 104)
         to_ref[160:192, :] = lay(done, out_ref[at + 160 : at + 192, :], 104, 152, 56)
+    by_side(place_ref, down_ref, up_ref, first_ref, second_ref)
 
 
 def late_kernel(own_ref, speed_ref, rim_ref, rate_ref, wrapped):
@@ -515,10 +538,11 @@
 
 
 def third_kernel(
-    own_ref, left_ref, right_ref, older, older_left, older_right, fixed_ref, old_left, old_right,
+    place_ref, own_ref, one_ref, two_ref, older, fixed_ref, old_left, old_right,
     speed_ref, rim_ref, rate_ref,
-    out_ref, wrapped, shaped, normal_x, normal_z, summed, spare,
+    out_ref, wrapped, shaped, normal_x, normal_z, summed, spare, left_ref, right_ref,
 ):
+    by_side(place_ref, one_ref, two_ref, left_ref, right_ref)
     spare[0:64, :] = unfolded(left_ref[0:64, :], left_ref[64:128, :])
     spare[64:128, :] = unfolded(right_ref[0:64, :], right_ref[64:128, :])
     places = (
@@ -593,7 +617,7 @@
 
     in_pairs(forces)
 
-    source = [sent_source(older_left, 1), older[256:288, :], older[288:320, :], sent_source(older_right, 0)]
+    source = [own_ref[512:544, :], older[256:288, :], older[288:320, :], own_ref[544:576, :]]
     once = [sent_sweep(left_ref)] + [own_ref[384 + row * FLOW : 384 + (row + 1) * FLOW, :] for row in range(4)]
     once = once + [sent_sweep(right_ref)]
     twice = [sweep(once[row], once[row + 1], once[row + 2], source[row]) for row in range(4)]
@@ -649,13 +673,16 @@
         in_specs=[smem] * scalars + [vmem] * len(held),
         out_specs=[vmem] * len(shapes) if len(shapes) > 1 else vmem,
         scratch_shapes=[pltpu.VMEM(shape, F32) for shape in scratch],
-        name=kernel.__name__,
     )(*args[:scalars], *held)
 
 
-def shifted(value, axis, shift):
-    count = lax.axis_size(axis)
-    return lax.ppermute(value, axis, [(i, (i + shift) % count) for i in range(count)])
+def swapped(first, second):
+    count = lax.axis_size("gx")
+    near = [(i, i ^ 1) for i in range(count)]
+    far = [(i, (i + (1 if i % 2 else -1)) % count) for i in range(count)]
+    first = lax.ppermute(first, "gx", near)
+    second = lax.ppermute(second, "gx", far)
+    return first, second
 
 
 def crossed(value, bit):
@@ -672,6 +699,7 @@
 
 def on_device(flow_fields, level_set, band_tiles, nozzle_phase):
     group = lax.axis_index("grp").astype(jnp.int32)[None]
+    place = lax.axis_index("gx").astype(jnp.int32)[None]
     raw, marks = call(
         pack_kernel,
         [(LEVEL + 8 * FINE, LANES), (2, 16, LANES)],
@@ -686,60 +714,81 @@
     half, edge = call(split_kernel, [(256, LANES), (80, LANES)], [], group, raw, other, marks, scalars=1)
     half = call(join_kernel, [(336, LANES)], [], crossed(half, 2), to_next_blocks(edge))
     far_half = crossed(half, 1)
-    fixed, up, down = call(
+    fixed, first, second = call(
         assemble_kernel,
         [(400, LANES), (176, LANES), (176, LANES)],
-        [],
+        [(176, LANES), (176, LANES)],
         group,
+        place,
         raw,
         other,
         marks,
         half,
         far_half,
+        scalars=2,
+    )
+    speed_shape = (3, 2, FINE, LANES)
+    first, second = swapped(first, second)
+    speeds, rates = call(inner_kernel, [speed_shape, (256, LANES)], [(4, 80, LANES)], fixed)
+    own, send, old_left, old_right = call(
+        first_kernel,
+        [(320, LANES), (224, LANES), (176, LANES), (176, LANES)],
+        [(128, LANES)],
+        place,
+        fixed,
+        first,
+        second,
+        speeds,
+        rates,
         scalars=1,
     )
-    speed_shape = (3, 2, FINE, LANES)
-    old_left, old_right = shifted(up, "gx", 1), shifted(down, "gx", -1)
-    speeds, rates = call(inner_kernel, [speed_shape, (256, LANES)], [(4, 80, LANES)], fixed)
-    own, send = call(
-        first_kernel, [(320, LANES), (224, LANES)], [(128, LANES)], fixed, old_left, old_right, speeds, rates
-    )
-    left, right = shifted(send, "gx", 1), shifted(send, "gx", -1)
+    first, second = swapped(send, send)
     rim, rates = call(
         middle_kernel, [speed_shape, (256, LANES)], [(4, 80, LANES)], own, old_left, old_right, speeds
     )
-    newer, up, down = call(
+    newer, first, second = call(
         second_kernel,
-        [(512, LANES), (192, LANES), (192, LANES)],
-        [(6, 80, LANES), (128, LANES)],
+        [(576, LANES), (192, LANES), (192, LANES)],
+        [(6, 80, LANES), (128, LANES), (224, LANES), (224, LANES), (192, LANES), (192, LANES)],
+        place,
         own,
-        left,
-        right,
+        first,
+        second,
         fixed,
         old_left,
         old_right,
         speeds,
         rim,
         rates,
-    )
-    newer_left, newer_right = shifted(up, "gx", 1), shifted(down, "gx", -1)
+        scalars=1,
+    )
+    first, second = swapped(first, second)
     rates = call(late_kernel, [(384, LANES)], [(6, 80, LANES)], newer, speeds, rim)
     result = call(
         third_kernel,
         [(64, LANES)],
-        [(8, 80, LANES), (8, 80, LANES), (6, FINE, LANES), (4, 80, LANES), (4, 2 * FINE, LANES), (128, LANES)],
+        [
+            (8, 80, LANES),
+            (8, 80, LANES),
+            (6, FINE, LANES),
+            (4, 80, LANES),
+            (4, 2 * FINE, LANES),
+            (128, LANES),
+            (192, LANES),
+            (192, LANES),
+        ],
+        place,
         newer,
-        newer_left,
-        newer_right,
+        first,
+        second,
         own,
-        left,
-        right,
         fixed,
         old_left,
         old_right,
         speeds,
         rim,
         rates,
+        scalars=1,
     )
     keep, send = call(
         sort_kernel, [(64, LANES), (64, LANES)], [], group, result, crossed(result, 1), scalars=1

time: 54.6 us -> 53.3 us (0.976)
  starting transfers between devices: 25.1 us -> 24 us
    ppermute x6, starting transfers between devices: 13.4 us -> 12.3 us  [the longest x3 10.5 us: swapped(): second = lax.ppermute(second, 'gx', far)]
  transfers between devices with their start and end apart: 12 -> 12, of which waited for: 8 -> 9; matrix products, arithmetic and copies ran while one was open for 0% -> 0% of each run, Pallas kernels for 9% -> 10%
where the time goes in v6:
time: 53.3 us; the launch traced here: 53.2 us
  starting transfers between devices  24 us (45%)
  waiting for transfers between devices  16.2 us (30%)
  Pallas kernels  12.9 us (24%)
    pallas_call x12, Pallas kernels, call(): pl.pallas_call(kernel, out_shape=shapes if len(shapes) > 1 else shapes[0]...  12.9 us
    ppermute x3, starting transfers between devices, swapped(): second = lax.ppermute(second, 'gx', far)  10.5 us
    ppermute x5, starting transfers between devices, crossed(): lax.ppermute(value, 'grp', [(i, i ^ bit) for i in range(lax.axis_size('gr...  9.04 us
    ppermute x5, waiting for transfers between devices, crossed(): lax.ppermute(value, 'grp', [(i, i ^ bit) for i in range(lax.axis_size('gr...  6.82 us
    ppermute x1, waiting for transfers between devices, to_next_blocks(): return lax.ppermute(value, ('grp', 'gy'), pairs)  4.19 us
    ppermute x3, waiting for transfers between devices, swapped(): second = lax.ppermute(second, 'gx', far)  3.69 us
    ppermute x1, starting transfers between devices, to_next_blocks(): return lax.ppermute(value, ('grp', 'gy'), pairs)  2.69 us
    ppermute x3, starting transfers between devices, swapped(): first = lax.ppermute(first, 'gx', near)  1.82 us
  transfers between devices with their start and end apart: 12, of which 9 were waited for; matrix products, arithmetic and copies ran while one was open for 0% of the time, Pallas kernels for 10%

profile of v6, /device:TPU:1, one launch (start us, length us, event | category | flops | bytes accessed | tf_op | source)
XLA Modules:
  0.0 53.2 jit_solution(6329439920588637188)
XLA Ops:
  0.0 1.3 %shard_map.46 = (f32[576,128]{1,0:T(8,128)S(1)}, f32[2,16,128]{2,1,0:T(8,128)S(1)}) custom-call(f32[32,2,128]{2,1,0:T(2,128)} %bitcast.7, f32[64,4,256]{2,1,0:T(4,128)} %bitcast.6, s32[8,16]{1,0:T(8,128)} %bitcast.8, s32[4,256]{1,0:T(4,128)} %nozzle_ref.1), custom_call_target="tpu_custom_call" | custom-call | tf_op jit(solution)/shard_map/pallas_call | solution.py:670
  1.3 3.2 %collective-permute-start = (f32[576,128]{1,0:T(8,128)S(1)}, f32[576,128]{1,0:T(8,128)S(1)}, u32[]{:S(2)}, u32[]{:S(2)}) collective-permute-start(f32[576,128]{1,0:T(8,128)S(1)} %get-tuple-element.25.raw_ref), channel_id=1, source_target_pairs={{0,64},{64,0},{128,192},{192,128},{1,65},{65,1},{129,193},{193,129... | collective-permute-start | bytes 884744 | tf_op jit(solution)/shard_map/ppermute | solution.py:689
  4.5 1.2 %collective-permute-done.other_ref = f32[576,128]{1,0:T(8,128)S(1)} collective-permute-done((f32[576,128]{1,0:T(8,128)S(1)}, f32[576,128]{1,0:T(8,128)S(1)}, u32[]{:S(2)}, u32[]{:S(2)}) %collective-permute-start) | collective-permute-done | bytes 294944 | tf_op jit(solution)/shard_map/ppermute | solution.py:689
  5.7 0.2 shard_map.47
  5.9 1.1 %collective-permute-start.1 = (f32[256,128]{1,0:T(8,128)S(1)}, f32[256,128]{1,0:T(8,128)S(1)}, u32[]{:S(2)}, u32[]{:S(2)}) collective-permute-start(f32[256,128]{1,0:T(8,128)S(1)} %get-tuple-element.27), channel_id=1, source_target_pairs={{0,128},{64,192},{128,0},{192,64},{1,129},{65,193},{129,1},{193,65... | collective-permute-start | bytes 393224 | tf_op jit(solution)/shard_map/ppermute | solution.py:689
  7.0 2.7 %collective-permute-start.2 = (f32[80,128]{1,0:T(8,128)S(1)}, f32[80,128]{1,0:T(8,128)S(1)}, u32[]{:S(2)}, u32[]{:S(2)}) collective-permute-start(f32[80,128]{1,0:T(8,128)S(1)} %get-tuple-element.28), channel_id=1, source_target_pairs={{0,1},{1,2},{2,3},{3,0},{64,195},{65,192},{66,193},{67,194},{128,1... | collective-permute-start | bytes 122888 | tf_op jit(solution)/shard_map/ppermute | solution.py:697
  9.7 4.2 %collective-permute-done.2.edge_ref = f32[80,128]{1,0:T(8,128)S(1)} collective-permute-done((f32[80,128]{1,0:T(8,128)S(1)}, f32[80,128]{1,0:T(8,128)S(1)}, u32[]{:S(2)}, u32[]{:S(2)}) %collective-permute-start.2) | collective-permute-done | bytes 40992 | tf_op jit(solution)/shard_map/ppermute | solution.py:697
  13.9 0.0 collective-permute-done.1.half_ref
  13.9 0.1 collective-permute-start.3
  14.0 1.4 %collective-permute-done.3.far_half_ref = f32[336,128]{1,0:T(8,128)S(1)} collective-permute-done((f32[336,128]{1,0:T(8,128)S(1)}, f32[336,128]{1,0:T(8,128)S(1)}, u32[]{:S(2)}, u32[]{:S(2)}) %collective-permute-start.3) | collective-permute-done | bytes 172064 | tf_op jit(solution)/shard_map/ppermute | solution.py:689
  15.4 0.4 shard_map.49
  15.8 1.7 %collective-permute-start.4 = (f32[176,128]{1,0:T(8,128)S(1)}, f32[176,128]{1,0:T(8,128)S(1)}, u32[]{:S(2)}, u32[]{:S(2)}) collective-permute-start(f32[176,128]{1,0:T(8,128)S(1)} %get-tuple-element.30), channel_id=1, source_target_pairs={{0,4},{4,0},{8,12},{12,8},{16,20},{20,16},{24,28},{28,24},{32,36},... | collective-permute-start | bytes 270344 | tf_op jit(solution)/shard_map/ppermute | solution.py:683
  17.5 5.2 %collective-permute-start.5 = (f32[176,128]{1,0:T(8,128)S(1)}, f32[176,128]{1,0:T(8,128)S(1)}, u32[]{:S(2)}, u32[]{:S(2)}) collective-permute-start(f32[176,128]{1,0:T(8,128)S(1)} %get-tuple-element.31), channel_id=1, source_target_pairs={{0,60},{4,8},{8,4},{12,16},{16,12},{20,24},{24,20},{28,32},{32,28}... | collective-permute-start | bytes 270344 | tf_op jit(solution)/shard_map/ppermute | solution.py:684
  22.7 1.8 %shard_map.50 = (f32[3,2,64,128]{3,2,1,0:T(8,128)S(1)}, f32[256,128]{1,0:T(8,128)S(1)}) custom-call(f32[400,128]{1,0:T(8,128)S(1)} %get-tuple-element.29.fixed_ref), custom_call_target="tpu_custom_call" | custom-call | tf_op jit(solution)/shard_map/pallas_call | solution.py:670
  24.5 0.8 %collective-permute-done.5.two_ref = f32[176,128]{1,0:T(8,128)S(1)} collective-permute-done((f32[176,128]{1,0:T(8,128)S(1)}, f32[176,128]{1,0:T(8,128)S(1)}, u32[]{:S(2)}, u32[]{:S(2)}) %collective-permute-start.5) | collective-permute-done | bytes 90144 | tf_op jit(solution)/shard_map/ppermute | solution.py:684
  25.3 0.7 %shard_map.51 = (f32[320,128]{1,0:T(8,128)S(1)}, f32[224,128]{1,0:T(8,128)S(1)}, f32[176,128]{1,0:T(8,128)S(1)}, f32[176,128]{1,0:T(8,128)S(1)}) custom-call(s32[1]{0:T(128)} %bitcast.1.place_ref, f32[400,128]{1,0:T(8,128)S(1)} %get-tuple-element.29.fixed_ref, f32[176,128]{1,0:T(8,128)S(1)} %collective-permute-done.4.one_ref, ...), custom_call_target="tpu_custom_call" | custom-call | tf_op jit(solution)/shard_map/pallas_call | solution.py:670
  26.1 3.4 %collective-permute-start.7 = (f32[224,128]{1,0:T(8,128)S(1)}, f32[224,128]{1,0:T(8,128)S(1)}, u32[]{:S(2)}, u32[]{:S(2)}) collective-permute-start(f32[224,128]{1,0:T(8,128)S(1)} %get-tuple-element.35), channel_id=1, source_target_pairs={{0,60},{4,8},{8,4},{12,16},{16,12},{20,24},{24,20},{28,32},{32,28}... | collective-permute-start | bytes 344072 | tf_op jit(solution)/shard_map/ppermute | solution.py:684
  29.4 1.8 %shard_map.52 = (f32[3,2,64,128]{3,2,1,0:T(8,128)S(1)}, f32[256,128]{1,0:T(8,128)S(1)}) custom-call(f32[320,128]{1,0:T(8,128)S(1)} %get-tuple-element.34.own_ref.older, f32[176,128]{1,0:T(8,128)S(1)} %get-tuple-element.36.old_left, f32[176,128]{1,0:T(8,128)S(1)} %get-tuple-element.37.old_right, f32[3,2,64,128]{3,2,1,0:T(8,128)S(1)} %get-tuple-element.32.speed_ref), custom_call_target="tpu_custom_call" | custom-call | tf_op jit(solution)/shard_map/pallas_call | solution.py:670
  31.2 0.7 %collective-permute-done.7.two_ref = f32[224,128]{1,0:T(8,128)S(1)} collective-permute-done((f32[224,128]{1,0:T(8,128)S(1)}, f32[224,128]{1,0:T(8,128)S(1)}, u32[]{:S(2)}, u32[]{:S(2)}) %collective-permute-start.7) | collective-permute-done | bytes 114720 | tf_op jit(solution)/shard_map/ppermute | solution.py:684
  31.9 1.5 %collective-permute-done.6.one_ref = f32[224,128]{1,0:T(8,128)S(1)} collective-permute-done((f32[224,128]{1,0:T(8,128)S(1)}, f32[224,128]{1,0:T(8,128)S(1)}, u32[]{:S(2)}, u32[]{:S(2)}) %collective-permute-start.6) | collective-permute-done | bytes 114720 | tf_op jit(solution)/shard_map/ppermute | solution.py:683
  33.4 1.8 %shard_map.53 = (f32[576,128]{1,0:T(8,128)S(1)}, f32[192,128]{1,0:T(8,128)S(1)}, f32[192,128]{1,0:T(8,128)S(1)}) custom-call(s32[1]{0:T(128)} %bitcast.1.place_ref, f32[320,128]{1,0:T(8,128)S(1)} %get-tuple-element.34.own_ref.older, f32[224,128]{1,0:T(8,128)S(1)} %collective-permute-done.6.one_ref, f32[224,128]{1,0:T(8,128)S(1)} %collective-permute-done.7.two_ref, ...), custom_call_target="tpu_custom_call" | custom-call | tf_op jit(solution)/shard_map/pallas_call | solution.py:670
  35.2 0.1 collective-permute-start.8
  35.3 1.9 %collective-permute-start.9 = (f32[192,128]{1,0:T(8,128)S(1)}, f32[192,128]{1,0:T(8,128)S(1)}, u32[]{:S(2)}, u32[]{:S(2)}) collective-permute-start(f32[192,128]{1,0:T(8,128)S(1)} %get-tuple-element.42), channel_id=1, source_target_pairs={{0,60},{4,8},{8,4},{12,16},{16,12},{20,24},{24,20},{28,32},{32,28}... | collective-permute-start | bytes 294920 | tf_op jit(solution)/shard_map/ppermute | solution.py:684
  37.2 1.6 %shard_map.54.rate_ref = f32[384,128]{1,0:T(8,128)S(1)} custom-call(f32[576,128]{1,0:T(8,128)S(1)} %get-tuple-element.40.own_ref, f32[3,2,64,128]{3,2,1,0:T(8,128)S(1)} %get-tuple-element.32.speed_ref, f32[3,2,64,128]{3,2,1,0:T(8,128)S(1)} %get-tuple-element.38.rim_ref), custom_call_target="tpu_custom_call" | custom-call | tf_op jit(solution)/shard_map/pallas_call | solution.py:670
  38.8 2.2 %collective-permute-done.9.two_ref = f32[192,128]{1,0:T(8,128)S(1)} collective-permute-done((f32[192,128]{1,0:T(8,128)S(1)}, f32[192,128]{1,0:T(8,128)S(1)}, u32[]{:S(2)}, u32[]{:S(2)}) %collective-permute-start.9) | collective-permute-done | bytes 98336 | tf_op jit(solution)/shard_map/ppermute | solution.py:684
  40.9 2.7 %shard_map.55.own_ref = f32[64,128]{1,0:T(8,128)S(1)} custom-call(s32[1]{0:T(128)} %bitcast.1.place_ref, f32[576,128]{1,0:T(8,128)S(1)} %get-tuple-element.40.own_ref, f32[192,128]{1,0:T(8,128)S(1)} %collective-permute-done.8.one_ref, f32[192,128]{1,0:T(8,128)S(1)} %collective-permute-done.9.two_ref, f32[320,128]{1,0:T(8,128)S(1)} %get-tuple-element.34.own_ref.older, ...), custom_call_target="tpu_custom_call" | custom-call | tf_op jit(solution)/shard_map/pallas_call | solution.py:670
  43.6 3.6 %collective-permute-start.10 = (f32[64,128]{1,0:T(8,128)S(1)}, f32[64,128]{1,0:T(8,128)S(1)}, u32[]{:S(2)}, u32[]{:S(2)}) collective-permute-start(f32[64,128]{1,0:T(8,128)S(1)} %shard_map.55.own_ref), channel_id=1, source_target_pairs={{0,64},{64,0},{128,192},{192,128},{1,65},{65,1},{129,193},{193,129... | collective-permute-start | bytes 98312 | tf_op jit(solution)/shard_map/ppermute | solution.py:689
  47.3 0.9 %collective-permute-done.10.other_ref = f32[64,128]{1,0:T(8,128)S(1)} collective-permute-done((f32[64,128]{1,0:T(8,128)S(1)}, f32[64,128]{1,0:T(8,128)S(1)}, u32[]{:S(2)}, u32[]{:S(2)}) %collective-permute-start.10) | collective-permute-done | bytes 32800 | tf_op jit(solution)/shard_map/ppermute | solution.py:689
  48.1 0.1 shard_map.56
  48.2 1.0 %collective-permute-start.11 = (f32[64,128]{1,0:T(8,128)S(1)}, f32[64,128]{1,0:T(8,128)S(1)}, u32[]{:S(2)}, u32[]{:S(2)}) collective-permute-start(f32[64,128]{1,0:T(8,128)S(1)} %get-tuple-element.44), channel_id=1, source_target_pairs={{0,128},{64,192},{128,0},{192,64},{1,129},{65,193},{129,1},{193,65... | collective-permute-start | bytes 98312 | tf_op jit(solution)/shard_map/ppermute | solution.py:689
  49.2 3.4 %collective-permute-done.11.far_ref = f32[64,128]{1,0:T(8,128)S(1)} collective-permute-done((f32[64,128]{1,0:T(8,128)S(1)}, f32[64,128]{1,0:T(8,128)S(1)}, u32[]{:S(2)}, u32[]{:S(2)}) %collective-permute-start.11) | collective-permute-done | bytes 32800 | tf_op jit(solution)/shard_map/ppermute | solution.py:689
  52.6 0.6 %shard_map.57 = f32[32,2,128]{2,1,0:T(2,128)} custom-call(s32[1]{0:T(128)} %bitcast.group_ref, f32[64,128]{1,0:T(8,128)S(1)} %get-tuple-element.43.keep_ref, f32[64,128]{1,0:T(8,128)S(1)} %collective-permute-done.11.far_ref), custom_call_target="tpu_custom_call" | custom-call | tf_op jit(solution)/shard_map/pallas_call | solution.py:670
  (4 shorter events, 0.0 us)
Async XLA Ops:
  1.3 4.4 %collective-permute-start = (f32[576,128]{1,0:T(8,128)S(1)}, f32[576,128]{1,0:T(8,128)S(1)}, u32[]{:S(2)}, u32[]{:S(2)}) collective-permute-start(f32[576,128]{1,0:T(8,128)S(1)} %get-tuple-element.25.raw_ref), channel_id=1, source_target_pairs={{0,64},{64,0},{128,192},{192,128},{1,65},{65,1},{129,193},{193,129... | collective-permute-start | bytes 884744 | tf_op jit(solution)/shard_map/ppermute | solution.py:689
  5.9 8.0 %collective-permute-start.1 = (f32[256,128]{1,0:T(8,128)S(1)}, f32[256,128]{1,0:T(8,128)S(1)}, u32[]{:S(2)}, u32[]{:S(2)}) collective-permute-start(f32[256,128]{1,0:T(8,128)S(1)} %get-tuple-element.27), channel_id=1, source_target_pairs={{0,128},{64,192},{128,0},{192,64},{1,129},{65,193},{129,1},{193,65... | collective-permute-start | bytes 393224 | tf_op jit(solution)/shard_map/ppermute | solution.py:689
  7.0 6.9 %collective-permute-start.2 = (f32[80,128]{1,0:T(8,128)S(1)}, f32[80,128]{1,0:T(8,128)S(1)}, u32[]{:S(2)}, u32[]{:S(2)}) collective-permute-start(f32[80,128]{1,0:T(8,128)S(1)} %get-tuple-element.28), channel_id=1, source_target_pairs={{0,1},{1,2},{2,3},{3,0},{64,195},{65,192},{66,193},{67,194},{128,1... | collective-permute-start | bytes 122888 | tf_op jit(solution)/shard_map/ppermute | solution.py:697
  13.9 1.5 %collective-permute-start.3 = (f32[336,128]{1,0:T(8,128)S(1)}, f32[336,128]{1,0:T(8,128)S(1)}, u32[]{:S(2)}, u32[]{:S(2)}) collective-permute-start(f32[336,128]{1,0:T(8,128)S(1)} %shard_map.48.half_ref), channel_id=1, source_target_pairs={{0,64},{64,0},{128,192},{192,128},{1,65},{65,1},{129,193},{193,129... | collective-permute-start | bytes 516104 | tf_op jit(solution)/shard_map/ppermute | solution.py:689
  15.8 8.7 %collective-permute-start.4 = (f32[176,128]{1,0:T(8,128)S(1)}, f32[176,128]{1,0:T(8,128)S(1)}, u32[]{:S(2)}, u32[]{:S(2)}) collective-permute-start(f32[176,128]{1,0:T(8,128)S(1)} %get-tuple-element.30), channel_id=1, source_target_pairs={{0,4},{4,0},{8,12},{12,8},{16,20},{20,16},{24,28},{28,24},{32,36},... | collective-permute-start | bytes 270344 | tf_op jit(solution)/shard_map/ppermute | solution.py:683
  17.5 7.8 %collective-permute-start.5 = (f32[176,128]{1,0:T(8,128)S(1)}, f32[176,128]{1,0:T(8,128)S(1)}, u32[]{:S(2)}, u32[]{:S(2)}) collective-permute-start(f32[176,128]{1,0:T(8,128)S(1)} %get-tuple-element.31), channel_id=1, source_target_pairs={{0,60},{4,8},{8,4},{12,16},{16,12},{20,24},{24,20},{28,32},{32,28}... | collective-permute-start | bytes 270344 | tf_op jit(solution)/shard_map/ppermute | solution.py:684
  26.1 5.8 %collective-permute-start.7 = (f32[224,128]{1,0:T(8,128)S(1)}, f32[224,128]{1,0:T(8,128)S(1)}, u32[]{:S(2)}, u32[]{:S(2)}) collective-permute-start(f32[224,128]{1,0:T(8,128)S(1)} %get-tuple-element.35), channel_id=1, source_target_pairs={{0,60},{4,8},{8,4},{12,16},{16,12},{20,24},{24,20},{28,32},{32,28}... | collective-permute-start | bytes 344072 | tf_op jit(solution)/shard_map/ppermute | solution.py:684
  29.4 3.9 %collective-permute-start.6 = (f32[224,128]{1,0:T(8,128)S(1)}, f32[224,128]{1,0:T(8,128)S(1)}, u32[]{:S(2)}, u32[]{:S(2)}) collective-permute-start(f32[224,128]{1,0:T(8,128)S(1)} %get-tuple-element.35), channel_id=1, source_target_pairs={{0,4},{4,0},{8,12},{12,8},{16,20},{20,16},{24,28},{28,24},{32,36},... | collective-permute-start | bytes 344072 | tf_op jit(solution)/shard_map/ppermute | solution.py:683
  35.2 3.6 %collective-permute-start.8 = (f32[192,128]{1,0:T(8,128)S(1)}, f32[192,128]{1,0:T(8,128)S(1)}, u32[]{:S(2)}, u32[]{:S(2)}) collective-permute-start(f32[192,128]{1,0:T(8,128)S(1)} %get-tuple-element.41), channel_id=1, source_target_pairs={{0,4},{4,0},{8,12},{12,8},{16,20},{20,16},{24,28},{28,24},{32,36},... | collective-permute-start | bytes 294920 | tf_op jit(solution)/shard_map/ppermute | solution.py:683
  35.3 5.7 %collective-permute-start.9 = (f32[192,128]{1,0:T(8,128)S(1)}, f32[192,128]{1,0:T(8,128)S(1)}, u32[]{:S(2)}, u32[]{:S(2)}) collective-permute-start(f32[192,128]{1,0:T(8,128)S(1)} %get-tuple-element.42), channel_id=1, source_target_pairs={{0,60},{4,8},{8,4},{12,16},{16,12},{20,24},{24,20},{28,32},{32,28}... | collective-permute-start | bytes 294920 | tf_op jit(solution)/shard_map/ppermute | solution.py:684
  43.6 4.5 %collective-permute-start.10 = (f32[64,128]{1,0:T(8,128)S(1)}, f32[64,128]{1,0:T(8,128)S(1)}, u32[]{:S(2)}, u32[]{:S(2)}) collective-permute-start(f32[64,128]{1,0:T(8,128)S(1)} %shard_map.55.own_ref), channel_id=1, source_target_pairs={{0,64},{64,0},{128,192},{192,128},{1,65},{65,1},{129,193},{193,129... | collective-permute-start | bytes 98312 | tf_op jit(solution)/shard_map/ppermute | solution.py:689
  48.2 4.4 %collective-permute-start.11 = (f32[64,128]{1,0:T(8,128)S(1)}, f32[64,128]{1,0:T(8,128)S(1)}, u32[]{:S(2)}, u32[]{:S(2)}) collective-permute-start(f32[64,128]{1,0:T(8,128)S(1)} %get-tuple-element.44), channel_id=1, source_target_pairs={{0,128},{64,192},{128,0},{192,64},{1,129},{65,193},{129,1},{193,65... | collective-permute-start | bytes 98312 | tf_op jit(solution)/shard_map/ppermute | solution.py:689

commit v7 on v6

--- a/solution.py
+++ b/solution.py
@@ -31,10 +31,6 @@
 
 def exact_dot(left, right):
     return jnp.dot(left, right, precision=lax.Precision.HIGHEST, preferred_element_type=F32)
-
-
-def chunk(index):
-    return pl.multiple_of(index * 8, 8)
 
 
 def folded(first, second, last):
@@ -339,14 +335,12 @@
     for index, place in enumerate(places):
         fill_wrapped(wrapped, index, *place)
 
-    def body(step, carry):
-        z = chunk(step)
+    def work(z):
         for index, place in enumerate(places):
             rate = across(load(place, z), wrapped, index, z, speed(1, index, z), speed(2, index, z))
             rate_ref[pl.ds(index * FINE + z, 8), :] = rate
-        return carry
-
-    lax.fori_loop(0, 8, body, 0)
+
+    in_pairs(work)
 
 
 def section(current, initial, speed, rates, wrapped, keep, blend, store):
@@ -355,8 +349,7 @@
         if rates[index] is None:
             fill_wrapped(wrapped, index, *current[index + 3])
 
-    def body(step, carry):
-        z = chunk(step)
+    def work(z):
         values = [load(place, z) for place in current]
         steps = [values[k + 1] - values[k] for k in range(rows + 5)]
         bends = [steps[k + 1] - steps[k] for k in range(rows + 4)]
@@ -377,9 +370,8 @@
             if keep:
                 moved = moved + keep * load(initial[index], z)
             store(index, z, moved)
-        return carry
-
-    lax.fori_loop(0, 8, body, 0)
+
+    in_pairs(work)
 
 
 def spread_speeds(stacked, speed_ref):
@@ -395,13 +387,13 @@
             speed_ref[component, row, pl.ds(1, FLOW, stride=2), :] = part
 
 
-def in_pairs(work):
+def in_pairs(work, parts=4):
     def body(step, carry):
-        for part in range(2):
-            work(pl.multiple_of(step * 16 + part * 8, 8))
+        for part in range(parts):
+            work(pl.multiple_of((step * parts + part) * 8, 8))
         return carry
 
-    lax.fori_loop(0, 4, body, 0)
+    lax.fori_loop(0, 8 // parts, body, 0)
 
 
 def centred(below, above):
@@ -648,16 +640,21 @@
     group = group_ref[0]
     lanes = lane_ids(64)
     beside = group + 1 - 2 * (group % 2)
-    for target, out_ref in ((group, keep_ref), ((group + 2) % 4, send_ref)):
+    sorted_parts = []
+    for target in (group, (group + 2) % 4):
         own = pltpu.roll(own_ref[...], (32 * group - 32 * target + LANES) % LANES, 1)
         other = pltpu.roll(other_ref[...], (32 * beside - 32 * target + LANES) % LANES, 1)
-        out_ref[...] = jnp.where(lanes // 32 == group, own, other)
+        sorted_parts.append(jnp.where(lanes // 32 == group, own, other))
+    keep_ref[...], send = sorted_parts
+    here = lane_ids(FLOW) // 64 == group // 2
+    send_ref[...] = jnp.where(here, send[0:FLOW, :], roll_lanes(send[FLOW:64, :], 64))
 
 
 def merge_kernel(group_ref, keep_ref, far_ref, out_ref):
-    merged = jnp.where(lane_ids(64) // 64 == group_ref[0] // 2, keep_ref[...], far_ref[...])
-    for row in range(2):
-        out_ref[:, row, :] = merged[row * FLOW : (row + 1) * FLOW, :]
+    here = lane_ids(FLOW) // 64 == group_ref[0] // 2
+    far = far_ref[...]
+    for row, part in enumerate((far, roll_lanes(far, 64))):
+        out_ref[:, row, :] = jnp.where(here, keep_ref[row * FLOW : (row + 1) * FLOW, :], part)
 
 
 def call(kernel, outs, scratch, *args, scalars=0, outer=False, last=False):
@@ -791,7 +788,7 @@
         scalars=1,
     )
     keep, send = call(
-        sort_kernel, [(64, LANES), (64, LANES)], [], group, result, crossed(result, 1), scalars=1
+        sort_kernel, [(64, LANES), (FLOW, LANES)], [], group, result, crossed(result, 1), scalars=1
     )
     return call(merge_kernel, [(FLOW, 2, LANES)], [], group, keep, crossed(send, 2), scalars=1, last=True)[None]
 

time: 53.3 us -> 51.7 us (0.970)
  Pallas kernels: 12.9 us -> 8.89 us
  waiting for transfers between devices: 16.2 us -> 18.6 us
    pallas_call x12, Pallas kernels: 12.9 us -> 8.89 us  [call(): pl.pallas_call(kernel, out_shape=shapes if len(shapes) > 1 else shapes[0]...]
    ppermute x3, waiting for transfers between devices: 3.69 us -> 5.54 us  [swapped(): second = lax.ppermute(second, 'gx', far)]
    ppermute x3, waiting for transfers between devices: 1.48 us -> 2.24 us  [swapped(): first = lax.ppermute(first, 'gx', near)]
  transfers between devices with their start and end apart: 12 -> 12, of which waited for: 9 -> 10; matrix products, arithmetic and copies ran while one was open for 0% -> 0% of each run, Pallas kernels for 10% -> 5%
where the time goes in v7:
time: 51.7 us; the launch traced here: 51.6 us
  starting transfers between devices  24 us (46%)
  waiting for transfers between devices  18.6 us (36%)
  Pallas kernels  8.89 us (17%)
    ppermute x3, starting transfers between devices, swapped(): second = lax.ppermute(second, 'gx', far)  10.5 us
    ppermute x5, starting transfers between devices, crossed(): lax.ppermute(value, 'grp', [(i, i ^ bit) for i in range(lax.axis_size('gr...  9 us
    pallas_call x12, Pallas kernels, call(): pl.pallas_call(kernel, out_shape=shapes if len(shapes) > 1 else shapes[0]...  8.89 us
    ppermute x5, waiting for transfers between devices, crossed(): lax.ppermute(value, 'grp', [(i, i ^ bit) for i in range(lax.axis_size('gr...  6.64 us
    ppermute x3, waiting for transfers between devices, swapped(): second = lax.ppermute(second, 'gx', far)  5.54 us
    ppermute x1, waiting for transfers between devices, to_next_blocks(): return lax.ppermute(value, ('grp', 'gy'), pairs)  4.19 us
    ppermute x1, starting transfers between devices, to_next_blocks(): return lax.ppermute(value, ('grp', 'gy'), pairs)  2.69 us
    ppermute x3, waiting for transfers between devices, swapped(): first = lax.ppermute(first, 'gx', near)  2.24 us
  transfers between devices with their start and end apart: 12, of which 10 were waited for; matrix products, arithmetic and copies ran while one was open for 0% of the time, Pallas kernels for 5%

profile of v7, /device:TPU:1, one launch (start us, length us, event | category | flops | bytes accessed | tf_op | source)
XLA Modules:
  0.0 51.6 jit_solution(7769682103737076034)
XLA Ops:
  0.0 1.3 %shard_map.46 = (f32[576,128]{1,0:T(8,128)S(1)}, f32[2,16,128]{2,1,0:T(8,128)S(1)}) custom-call(f32[32,2,128]{2,1,0:T(2,128)} %bitcast.7, f32[64,4,256]{2,1,0:T(4,128)} %bitcast.6, s32[8,16]{1,0:T(8,128)} %bitcast.8, s32[4,256]{1,0:T(4,128)} %nozzle_ref.1), custom_call_target="tpu_custom_call" | custom-call | tf_op jit(solution)/shard_map/pallas_call | solution.py:667
  1.3 3.2 %collective-permute-start = (f32[576,128]{1,0:T(8,128)S(1)}, f32[576,128]{1,0:T(8,128)S(1)}, u32[]{:S(2)}, u32[]{:S(2)}) collective-permute-start(f32[576,128]{1,0:T(8,128)S(1)} %get-tuple-element.25.raw_ref), channel_id=1, source_target_pairs={{0,64},{64,0},{128,192},{192,128},{1,65},{65,1},{129,193},{193,129... | collective-permute-start | bytes 884744 | tf_op jit(solution)/shard_map/ppermute | solution.py:686
  4.5 1.2 %collective-permute-done.other_ref = f32[576,128]{1,0:T(8,128)S(1)} collective-permute-done((f32[576,128]{1,0:T(8,128)S(1)}, f32[576,128]{1,0:T(8,128)S(1)}, u32[]{:S(2)}, u32[]{:S(2)}) %collective-permute-start) | collective-permute-done | bytes 294944 | tf_op jit(solution)/shard_map/ppermute | solution.py:686
  5.7 0.2 shard_map.47
  5.9 1.1 %collective-permute-start.1 = (f32[256,128]{1,0:T(8,128)S(1)}, f32[256,128]{1,0:T(8,128)S(1)}, u32[]{:S(2)}, u32[]{:S(2)}) collective-permute-start(f32[256,128]{1,0:T(8,128)S(1)} %get-tuple-element.27), channel_id=1, source_target_pairs={{0,128},{64,192},{128,0},{192,64},{1,129},{65,193},{129,1},{193,65... | collective-permute-start | bytes 393224 | tf_op jit(solution)/shard_map/ppermute | solution.py:686
  7.0 2.7 %collective-permute-start.2 = (f32[80,128]{1,0:T(8,128)S(1)}, f32[80,128]{1,0:T(8,128)S(1)}, u32[]{:S(2)}, u32[]{:S(2)}) collective-permute-start(f32[80,128]{1,0:T(8,128)S(1)} %get-tuple-element.28), channel_id=1, source_target_pairs={{0,1},{1,2},{2,3},{3,0},{64,195},{65,192},{66,193},{67,194},{128,1... | collective-permute-start | bytes 122888 | tf_op jit(solution)/shard_map/ppermute | solution.py:694
  9.7 4.2 %collective-permute-done.2.edge_ref = f32[80,128]{1,0:T(8,128)S(1)} collective-permute-done((f32[80,128]{1,0:T(8,128)S(1)}, f32[80,128]{1,0:T(8,128)S(1)}, u32[]{:S(2)}, u32[]{:S(2)}) %collective-permute-start.2) | collective-permute-done | bytes 40992 | tf_op jit(solution)/shard_map/ppermute | solution.py:694
  13.9 0.1 collective-permute-start.3
  14.0 1.4 %collective-permute-done.3.far_half_ref = f32[336,128]{1,0:T(8,128)S(1)} collective-permute-done((f32[336,128]{1,0:T(8,128)S(1)}, f32[336,128]{1,0:T(8,128)S(1)}, u32[]{:S(2)}, u32[]{:S(2)}) %collective-permute-start.3) | collective-permute-done | bytes 172064 | tf_op jit(solution)/shard_map/ppermute | solution.py:686
  15.4 0.4 shard_map.49
  15.8 1.7 %collective-permute-start.4 = (f32[176,128]{1,0:T(8,128)S(1)}, f32[176,128]{1,0:T(8,128)S(1)}, u32[]{:S(2)}, u32[]{:S(2)}) collective-permute-start(f32[176,128]{1,0:T(8,128)S(1)} %get-tuple-element.30), channel_id=1, source_target_pairs={{0,4},{4,0},{8,12},{12,8},{16,20},{20,16},{24,28},{28,24},{32,36},... | collective-permute-start | bytes 270344 | tf_op jit(solution)/shard_map/ppermute | solution.py:680
  17.5 5.2 %collective-permute-start.5 = (f32[176,128]{1,0:T(8,128)S(1)}, f32[176,128]{1,0:T(8,128)S(1)}, u32[]{:S(2)}, u32[]{:S(2)}) collective-permute-start(f32[176,128]{1,0:T(8,128)S(1)} %get-tuple-element.31), channel_id=1, source_target_pairs={{0,60},{4,8},{8,4},{12,16},{16,12},{20,24},{24,20},{28,32},{32,28}... | collective-permute-start | bytes 270344 | tf_op jit(solution)/shard_map/ppermute | solution.py:681
  22.7 0.9 %shard_map.50 = (f32[3,2,64,128]{3,2,1,0:T(8,128)S(1)}, f32[256,128]{1,0:T(8,128)S(1)}) custom-call(f32[400,128]{1,0:T(8,128)S(1)} %get-tuple-element.29.fixed_ref), custom_call_target="tpu_custom_call" | custom-call | tf_op jit(solution)/shard_map/pallas_call | solution.py:667
  23.6 1.7 %collective-permute-done.5.two_ref = f32[176,128]{1,0:T(8,128)S(1)} collective-permute-done((f32[176,128]{1,0:T(8,128)S(1)}, f32[176,128]{1,0:T(8,128)S(1)}, u32[]{:S(2)}, u32[]{:S(2)}) %collective-permute-start.5) | collective-permute-done | bytes 90144 | tf_op jit(solution)/shard_map/ppermute | solution.py:681
  25.3 0.7 %shard_map.51 = (f32[320,128]{1,0:T(8,128)S(1)}, f32[224,128]{1,0:T(8,128)S(1)}, f32[176,128]{1,0:T(8,128)S(1)}, f32[176,128]{1,0:T(8,128)S(1)}) custom-call(s32[1]{0:T(128)} %bitcast.1.place_ref, f32[400,128]{1,0:T(8,128)S(1)} %get-tuple-element.29.fixed_ref, f32[176,128]{1,0:T(8,128)S(1)} %collective-permute-done.4.one_ref, ...), custom_call_target="tpu_custom_call" | custom-call | tf_op jit(solution)/shard_map/pallas_call | solution.py:667
  26.0 3.4 %collective-permute-start.7 = (f32[224,128]{1,0:T(8,128)S(1)}, f32[224,128]{1,0:T(8,128)S(1)}, u32[]{:S(2)}, u32[]{:S(2)}) collective-permute-start(f32[224,128]{1,0:T(8,128)S(1)} %get-tuple-element.35), channel_id=1, source_target_pairs={{0,60},{4,8},{8,4},{12,16},{16,12},{20,24},{24,20},{28,32},{32,28}... | collective-permute-start | bytes 344072 | tf_op jit(solution)/shard_map/ppermute | solution.py:681
  29.4 0.9 %shard_map.52 = (f32[3,2,64,128]{3,2,1,0:T(8,128)S(1)}, f32[256,128]{1,0:T(8,128)S(1)}) custom-call(f32[320,128]{1,0:T(8,128)S(1)} %get-tuple-element.34.own_ref.older, f32[176,128]{1,0:T(8,128)S(1)} %get-tuple-element.36.old_left, f32[176,128]{1,0:T(8,128)S(1)} %get-tuple-element.37.old_right, f32[3,2,64,128]{3,2,1,0:T(8,128)S(1)} %get-tuple-element.32.speed_ref), custom_call_target="tpu_custom_call" | custom-call | tf_op jit(solution)/shard_map/pallas_call | solution.py:667
  30.2 1.6 %collective-permute-done.7.two_ref = f32[224,128]{1,0:T(8,128)S(1)} collective-permute-done((f32[224,128]{1,0:T(8,128)S(1)}, f32[224,128]{1,0:T(8,128)S(1)}, u32[]{:S(2)}, u32[]{:S(2)}) %collective-permute-start.7) | collective-permute-done | bytes 114720 | tf_op jit(solution)/shard_map/ppermute | solution.py:681
  31.8 1.5 %collective-permute-done.6.one_ref = f32[224,128]{1,0:T(8,128)S(1)} collective-permute-done((f32[224,128]{1,0:T(8,128)S(1)}, f32[224,128]{1,0:T(8,128)S(1)}, u32[]{:S(2)}, u32[]{:S(2)}) %collective-permute-start.6) | collective-permute-done | bytes 114720 | tf_op jit(solution)/shard_map/ppermute | solution.py:680
  33.3 1.2 %shard_map.53 = (f32[576,128]{1,0:T(8,128)S(1)}, f32[192,128]{1,0:T(8,128)S(1)}, f32[192,128]{1,0:T(8,128)S(1)}) custom-call(s32[1]{0:T(128)} %bitcast.1.place_ref, f32[320,128]{1,0:T(8,128)S(1)} %get-tuple-element.34.own_ref.older, f32[224,128]{1,0:T(8,128)S(1)} %collective-permute-done.6.one_ref, f32[224,128]{1,0:T(8,128)S(1)} %collective-permute-done.7.two_ref, ...), custom_call_target="tpu_custom_call" | custom-call | tf_op jit(solution)/shard_map/pallas_call | solution.py:667
  34.5 0.1 collective-permute-start.8
  34.6 1.9 %collective-permute-start.9 = (f32[192,128]{1,0:T(8,128)S(1)}, f32[192,128]{1,0:T(8,128)S(1)}, u32[]{:S(2)}, u32[]{:S(2)}) collective-permute-start(f32[192,128]{1,0:T(8,128)S(1)} %get-tuple-element.42), channel_id=1, source_target_pairs={{0,60},{4,8},{8,4},{12,16},{16,12},{20,24},{24,20},{28,32},{32,28}... | collective-permute-start | bytes 294920 | tf_op jit(solution)/shard_map/ppermute | solution.py:681
  36.5 0.8 %shard_map.54.rate_ref = f32[384,128]{1,0:T(8,128)S(1)} custom-call(f32[576,128]{1,0:T(8,128)S(1)} %get-tuple-element.40.own_ref, f32[3,2,64,128]{3,2,1,0:T(8,128)S(1)} %get-tuple-element.32.speed_ref, f32[3,2,64,128]{3,2,1,0:T(8,128)S(1)} %get-tuple-element.38.rim_ref), custom_call_target="tpu_custom_call" | custom-call | tf_op jit(solution)/shard_map/pallas_call | solution.py:667
  37.3 0.8 %collective-permute-done.8.one_ref = f32[192,128]{1,0:T(8,128)S(1)} collective-permute-done((f32[192,128]{1,0:T(8,128)S(1)}, f32[192,128]{1,0:T(8,128)S(1)}, u32[]{:S(2)}, u32[]{:S(2)}) %collective-permute-start.8) | collective-permute-done | bytes 98336 | tf_op jit(solution)/shard_map/ppermute | solution.py:680
  38.0 2.2 %collective-permute-done.9.two_ref = f32[192,128]{1,0:T(8,128)S(1)} collective-permute-done((f32[192,128]{1,0:T(8,128)S(1)}, f32[192,128]{1,0:T(8,128)S(1)}, u32[]{:S(2)}, u32[]{:S(2)}) %collective-permute-start.9) | collective-permute-done | bytes 98336 | tf_op jit(solution)/shard_map/ppermute | solution.py:681
  40.2 1.9 %shard_map.55.own_ref = f32[64,128]{1,0:T(8,128)S(1)} custom-call(s32[1]{0:T(128)} %bitcast.1.place_ref, f32[576,128]{1,0:T(8,128)S(1)} %get-tuple-element.40.own_ref, f32[192,128]{1,0:T(8,128)S(1)} %collective-permute-done.8.one_ref, f32[192,128]{1,0:T(8,128)S(1)} %collective-permute-done.9.two_ref, f32[320,128]{1,0:T(8,128)S(1)} %get-tuple-element.34.own_ref.older, ...), custom_call_target="tpu_custom_call" | custom-call | tf_op jit(solution)/shard_map/pallas_call | solution.py:667
  42.2 3.6 %collective-permute-start.10 = (f32[64,128]{1,0:T(8,128)S(1)}, f32[64,128]{1,0:T(8,128)S(1)}, u32[]{:S(2)}, u32[]{:S(2)}) collective-permute-start(f32[64,128]{1,0:T(8,128)S(1)} %shard_map.55.own_ref), channel_id=1, source_target_pairs={{0,64},{64,0},{128,192},{192,128},{1,65},{65,1},{129,193},{193,129... | collective-permute-start | bytes 98312 | tf_op jit(solution)/shard_map/ppermute | solution.py:686
  45.8 0.9 %collective-permute-done.10.other_ref = f32[64,128]{1,0:T(8,128)S(1)} collective-permute-done((f32[64,128]{1,0:T(8,128)S(1)}, f32[64,128]{1,0:T(8,128)S(1)}, u32[]{:S(2)}, u32[]{:S(2)}) %collective-permute-start.10) | collective-permute-done | bytes 32800 | tf_op jit(solution)/shard_map/ppermute | solution.py:686
  46.6 0.1 shard_map.56
  46.8 1.0 %collective-permute-start.11 = (f32[32,128]{1,0:T(8,128)S(1)}, f32[32,128]{1,0:T(8,128)S(1)}, u32[]{:S(2)}, u32[]{:S(2)}) collective-permute-start(f32[32,128]{1,0:T(8,128)S(1)} %get-tuple-element.44), channel_id=1, source_target_pairs={{0,128},{64,192},{128,0},{192,64},{1,129},{65,193},{129,1},{193,65... | collective-permute-start | bytes 49160 | tf_op jit(solution)/shard_map/ppermute | solution.py:686
  47.8 3.2 %collective-permute-done.11.far_ref = f32[32,128]{1,0:T(8,128)S(1)} collective-permute-done((f32[32,128]{1,0:T(8,128)S(1)}, f32[32,128]{1,0:T(8,128)S(1)}, u32[]{:S(2)}, u32[]{:S(2)}) %collective-permute-start.11) | collective-permute-done | bytes 16416 | tf_op jit(solution)/shard_map/ppermute | solution.py:686
  50.9 0.7 %shard_map.57 = f32[32,2,128]{2,1,0:T(2,128)} custom-call(s32[1]{0:T(128)} %bitcast.group_ref, f32[64,128]{1,0:T(8,128)S(1)} %get-tuple-element.43.keep_ref, f32[32,128]{1,0:T(8,128)S(1)} %collective-permute-done.11.far_ref), custom_call_target="tpu_custom_call" | custom-call | tf_op jit(solution)/shard_map/pallas_call | solution.py:667
  (4 shorter events, 0.0 us)
Async XLA Ops:
  1.3 4.4 %collective-permute-start = (f32[576,128]{1,0:T(8,128)S(1)}, f32[576,128]{1,0:T(8,128)S(1)}, u32[]{:S(2)}, u32[]{:S(2)}) collective-permute-start(f32[576,128]{1,0:T(8,128)S(1)} %get-tuple-element.25.raw_ref), channel_id=1, source_target_pairs={{0,64},{64,0},{128,192},{192,128},{1,65},{65,1},{129,193},{193,129... | collective-permute-start | bytes 884744 | tf_op jit(solution)/shard_map/ppermute | solution.py:686
  5.9 8.0 %collective-permute-start.1 = (f32[256,128]{1,0:T(8,128)S(1)}, f32[256,128]{1,0:T(8,128)S(1)}, u32[]{:S(2)}, u32[]{:S(2)}) collective-permute-start(f32[256,128]{1,0:T(8,128)S(1)} %get-tuple-element.27), channel_id=1, source_target_pairs={{0,128},{64,192},{128,0},{192,64},{1,129},{65,193},{129,1},{193,65... | collective-permute-start | bytes 393224 | tf_op jit(solution)/shard_map/ppermute | solution.py:686
  7.0 6.9 %collective-permute-start.2 = (f32[80,128]{1,0:T(8,128)S(1)}, f32[80,128]{1,0:T(8,128)S(1)}, u32[]{:S(2)}, u32[]{:S(2)}) collective-permute-start(f32[80,128]{1,0:T(8,128)S(1)} %get-tuple-element.28), channel_id=1, source_target_pairs={{0,1},{1,2},{2,3},{3,0},{64,195},{65,192},{66,193},{67,194},{128,1... | collective-permute-start | bytes 122888 | tf_op jit(solution)/shard_map/ppermute | solution.py:694
  13.9 1.5 %collective-permute-start.3 = (f32[336,128]{1,0:T(8,128)S(1)}, f32[336,128]{1,0:T(8,128)S(1)}, u32[]{:S(2)}, u32[]{:S(2)}) collective-permute-start(f32[336,128]{1,0:T(8,128)S(1)} %shard_map.48.half_ref), channel_id=1, source_target_pairs={{0,64},{64,0},{128,192},{192,128},{1,65},{65,1},{129,193},{193,129... | collective-permute-start | bytes 516104 | tf_op jit(solution)/shard_map/ppermute | solution.py:686
  15.8 7.8 %collective-permute-start.4 = (f32[176,128]{1,0:T(8,128)S(1)}, f32[176,128]{1,0:T(8,128)S(1)}, u32[]{:S(2)}, u32[]{:S(2)}) collective-permute-start(f32[176,128]{1,0:T(8,128)S(1)} %get-tuple-element.30), channel_id=1, source_target_pairs={{0,4},{4,0},{8,12},{12,8},{16,20},{20,16},{24,28},{28,24},{32,36},... | collective-permute-start | bytes 270344 | tf_op jit(solution)/shard_map/ppermute | solution.py:680
  17.5 7.8 %collective-permute-start.5 = (f32[176,128]{1,0:T(8,128)S(1)}, f32[176,128]{1,0:T(8,128)S(1)}, u32[]{:S(2)}, u32[]{:S(2)}) collective-permute-start(f32[176,128]{1,0:T(8,128)S(1)} %get-tuple-element.31), channel_id=1, source_target_pairs={{0,60},{4,8},{8,4},{12,16},{16,12},{20,24},{24,20},{28,32},{32,28}... | collective-permute-start | bytes 270344 | tf_op jit(solution)/shard_map/ppermute | solution.py:681
  26.0 5.8 %collective-permute-start.7 = (f32[224,128]{1,0:T(8,128)S(1)}, f32[224,128]{1,0:T(8,128)S(1)}, u32[]{:S(2)}, u32[]{:S(2)}) collective-permute-start(f32[224,128]{1,0:T(8,128)S(1)} %get-tuple-element.35), channel_id=1, source_target_pairs={{0,60},{4,8},{8,4},{12,16},{16,12},{20,24},{24,20},{28,32},{32,28}... | collective-permute-start | bytes 344072 | tf_op jit(solution)/shard_map/ppermute | solution.py:681
  29.4 3.9 %collective-permute-start.6 = (f32[224,128]{1,0:T(8,128)S(1)}, f32[224,128]{1,0:T(8,128)S(1)}, u32[]{:S(2)}, u32[]{:S(2)}) collective-permute-start(f32[224,128]{1,0:T(8,128)S(1)} %get-tuple-element.35), channel_id=1, source_target_pairs={{0,4},{4,0},{8,12},{12,8},{16,20},{20,16},{24,28},{28,24},{32,36},... | collective-permute-start | bytes 344072 | tf_op jit(solution)/shard_map/ppermute | solution.py:680
  34.5 3.6 %collective-permute-start.8 = (f32[192,128]{1,0:T(8,128)S(1)}, f32[192,128]{1,0:T(8,128)S(1)}, u32[]{:S(2)}, u32[]{:S(2)}) collective-permute-start(f32[192,128]{1,0:T(8,128)S(1)} %get-tuple-element.41), channel_id=1, source_target_pairs={{0,4},{4,0},{8,12},{12,8},{16,20},{20,16},{24,28},{28,24},{32,36},... | collective-permute-start | bytes 294920 | tf_op jit(solution)/shard_map/ppermute | solution.py:680
  34.6 5.7 %collective-permute-start.9 = (f32[192,128]{1,0:T(8,128)S(1)}, f32[192,128]{1,0:T(8,128)S(1)}, u32[]{:S(2)}, u32[]{:S(2)}) collective-permute-start(f32[192,128]{1,0:T(8,128)S(1)} %get-tuple-element.42), channel_id=1, source_target_pairs={{0,60},{4,8},{8,4},{12,16},{16,12},{20,24},{24,20},{28,32},{32,28}... | collective-permute-start | bytes 294920 | tf_op jit(solution)/shard_map/ppermute | solution.py:681
  42.2 4.5 %collective-permute-start.10 = (f32[64,128]{1,0:T(8,128)S(1)}, f32[64,128]{1,0:T(8,128)S(1)}, u32[]{:S(2)}, u32[]{:S(2)}) collective-permute-start(f32[64,128]{1,0:T(8,128)S(1)} %shard_map.55.own_ref), channel_id=1, source_target_pairs={{0,64},{64,0},{128,192},{192,128},{1,65},{65,1},{129,193},{193,129... | collective-permute-start | bytes 98312 | tf_op jit(solution)/shard_map/ppermute | solution.py:686
  46.8 4.1 %collective-permute-start.11 = (f32[32,128]{1,0:T(8,128)S(1)}, f32[32,128]{1,0:T(8,128)S(1)}, u32[]{:S(2)}, u32[]{:S(2)}) collective-permute-start(f32[32,128]{1,0:T(8,128)S(1)} %get-tuple-element.44), channel_id=1, source_target_pairs={{0,128},{64,192},{128,0},{192,64},{1,129},{65,193},{129,1},{193,65... | collective-permute-start | bytes 49160 | tf_op jit(solution)/shard_map/ppermute | solution.py:686

commit v8 on v7

--- a/solution.py
+++ b/solution.py
@@ -387,13 +387,9 @@
             speed_ref[component, row, pl.ds(1, FLOW, stride=2), :] = part
 
 
-def in_pairs(work, parts=4):
-    def body(step, carry):
-        for part in range(parts):
-            work(pl.multiple_of((step * parts + part) * 8, 8))
-        return carry
-
-    lax.fori_loop(0, 8 // parts, body, 0)
+def in_pairs(work):
+    for part in range(8):
+        work(part * 8)
 
 
 def centred(below, above):

time: 51.7 us -> 51.1 us (0.988)
  waiting for transfers between devices: 18.6 us -> 17.5 us
  Pallas kernels: 8.89 us -> 9.42 us
    ppermute x3, waiting for transfers between devices: 2.24 us -> 1.48 us  [swapped(): first = lax.ppermute(first, 'gx', near)]
    pallas_call x12, Pallas kernels: 8.89 us -> 9.42 us  [call(): pl.pallas_call(kernel, out_shape=shapes if len(shapes) > 1 else shapes[0]...]
  transfers between devices with their start and end apart: 12 -> 12, of which waited for: 10 -> 9; matrix products, arithmetic and copies ran while one was open for 0% -> 0% of each run, Pallas kernels for 5% -> 7%
where the time goes in v8:
time: 51.1 us; the launch traced here: 51 us
  starting transfers between devices  24 us (47%)
  waiting for transfers between devices  17.5 us (34%)
  Pallas kernels  9.42 us (18%)
    ppermute x3, starting transfers between devices, swapped(): second = lax.ppermute(second, 'gx', far)  10.5 us
    pallas_call x12, Pallas kernels, call(): pl.pallas_call(kernel, out_shape=shapes if len(shapes) > 1 else shapes[0]...  9.42 us
    ppermute x5, starting transfers between devices, crossed(): lax.ppermute(value, 'grp', [(i, i ^ bit) for i in range(lax.axis_size('gr...  8.99 us
    ppermute x5, waiting for transfers between devices, crossed(): lax.ppermute(value, 'grp', [(i, i ^ bit) for i in range(lax.axis_size('gr...  6.64 us
    ppermute x3, waiting for transfers between devices, swapped(): second = lax.ppermute(second, 'gx', far)  5.18 us
    ppermute x1, waiting for transfers between devices, to_next_blocks(): return lax.ppermute(value, ('grp', 'gy'), pairs)  4.19 us
    ppermute x1, starting transfers between devices, to_next_blocks(): return lax.ppermute(value, ('grp', 'gy'), pairs)  2.69 us
    ppermute x3, starting transfers between devices, swapped(): first = lax.ppermute(first, 'gx', near)  1.82 us
  transfers between devices with their start and end apart: 12, of which 9 were waited for; matrix products, arithmetic and copies ran while one was open for 0% of the time, Pallas kernels for 7%

profile of v8, /device:TPU:1, one launch (start us, length us, event | category | flops | bytes accessed | tf_op | source)
XLA Modules:
  0.0 51.0 jit_solution(6231631388768081483)
XLA Ops:
  0.0 1.3 %shard_map.46 = (f32[576,128]{1,0:T(8,128)S(1)}, f32[2,16,128]{2,1,0:T(8,128)S(1)}) custom-call(f32[32,2,128]{2,1,0:T(2,128)} %bitcast.7, f32[64,4,256]{2,1,0:T(4,128)} %bitcast.6, s32[8,16]{1,0:T(8,128)} %bitcast.8, s32[4,256]{1,0:T(4,128)} %nozzle_ref.1), custom_call_target="tpu_custom_call" | custom-call | tf_op jit(solution)/shard_map/pallas_call | solution.py:663
  1.3 3.2 %collective-permute-start = (f32[576,128]{1,0:T(8,128)S(1)}, f32[576,128]{1,0:T(8,128)S(1)}, u32[]{:S(2)}, u32[]{:S(2)}) collective-permute-start(f32[576,128]{1,0:T(8,128)S(1)} %get-tuple-element.25.raw_ref), channel_id=1, source_target_pairs={{0,64},{64,0},{128,192},{192,128},{1,65},{65,1},{129,193},{193,129... | collective-permute-start | bytes 884744 | tf_op jit(solution)/shard_map/ppermute | solution.py:682
  4.5 1.2 %collective-permute-done.other_ref = f32[576,128]{1,0:T(8,128)S(1)} collective-permute-done((f32[576,128]{1,0:T(8,128)S(1)}, f32[576,128]{1,0:T(8,128)S(1)}, u32[]{:S(2)}, u32[]{:S(2)}) %collective-permute-start) | collective-permute-done | bytes 294944 | tf_op jit(solution)/shard_map/ppermute | solution.py:682
  5.7 0.2 shard_map.47
  5.9 1.1 %collective-permute-start.1 = (f32[256,128]{1,0:T(8,128)S(1)}, f32[256,128]{1,0:T(8,128)S(1)}, u32[]{:S(2)}, u32[]{:S(2)}) collective-permute-start(f32[256,128]{1,0:T(8,128)S(1)} %get-tuple-element.27), channel_id=1, source_target_pairs={{0,128},{64,192},{128,0},{192,64},{1,129},{65,193},{129,1},{193,65... | collective-permute-start | bytes 393224 | tf_op jit(solution)/shard_map/ppermute | solution.py:682
  7.0 2.7 %collective-permute-start.2 = (f32[80,128]{1,0:T(8,128)S(1)}, f32[80,128]{1,0:T(8,128)S(1)}, u32[]{:S(2)}, u32[]{:S(2)}) collective-permute-start(f32[80,128]{1,0:T(8,128)S(1)} %get-tuple-element.28), channel_id=1, source_target_pairs={{0,1},{1,2},{2,3},{3,0},{64,195},{65,192},{66,193},{67,194},{128,1... | collective-permute-start | bytes 122888 | tf_op jit(solution)/shard_map/ppermute | solution.py:690
  9.7 4.2 %collective-permute-done.2.edge_ref = f32[80,128]{1,0:T(8,128)S(1)} collective-permute-done((f32[80,128]{1,0:T(8,128)S(1)}, f32[80,128]{1,0:T(8,128)S(1)}, u32[]{:S(2)}, u32[]{:S(2)}) %collective-permute-start.2) | collective-permute-done | bytes 40992 | tf_op jit(solution)/shard_map/ppermute | solution.py:690
  13.9 0.0 collective-permute-done.1.half_ref
  13.9 0.1 collective-permute-start.3
  14.0 1.4 %collective-permute-done.3.far_half_ref = f32[336,128]{1,0:T(8,128)S(1)} collective-permute-done((f32[336,128]{1,0:T(8,128)S(1)}, f32[336,128]{1,0:T(8,128)S(1)}, u32[]{:S(2)}, u32[]{:S(2)}) %collective-permute-start.3) | collective-permute-done | bytes 172064 | tf_op jit(solution)/shard_map/ppermute | solution.py:682
  15.4 0.4 shard_map.49
  15.8 1.7 %collective-permute-start.4 = (f32[176,128]{1,0:T(8,128)S(1)}, f32[176,128]{1,0:T(8,128)S(1)}, u32[]{:S(2)}, u32[]{:S(2)}) collective-permute-start(f32[176,128]{1,0:T(8,128)S(1)} %get-tuple-element.30), channel_id=1, source_target_pairs={{0,4},{4,0},{8,12},{12,8},{16,20},{20,16},{24,28},{28,24},{32,36},... | collective-permute-start | bytes 270344 | tf_op jit(solution)/shard_map/ppermute | solution.py:676
  17.5 5.2 %collective-permute-start.5 = (f32[176,128]{1,0:T(8,128)S(1)}, f32[176,128]{1,0:T(8,128)S(1)}, u32[]{:S(2)}, u32[]{:S(2)}) collective-permute-start(f32[176,128]{1,0:T(8,128)S(1)} %get-tuple-element.31), channel_id=1, source_target_pairs={{0,60},{4,8},{8,4},{12,16},{16,12},{20,24},{24,20},{28,32},{32,28}... | collective-permute-start | bytes 270344 | tf_op jit(solution)/shard_map/ppermute | solution.py:677
  22.7 0.9 %shard_map.50 = (f32[3,2,64,128]{3,2,1,0:T(8,128)S(1)}, f32[256,128]{1,0:T(8,128)S(1)}) custom-call(f32[400,128]{1,0:T(8,128)S(1)} %get-tuple-element.29.fixed_ref), custom_call_target="tpu_custom_call" | custom-call | tf_op jit(solution)/shard_map/pallas_call | solution.py:663
  23.6 1.7 %collective-permute-done.5.two_ref = f32[176,128]{1,0:T(8,128)S(1)} collective-permute-done((f32[176,128]{1,0:T(8,128)S(1)}, f32[176,128]{1,0:T(8,128)S(1)}, u32[]{:S(2)}, u32[]{:S(2)}) %collective-permute-start.5) | collective-permute-done | bytes 90144 | tf_op jit(solution)/shard_map/ppermute | solution.py:677
  25.3 0.5 shard_map.51
  25.8 3.4 %collective-permute-start.7 = (f32[224,128]{1,0:T(8,128)S(1)}, f32[224,128]{1,0:T(8,128)S(1)}, u32[]{:S(2)}, u32[]{:S(2)}) collective-permute-start(f32[224,128]{1,0:T(8,128)S(1)} %get-tuple-element.35), channel_id=1, source_target_pairs={{0,60},{4,8},{8,4},{12,16},{16,12},{20,24},{24,20},{28,32},{32,28}... | collective-permute-start | bytes 344072 | tf_op jit(solution)/shard_map/ppermute | solution.py:677
  29.2 0.8 %shard_map.52 = (f32[3,2,64,128]{3,2,1,0:T(8,128)S(1)}, f32[256,128]{1,0:T(8,128)S(1)}) custom-call(f32[320,128]{1,0:T(8,128)S(1)} %get-tuple-element.34.own_ref.older, f32[176,128]{1,0:T(8,128)S(1)} %get-tuple-element.36.old_left, f32[176,128]{1,0:T(8,128)S(1)} %get-tuple-element.37.old_right, f32[3,2,64,128]{3,2,1,0:T(8,128)S(1)} %get-tuple-element.32.speed_ref), custom_call_target="tpu_custom_call" | custom-call | tf_op jit(solution)/shard_map/pallas_call | solution.py:663
  29.9 1.7 %collective-permute-done.7.two_ref = f32[224,128]{1,0:T(8,128)S(1)} collective-permute-done((f32[224,128]{1,0:T(8,128)S(1)}, f32[224,128]{1,0:T(8,128)S(1)}, u32[]{:S(2)}, u32[]{:S(2)}) %collective-permute-start.7) | collective-permute-done | bytes 114720 | tf_op jit(solution)/shard_map/ppermute | solution.py:677
  31.6 1.5 %collective-permute-done.6.one_ref = f32[224,128]{1,0:T(8,128)S(1)} collective-permute-done((f32[224,128]{1,0:T(8,128)S(1)}, f32[224,128]{1,0:T(8,128)S(1)}, u32[]{:S(2)}, u32[]{:S(2)}) %collective-permute-start.6) | collective-permute-done | bytes 114720 | tf_op jit(solution)/shard_map/ppermute | solution.py:676
  33.1 1.1 %shard_map.53 = (f32[576,128]{1,0:T(8,128)S(1)}, f32[192,128]{1,0:T(8,128)S(1)}, f32[192,128]{1,0:T(8,128)S(1)}) custom-call(s32[1]{0:T(128)} %bitcast.1.place_ref, f32[320,128]{1,0:T(8,128)S(1)} %get-tuple-element.34.own_ref.older, f32[224,128]{1,0:T(8,128)S(1)} %collective-permute-done.6.one_ref, f32[224,128]{1,0:T(8,128)S(1)} %collective-permute-done.7.two_ref, ...), custom_call_target="tpu_custom_call" | custom-call | tf_op jit(solution)/shard_map/pallas_call | solution.py:663
  34.2 0.1 collective-permute-start.8
  34.3 1.9 %collective-permute-start.9 = (f32[192,128]{1,0:T(8,128)S(1)}, f32[192,128]{1,0:T(8,128)S(1)}, u32[]{:S(2)}, u32[]{:S(2)}) collective-permute-start(f32[192,128]{1,0:T(8,128)S(1)} %get-tuple-element.42), channel_id=1, source_target_pairs={{0,60},{4,8},{8,4},{12,16},{16,12},{20,24},{24,20},{28,32},{32,28}... | collective-permute-start | bytes 294920 | tf_op jit(solution)/shard_map/ppermute | solution.py:677
  36.2 1.9 %shard_map.54.rate_ref = f32[384,128]{1,0:T(8,128)S(1)} custom-call(f32[576,128]{1,0:T(8,128)S(1)} %get-tuple-element.40.own_ref, f32[3,2,64,128]{3,2,1,0:T(8,128)S(1)} %get-tuple-element.32.speed_ref, f32[3,2,64,128]{3,2,1,0:T(8,128)S(1)} %get-tuple-element.38.rim_ref), custom_call_target="tpu_custom_call" | custom-call | tf_op jit(solution)/shard_map/pallas_call | solution.py:663
  38.2 1.8 %collective-permute-done.9.two_ref = f32[192,128]{1,0:T(8,128)S(1)} collective-permute-done((f32[192,128]{1,0:T(8,128)S(1)}, f32[192,128]{1,0:T(8,128)S(1)}, u32[]{:S(2)}, u32[]{:S(2)}) %collective-permute-start.9) | collective-permute-done | bytes 98336 | tf_op jit(solution)/shard_map/ppermute | solution.py:677
  40.0 1.6 %shard_map.55.own_ref = f32[64,128]{1,0:T(8,128)S(1)} custom-call(s32[1]{0:T(128)} %bitcast.1.place_ref, f32[576,128]{1,0:T(8,128)S(1)} %get-tuple-element.40.own_ref, f32[192,128]{1,0:T(8,128)S(1)} %collective-permute-done.8.one_ref, f32[192,128]{1,0:T(8,128)S(1)} %collective-permute-done.9.two_ref, f32[320,128]{1,0:T(8,128)S(1)} %get-tuple-element.34.own_ref.older, ...), custom_call_target="tpu_custom_call" | custom-call | tf_op jit(solution)/shard_map/pallas_call | solution.py:663
  41.6 3.6 %collective-permute-start.10 = (f32[64,128]{1,0:T(8,128)S(1)}, f32[64,128]{1,0:T(8,128)S(1)}, u32[]{:S(2)}, u32[]{:S(2)}) collective-permute-start(f32[64,128]{1,0:T(8,128)S(1)} %shard_map.55.own_ref), channel_id=1, source_target_pairs={{0,64},{64,0},{128,192},{192,128},{1,65},{65,1},{129,193},{193,129... | collective-permute-start | bytes 98312 | tf_op jit(solution)/shard_map/ppermute | solution.py:682
  45.2 0.9 %collective-permute-done.10.other_ref = f32[64,128]{1,0:T(8,128)S(1)} collective-permute-done((f32[64,128]{1,0:T(8,128)S(1)}, f32[64,128]{1,0:T(8,128)S(1)}, u32[]{:S(2)}, u32[]{:S(2)}) %collective-permute-start.10) | collective-permute-done | bytes 32800 | tf_op jit(solution)/shard_map/ppermute | solution.py:682
  46.0 0.1 shard_map.56
  46.2 1.0 %collective-permute-start.11 = (f32[32,128]{1,0:T(8,128)S(1)}, f32[32,128]{1,0:T(8,128)S(1)}, u32[]{:S(2)}, u32[]{:S(2)}) collective-permute-start(f32[32,128]{1,0:T(8,128)S(1)} %get-tuple-element.44), channel_id=1, source_target_pairs={{0,128},{64,192},{128,0},{192,64},{1,129},{65,193},{129,1},{193,65... | collective-permute-start | bytes 49160 | tf_op jit(solution)/shard_map/ppermute | solution.py:682
  47.1 3.2 %collective-permute-done.11.far_ref = f32[32,128]{1,0:T(8,128)S(1)} collective-permute-done((f32[32,128]{1,0:T(8,128)S(1)}, f32[32,128]{1,0:T(8,128)S(1)}, u32[]{:S(2)}, u32[]{:S(2)}) %collective-permute-start.11) | collective-permute-done | bytes 16416 | tf_op jit(solution)/shard_map/ppermute | solution.py:682
  50.3 0.7 %shard_map.57 = f32[32,2,128]{2,1,0:T(2,128)} custom-call(s32[1]{0:T(128)} %bitcast.group_ref, f32[64,128]{1,0:T(8,128)S(1)} %get-tuple-element.43.keep_ref, f32[32,128]{1,0:T(8,128)S(1)} %collective-permute-done.11.far_ref), custom_call_target="tpu_custom_call" | custom-call | tf_op jit(solution)/shard_map/pallas_call | solution.py:663
  (4 shorter events, 0.0 us)
Async XLA Ops:
  1.3 4.4 %collective-permute-start = (f32[576,128]{1,0:T(8,128)S(1)}, f32[576,128]{1,0:T(8,128)S(1)}, u32[]{:S(2)}, u32[]{:S(2)}) collective-permute-start(f32[576,128]{1,0:T(8,128)S(1)} %get-tuple-element.25.raw_ref), channel_id=1, source_target_pairs={{0,64},{64,0},{128,192},{192,128},{1,65},{65,1},{129,193},{193,129... | collective-permute-start | bytes 884744 | tf_op jit(solution)/shard_map/ppermute | solution.py:682
  5.9 8.0 %collective-permute-start.1 = (f32[256,128]{1,0:T(8,128)S(1)}, f32[256,128]{1,0:T(8,128)S(1)}, u32[]{:S(2)}, u32[]{:S(2)}) collective-permute-start(f32[256,128]{1,0:T(8,128)S(1)} %get-tuple-element.27), channel_id=1, source_target_pairs={{0,128},{64,192},{128,0},{192,64},{1,129},{65,193},{129,1},{193,65... | collective-permute-start | bytes 393224 | tf_op jit(solution)/shard_map/ppermute | solution.py:682
  7.0 6.9 %collective-permute-start.2 = (f32[80,128]{1,0:T(8,128)S(1)}, f32[80,128]{1,0:T(8,128)S(1)}, u32[]{:S(2)}, u32[]{:S(2)}) collective-permute-start(f32[80,128]{1,0:T(8,128)S(1)} %get-tuple-element.28), channel_id=1, source_target_pairs={{0,1},{1,2},{2,3},{3,0},{64,195},{65,192},{66,193},{67,194},{128,1... | collective-permute-start | bytes 122888 | tf_op jit(solution)/shard_map/ppermute | solution.py:690
  13.9 1.5 %collective-permute-start.3 = (f32[336,128]{1,0:T(8,128)S(1)}, f32[336,128]{1,0:T(8,128)S(1)}, u32[]{:S(2)}, u32[]{:S(2)}) collective-permute-start(f32[336,128]{1,0:T(8,128)S(1)} %shard_map.48.half_ref), channel_id=1, source_target_pairs={{0,64},{64,0},{128,192},{192,128},{1,65},{65,1},{129,193},{193,129... | collective-permute-start | bytes 516104 | tf_op jit(solution)/shard_map/ppermute | solution.py:682
  15.8 7.8 %collective-permute-start.4 = (f32[176,128]{1,0:T(8,128)S(1)}, f32[176,128]{1,0:T(8,128)S(1)}, u32[]{:S(2)}, u32[]{:S(2)}) collective-permute-start(f32[176,128]{1,0:T(8,128)S(1)} %get-tuple-element.30), channel_id=1, source_target_pairs={{0,4},{4,0},{8,12},{12,8},{16,20},{20,16},{24,28},{28,24},{32,36},... | collective-permute-start | bytes 270344 | tf_op jit(solution)/shard_map/ppermute | solution.py:676
  17.5 7.8 %collective-permute-start.5 = (f32[176,128]{1,0:T(8,128)S(1)}, f32[176,128]{1,0:T(8,128)S(1)}, u32[]{:S(2)}, u32[]{:S(2)}) collective-permute-start(f32[176,128]{1,0:T(8,128)S(1)} %get-tuple-element.31), channel_id=1, source_target_pairs={{0,60},{4,8},{8,4},{12,16},{16,12},{20,24},{24,20},{28,32},{32,28}... | collective-permute-start | bytes 270344 | tf_op jit(solution)/shard_map/ppermute | solution.py:677
  25.8 5.8 %collective-permute-start.7 = (f32[224,128]{1,0:T(8,128)S(1)}, f32[224,128]{1,0:T(8,128)S(1)}, u32[]{:S(2)}, u32[]{:S(2)}) collective-permute-start(f32[224,128]{1,0:T(8,128)S(1)} %get-tuple-element.35), channel_id=1, source_target_pairs={{0,60},{4,8},{8,4},{12,16},{16,12},{20,24},{24,20},{28,32},{32,28}... | collective-permute-start | bytes 344072 | tf_op jit(solution)/shard_map/ppermute | solution.py:677
  29.1 3.9 %collective-permute-start.6 = (f32[224,128]{1,0:T(8,128)S(1)}, f32[224,128]{1,0:T(8,128)S(1)}, u32[]{:S(2)}, u32[]{:S(2)}) collective-permute-start(f32[224,128]{1,0:T(8,128)S(1)} %get-tuple-element.35), channel_id=1, source_target_pairs={{0,4},{4,0},{8,12},{12,8},{16,20},{20,16},{24,28},{28,24},{32,36},... | collective-permute-start | bytes 344072 | tf_op jit(solution)/shard_map/ppermute | solution.py:676
  34.2 4.0 %collective-permute-start.8 = (f32[192,128]{1,0:T(8,128)S(1)}, f32[192,128]{1,0:T(8,128)S(1)}, u32[]{:S(2)}, u32[]{:S(2)}) collective-permute-start(f32[192,128]{1,0:T(8,128)S(1)} %get-tuple-element.41), channel_id=1, source_target_pairs={{0,4},{4,0},{8,12},{12,8},{16,20},{20,16},{24,28},{28,24},{32,36},... | collective-permute-start | bytes 294920 | tf_op jit(solution)/shard_map/ppermute | solution.py:676
  34.3 5.7 %collective-permute-start.9 = (f32[192,128]{1,0:T(8,128)S(1)}, f32[192,128]{1,0:T(8,128)S(1)}, u32[]{:S(2)}, u32[]{:S(2)}) collective-permute-start(f32[192,128]{1,0:T(8,128)S(1)} %get-tuple-element.42), channel_id=1, source_target_pairs={{0,60},{4,8},{8,4},{12,16},{16,12},{20,24},{24,20},{28,32},{32,28}... | collective-permute-start | bytes 294920 | tf_op jit(solution)/shard_map/ppermute | solution.py:677
  41.6 4.5 %collective-permute-start.10 = (f32[64,128]{1,0:T(8,128)S(1)}, f32[64,128]{1,0:T(8,128)S(1)}, u32[]{:S(2)}, u32[]{:S(2)}) collective-permute-start(f32[64,128]{1,0:T(8,128)S(1)} %shard_map.55.own_ref), channel_id=1, source_target_pairs={{0,64},{64,0},{128,192},{192,128},{1,65},{65,1},{129,193},{193,129... | collective-permute-start | bytes 98312 | tf_op jit(solution)/shard_map/ppermute | solution.py:682
  46.2 4.1 %collective-permute-start.11 = (f32[32,128]{1,0:T(8,128)S(1)}, f32[32,128]{1,0:T(8,128)S(1)}, u32[]{:S(2)}, u32[]{:S(2)}) collective-permute-start(f32[32,128]{1,0:T(8,128)S(1)} %get-tuple-element.44), channel_id=1, source_target_pairs={{0,128},{64,192},{128,0},{192,64},{1,129},{65,193},{129,1},{193,65... | collective-permute-start | bytes 49160 | tf_op jit(solution)/shard_map/ppermute | solution.py:682
